TPU v7x, 32 devices: a whole 2x2x4 slice. The times are simulated.
32 devices in a mesh: groups: 2 (over y), blk: 4 (over z), rep: 4 (over x, core).
Axes of the slice: x: 2, y: 2, z: 4, core: 2. Of those that a mesh axis runs over, the one named last changes fastest.
Arguments:
- orbitals: float32 [8, 262144], P(('groups', 'blk')), parts along dimension 0, may hold values from -6 to 6
- offsets: int32 [8], P('groups'), parts along dimension 0, may hold values from 0 to 3
Outputs:
- exchanged: float32 [8, 262144], P(('groups', 'blk'), 'rep'), parts along dimension 0
- margin: float32 [8, 4], P(('groups', 'blk')), parts along dimension 0
There are 2 independent parts, one for each index of `groups`. A program takes and returns all parts, laid end to end along the dimension named above; each array names one. Nothing has to cross between parts.
All inputs are finite; a program needn't handle non-finite values.
Results may differ from a plain program's by a relative error of at most 0.0001.
Values sent between devices are 32-bit elements; how exact they have to be, the bound alone decides.
No kernel may reach another device: no remote copies, remote signals or barrier semaphores. Data moves between devices by JAX's collectives and lax.ppermute only.
A program may use at most 64 MiB of HBM per device.

v0:
```python
import jax
import jax.numpy as jnp
from jax import lax
from jax.sharding import PartitionSpec as P

NG = 64


precise_mode = lax.Precision.HIGHEST
screen_scale = 0.05


def passed_along(block, axis, distance):
    devices = range(lax.axis_size(axis))
    route = [((i - distance) % len(devices), i) for i in devices]
    return lax.ppermute(block, axis, route)


def cas_table(grid_points):
    grid_index = jnp.arange(grid_points, dtype=jnp.int32)
    product = grid_index[:, None] * grid_index[None, :] % grid_points
    phase_angle = 2.0 * jnp.pi / grid_points * product.astype(jnp.float32)
    return jnp.cos(phase_angle) + jnp.sin(phase_angle)


def screened_kernel(grid_points):
    grid_index = jnp.arange(grid_points, dtype=jnp.int32)
    folded = jnp.where(grid_index <= grid_points // 2, grid_index, grid_index - grid_points).astype(
        jnp.float32
    )
    squares = folded * folded
    k_squared = squares[:, None, None] + squares[None, :, None] + squares[None, None, :]
    safe_square = jnp.maximum(k_squared, 1.0)
    screened = (
        4.0
        * jnp.pi
        / (screen_scale * safe_square)
        * (1.0 - jnp.exp(-screen_scale * safe_square / (4.0 * jnp.pi)))
    )
    return jnp.where(k_squared > 0.5, screened, jnp.ones_like(screened))


def transform(values_field, cas_values, cas_paired):
    batch_size = values_field.shape[0]
    grid_points = values_field.shape[1]
    values_field = jnp.einsum(
        "kx,pxq->pkq",
        cas_values,
        values_field.reshape(batch_size, grid_points, grid_points * grid_points),
        precision=precise_mode,
    )
    values_field = jnp.einsum(
        "ky,ayz->akz",
        cas_values,
        values_field.reshape(batch_size * grid_points, grid_points, grid_points),
        precision=precise_mode,
    )
    values_field = jnp.dot(
        values_field.reshape(batch_size * grid_points * grid_points // 2, 2 * grid_points),
        cas_paired,
        precision=precise_mode,
    )
    return values_field.reshape(batch_size, grid_points, grid_points, grid_points)


def cycle_term(own_block, visiting, cas_values, cas_paired, kernel):
    grid_points = kernel.shape[0]
    block_rows = own_block.shape[0]
    density = (own_block[:, None, :] * visiting[None, :, :]).reshape(
        block_rows * block_rows, grid_points, grid_points, grid_points
    )
    spectrum = transform(density, cas_values, cas_paired) * kernel[None]
    potential = transform(spectrum, cas_values, cas_paired).reshape(
        block_rows, block_rows, grid_points**3
    ) / float(grid_points**3)
    return jnp.sum(potential * visiting[None, :, :], axis=1)


def position_block(orbital_block, amount):
    bit_count = (lax.axis_size("blk") - 1).bit_length()
    for bit_level in range(bit_count):
        moved_block = passed_along(orbital_block, "blk", 1 << bit_level)
        orbital_block = jnp.where(amount // (1 << bit_level) % 2 == 1, moved_block, orbital_block)
    return orbital_block


def local(orbitals, offsets):
    cas_values = cas_table(NG)
    cas_paired = jnp.kron(jnp.eye(2, dtype=jnp.float32), cas_values)
    kernel = screened_kernel(NG)
    cycle_size = lax.axis_size("blk")
    replica = lax.axis_index("rep")
    start_block = offsets[replica]
    first_visit = position_block(orbitals, (start_block + 1) % cycle_size)
    behind = passed_along(first_visit, "blk", -1)
    accumulator = cycle_term(orbitals, first_visit, cas_values, cas_paired, kernel)
    ahead_block = first_visit
    ahead_block = passed_along(ahead_block, "blk", 1)
    accumulator = accumulator + cycle_term(orbitals, ahead_block, cas_values, cas_paired, kernel)
    accumulator = accumulator + cycle_term(orbitals, behind, cas_values, cas_paired, kernel)
    exchanged = lax.psum_scatter(accumulator, "rep", scatter_dimension=1, tiled=True)
    quarter_cells = exchanged.shape[1]
    quarter = lax.dynamic_slice_in_dim(orbitals, replica * quarter_cells, quarter_cells, 1)
    slab_orbitals, slab_exchanged = (
        lax.all_to_all(quarter, "blk", split_axis=1, concat_axis=0, tiled=True),
        lax.all_to_all(exchanged, "blk", split_axis=1, concat_axis=0, tiled=True),
    )
    partial_value = lax.dot_general(
        slab_orbitals, slab_exchanged, (((1,), (1,)), ((), ())), precision=precise_mode
    ) / float(NG**3)
    gram_rows = lax.psum_scatter(partial_value, "blk", scatter_dimension=0, tiled=True)
    margin = lax.psum(gram_rows, "rep")
    return (exchanged, margin)


def solution(mesh):
    placed = (P(("groups", "blk"), None), P("groups"))
    return jax.shard_map(
        local,
        mesh=mesh,
        in_specs=placed,
        out_specs=(P(("groups", "blk"), "rep"), P(("groups", "blk"), None)),
        check_vma=False,
    )
```

profile of v0, /device:TPU:0, one launch (start us, length us, event | category | flops | bytes accessed | tf_op | source)
XLA Modules:
  0.0 327.6 jit_solution(143955642018694958)
XLA Ops:
  12.2 23.5 %collective-permute-done = f32[1,262144]{1,0:T(1,128)S(1)} collective-permute-done((f32[1,262144]{1,0:T(1,128)}, f32[1,262144]{1,0:T(1,128)S(1)}, u32[]{:S(2)}, u32[]{:S(2)}) %collective-permute-start) | collective-permute-done | bytes 1048608 | tf_op jit(solution)/shard_map/ppermute | solution.py:16
  37.6 46.9 %collective-permute-done.1 = f32[1,262144]{1,0:T(1,128)S(1)} collective-permute-done((f32[1,262144]{1,0:T(1,128)S(1)}, f32[1,262144]{1,0:T(1,128)S(1)}, u32[]{:S(2)}, u32[]{:S(2)}) %collective-permute-start.1) | collective-permute-done | bytes 1048608 | tf_op jit(solution)/shard_map/ppermute | solution.py:16
  85.7 3.8 %collective-permute-start.3 = (f32[1,262144]{1,0:T(1,128)S(1)}, f32[1,262144]{1,0:T(1,128)}, u32[]{:S(2)}, u32[]{:S(2)}) collective-permute-start(f32[1,262144]{1,0:T(1,128)S(1)} %broadcast_select_fusion.1), channel_id=1, source_target_pairs={{4,0},{8,4},{12,8},{0,12},{5,1},{9,5},{13,9},{1,13},{6,2},{10,6},{... | collective-permute-start | bytes 3145736 | tf_op jit(solution)/shard_map/ppermute | solution.py:16
  92.3 21.4 %collective-permute-done.2 = f32[1,262144]{1,0:T(1,128)} collective-permute-done((f32[1,262144]{1,0:T(1,128)S(1)}, f32[1,262144]{1,0:T(1,128)}, u32[]{:S(2)}, u32[]{:S(2)}) %collective-permute-start.2) | collective-permute-done | bytes 1048608 | tf_op jit(solution)/shard_map/ppermute | solution.py:16
  113.7 19.8 %collective-permute-done.3 = f32[1,262144]{1,0:T(1,128)} collective-permute-done((f32[1,262144]{1,0:T(1,128)S(1)}, f32[1,262144]{1,0:T(1,128)}, u32[]{:S(2)}, u32[]{:S(2)}) %collective-permute-start.3) | collective-permute-done | bytes 1048608 | tf_op jit(solution)/shard_map/ppermute | solution.py:16
  133.4 14.2 %multiply_reduce_fusion.2 = (f32[262144]{0:T(1024)}, f32[262144]{0:T(1024)S(1)}, f32[262144]{0:T(1024)}) fusion(f32[1,262144]{1,0:T(1,128)} %param.2, f32[1,262144]{1,0:T(1,128)S(1)} %broadcast_select_fusion.1, f32[1,262144]{1,0:T(1,128)} %collective-permute-done.2, f32[1,262144]{1,0:T(1,128)} %collective-permute-done.3), kind=kLoop, calls=%fused_computation.25 | loop fusion | flops 786432 | bytes 7340032 | tf_op jit(solution)/shard_map/mul | solution.py:69
  152.1 4.8 %convolution_bitcast_fusion.9 = f32[64,64,64]{1,2,0:T(8,128)} fusion(f32[64,64,64]{2,1,0:T(8,128)S(1)} %reshape.337), kind=kOutput, calls=%fused_computation.14 | convolution fusion | flops 201388032 | bytes 2097152 | tf_op jit(solution)/shard_map/ky,ayz->akz/dot_general | solution.py:52
  163.8 3.9 %convolution_bitcast_fusion.2 = f32[1,64,4096]{2,1,0:T(8,128)} fusion(f32[64,4096]{1,0:T(8,128)} %reshape.339, f32[64,4096]{1,0:T(8,128)S(1)} %copy-done.4, f32[4096]{0:T(1024)S(1)} %add.227), kind=kOutput, calls=%fused_computation.2 | convolution fusion | flops 204009472 | bytes 3162112 | tf_op jit(solution)/shard_map/kx,pxq->pkq/dot_general | solution.py:46
  169.6 4.8 %convolution_bitcast_fusion.8 = f32[64,64,64]{1,2,0:T(8,128)} fusion(f32[64,64,64]{2,1,0:T(8,128)S(1)} %reshape.340), kind=kOutput, calls=%fused_computation.13 | convolution fusion | flops 201388032 | bytes 2097152 | tf_op jit(solution)/shard_map/ky,ayz->akz/dot_general | solution.py:52
  177.7 3.3 %convolution_multiply_fusion.1 = f32[2048,128]{1,0:T(8,128)} fusion(f32[2048,128]{1,0:T(8,128)} %reshape.341, f32[128,128]{1,0:T(8,128)S(1)} %mul.403), kind=kOutput, calls=%fused_computation.7 | convolution fusion | flops 402915328 | bytes 2162688 | tf_op jit(solution)/shard_map/dot_general | solution.py:58
  185.5 4.8 %convolution_bitcast_fusion.11 = f32[64,64,64]{1,2,0:T(8,128)} fusion(f32[64,64,64]{2,1,0:T(8,128)S(1)} %reshape.332), kind=kOutput, calls=%fused_computation.16 | convolution fusion | flops 201388032 | bytes 2097152 | tf_op jit(solution)/shard_map/ky,ayz->akz/dot_general | solution.py:52
  197.0 3.9 %convolution_bitcast_fusion.4 = f32[1,64,4096]{2,1,0:T(8,128)} fusion(f32[64,4096]{1,0:T(8,128)} %reshape.334, f32[64,4096]{1,0:T(8,128)S(1)} %copy-done.5, f32[4096]{0:T(1024)S(1)} %add.227), kind=kOutput, calls=%fused_computation.4 | convolution fusion | flops 204009472 | bytes 3162112 | tf_op jit(solution)/shard_map/kx,pxq->pkq/dot_general | solution.py:46
  202.9 4.8 %convolution_bitcast_fusion.10 = f32[64,64,64]{1,2,0:T(8,128)} fusion(f32[64,64,64]{2,1,0:T(8,128)S(1)} %reshape.335), kind=kOutput, calls=%fused_computation.15 | convolution fusion | flops 201388032 | bytes 2097152 | tf_op jit(solution)/shard_map/ky,ayz->akz/dot_general | solution.py:52
  211.4 3.3 %convolution_multiply_fusion.2 = f32[2048,128]{1,0:T(8,128)} fusion(f32[2048,128]{1,0:T(8,128)} %reshape.336, f32[128,128]{1,0:T(8,128)S(1)} %mul.403), kind=kOutput, calls=%fused_computation.8 | convolution fusion | flops 402915328 | bytes 2162688 | tf_op jit(solution)/shard_map/dot_general | solution.py:58
  219.0 4.8 %convolution_bitcast_fusion.7 = f32[64,64,64]{1,2,0:T(8,128)} fusion(f32[64,64,64]{2,1,0:T(8,128)S(1)} %reshape.342), kind=kOutput, calls=%fused_computation.12 | convolution fusion | flops 201388032 | bytes 2097152 | tf_op jit(solution)/shard_map/ky,ayz->akz/dot_general | solution.py:52
  230.6 3.9 %convolution_bitcast_fusion = f32[1,64,4096]{2,1,0:T(8,128)} fusion(f32[64,4096]{1,0:T(8,128)} %reshape.344, f32[64,4096]{1,0:T(8,128)S(1)} %copy-done.6, f32[4096]{0:T(1024)S(1)} %add.227), kind=kOutput, calls=%fused_computation | convolution fusion | flops 204009472 | bytes 3162112 | tf_op jit(solution)/shard_map/kx,pxq->pkq/dot_general | solution.py:46
  236.6 4.8 %convolution_bitcast_fusion.6 = f32[64,64,64]{1,2,0:T(8,128)} fusion(f32[64,64,64]{2,1,0:T(8,128)S(1)} %reshape.345), kind=kOutput, calls=%fused_computation.11 | convolution fusion | flops 201388032 | bytes 2097152 | tf_op jit(solution)/shard_map/ky,ayz->akz/dot_general | solution.py:52
  247.1 4.5 %multiply_add_fusion = f32[1,262144]{1,0:T(1,128)} fusion(f32[1,262144]{1,0:T(1,128)S(1)} %bitcast.88, f32[1,262144]{1,0:T(1,128)} %collective-permute-done.3, f32[1,262144]{1,0:T(1,128)S(1)} %bitcast.86, f32[1,262144]{1,0:T(1,128)} %collective-permute-done.2, f32[1,262144]{1,0:T(1,128)S(1)} %bitcast.87, f32[1,262144]{1,0:T(1,128)S(1)} %broadcast_select_fusion.1), kind=kLoop, calls=%fused_computation.18 | loop fusion | flops 1310720 | bytes 7340032 | tf_op jit(solution)/shard_map/add | solution.py:100
  253.3 3.7 %all-to-all-start = ((f32[1,4,16384]{2,0,1:T(1,128)}), f32[1,4,16384]{2,0,1:T(1,128)S(1)}, u32[]{:S(2)}, u32[]{:S(2)}) async-start(f32[1,4,16384]{2,0,1:T(1,128)} %bitcast.23), calls=%async_computation | async-start | bytes 524288 | tf_op jit(solution)/shard_map/all_to_all | solution.py:105
  258.2 29.9 %all-reduce.4.cloned.1.call-done = f32[1,262144]{1,0:T(1,128)} async-done(((f32[1,262144]{1,0:T(1,128)}), f32[1,262144]{1,0:T(1,128)}) %all-reduce.4.cloned.1.call-update) | async-done | bytes 1048592
  289.8 4.6 %all-to-all-start.1 = ((f32[1,4,16384]{2,0,1:T(1,128)}), f32[1,4,16384]{2,0,1:T(1,128)S(1)}, u32[]{:S(2)}, u32[]{:S(2)}) async-start(f32[1,4,16384]{2,0,1:T(1,128)} %bitcast.24), calls=%async_computation.1 | async-start | bytes 524288 | tf_op jit(solution)/shard_map/all_to_all | solution.py:106
  295.0 7.7 %all-to-all-done.1 = f32[1,4,16384]{2,0,1:T(1,128)S(1)} async-done(((f32[1,4,16384]{2,0,1:T(1,128)}), f32[1,4,16384]{2,0,1:T(1,128)S(1)}, u32[]{:S(2)}, u32[]{:S(2)}) %all-to-all-start.1) | async-done | bytes 262176 | tf_op jit(solution)/shard_map/all_to_all | solution.py:106
  304.0 9.8 %all-reduce.1 = f32[4,4]{1,0:T(4,128)S(1)} all-reduce(f32[4,4]{1,0:T(4,128)S(1)} %convolution_multiply_fusion.3), channel_id=3, replica_groups=mesh['groups'=2,'blk'=4,'rep'=4] {'blk'}, use_global_device_ids=true, to_apply=%region_1.2.clone | all-reduce | flops 16 | bytes 128
  314.4 6.2 %psum.7 = f32[1,4]{1,0:T(1,128)} all-reduce(f32[1,4]{1,0:T(1,128)S(1)} %constant_dynamic-slice_fusion), channel_id=1, replica_groups=mesh['groups'=2,'blk'=4,'rep'=4] {'rep'}, use_global_device_ids=true, to_apply=%region_2.3 | all-reduce | flops 4 | bytes 32 | tf_op jit(solution)/shard_map/psum | solution.py:112
  (74 shorter events, 69.0 us)
Async XLA Ops:
  7.2 280.9 %all-reduce.4.cloned.1.call-start = ((), (), s32[]{:S(2)}) async-start(), calls=%async_computation.2 | async-start | bytes 2097152
  7.2 28.5 %collective-permute-start = (f32[1,262144]{1,0:T(1,128)}, f32[1,262144]{1,0:T(1,128)S(1)}, u32[]{:S(2)}, u32[]{:S(2)}) collective-permute-start(f32[1,262144]{1,0:T(1,128)} %param.2), channel_id=1, source_target_pairs={{12,0},{0,4},{4,8},{8,12},{13,1},{1,5},{5,9},{9,13},{14,2},{2,6},{... | collective-permute-start | bytes 3145736 | tf_op jit(solution)/shard_map/ppermute | solution.py:16
  36.8 47.7 %collective-permute-start.1 = (f32[1,262144]{1,0:T(1,128)S(1)}, f32[1,262144]{1,0:T(1,128)S(1)}, u32[]{:S(2)}, u32[]{:S(2)}) collective-permute-start(f32[1,262144]{1,0:T(1,128)S(1)} %broadcast_select_fusion), channel_id=1, source_target_pairs={{8,0},{12,4},{0,8},{4,12},{9,1},{13,5},{1,9},{5,13},{10,2},{14,6},... | collective-permute-start | bytes 3145736 | tf_op jit(solution)/shard_map/ppermute | solution.py:16
  85.6 28.0 %collective-permute-start.2 = (f32[1,262144]{1,0:T(1,128)S(1)}, f32[1,262144]{1,0:T(1,128)}, u32[]{:S(2)}, u32[]{:S(2)}) collective-permute-start(f32[1,262144]{1,0:T(1,128)S(1)} %broadcast_select_fusion.1), channel_id=1, source_target_pairs={{12,0},{0,4},{4,8},{8,12},{13,1},{1,5},{5,9},{9,13},{14,2},{2,6},{... | collective-permute-start | bytes 3145736 | tf_op jit(solution)/shard_map/ppermute | solution.py:16
  85.7 47.7 %collective-permute-start.3 = (f32[1,262144]{1,0:T(1,128)S(1)}, f32[1,262144]{1,0:T(1,128)}, u32[]{:S(2)}, u32[]{:S(2)}) collective-permute-start(f32[1,262144]{1,0:T(1,128)S(1)} %broadcast_select_fusion.1), channel_id=1, source_target_pairs={{4,0},{8,4},{12,8},{0,12},{5,1},{9,5},{13,9},{1,13},{6,2},{10,6},{... | collective-permute-start | bytes 3145736 | tf_op jit(solution)/shard_map/ppermute | solution.py:16
  160.3 3.5 %copy-start.4 = (f32[64,4096]{1,0:T(8,128)S(1)}, f32[64,4096]{1,0:T(8,128)}, u32[]{:S(2)}) copy-start(f32[64,4096]{1,0:T(8,128)} %add.226) | copy-start | bytes 3145732
  177.7 3.3 %copy-start.3 = (f32[262144]{0:T(1024)S(1)}, f32[262144]{0:T(1024)}, u32[]{:S(2)}) copy-start(f32[262144]{0:T(1024)} %get-tuple-element.2) | copy-start | bytes 3145732
  193.6 3.4 %copy-start.5 = (f32[64,4096]{1,0:T(8,128)S(1)}, f32[64,4096]{1,0:T(8,128)}, u32[]{:S(2)}) copy-start(f32[64,4096]{1,0:T(8,128)} %add.226) | copy-start | bytes 3145732
  211.4 3.3 %copy-start.1 = (f32[262144]{0:T(1024)S(1)}, f32[262144]{0:T(1024)}, u32[]{:S(2)}) copy-start(f32[262144]{0:T(1024)} %get-tuple-element.4) | copy-start | bytes 3145732
  227.1 3.5 %copy-start.6 = (f32[64,4096]{1,0:T(8,128)S(1)}, f32[64,4096]{1,0:T(8,128)}, u32[]{:S(2)}) copy-start(f32[64,4096]{1,0:T(8,128)} %add.226) | copy-start | bytes 3145732
  244.7 2.4 copy-start
  244.7 2.4 copy-start.2
  251.6 5.4 %copy-start.8 = (u32[32]{0:T(128)S(1)}, u32[32]{0:T(128)}, u32[]{:S(2)}) copy-start(u32[32]{0:T(128)} %constant.106) | copy-start | bytes 388
  251.6 42.8 %copy-start.7 = (u32[32]{0:T(128)S(1)}, u32[32]{0:T(128)}, u32[]{:S(2)}) copy-start(u32[32]{0:T(128)} %constant.110) | copy-start | bytes 388
  253.3 36.5 %all-to-all-start = ((f32[1,4,16384]{2,0,1:T(1,128)}), f32[1,4,16384]{2,0,1:T(1,128)S(1)}, u32[]{:S(2)}, u32[]{:S(2)}) async-start(f32[1,4,16384]{2,0,1:T(1,128)} %bitcast.23), calls=%async_computation | async-start | bytes 524288 | tf_op jit(solution)/shard_map/all_to_all | solution.py:105
  289.8 12.9 %all-to-all-start.1 = ((f32[1,4,16384]{2,0,1:T(1,128)}), f32[1,4,16384]{2,0,1:T(1,128)S(1)}, u32[]{:S(2)}, u32[]{:S(2)}) async-start(f32[1,4,16384]{2,0,1:T(1,128)} %bitcast.24), calls=%async_computation.1 | async-start | bytes 524288 | tf_op jit(solution)/shard_map/all_to_all | solution.py:106
Sparse Core Ops, SparseCore 0:
  251.7 36.3 all-reduce.3
where the time goes:
time: 331 us; the launch traced here: 328 us
  waiting for transfers between devices  149 us (45%)
  matrix products  64 us (19%)
  local copies, waits for them, and re-layouts  45.4 us (14%)
  other arithmetic  21.3 us (6%)
  starting transfers between devices  16.1 us (5%)
  blocking collectives  16 us (5%)
  between operations  15.8 us (5%)
    ppermute x4, waiting for transfers between devices, passed_along(): return lax.ppermute(block, axis, route)  111 us
    unnamed x2, waiting for transfers between devices  29.9 us
    dot_general x6, matrix products, transform(): jnp.einsum('ky,ayz->akz', cas_values, values_field.reshape(batch_size * g...  28.7 us
    dot_general x6, matrix products, transform(): jnp.einsum('kx,pxq->pkq', cas_values, values_field.reshape(batch_size, gr...  18.2 us
    dot_general x6, matrix products, transform(): jnp.dot(values_field.reshape(batch_size * grid_points * grid_points // 2,...  15.8 us
    mul x1, other arithmetic, cycle_term(): own_block[:, None, :] * visiting[None, :, :]  14.2 us
    reshape x6, local copies, waits for them, and re-layouts, transform(): values_field.reshape(batch_size * grid_points, grid_points, grid_points)  12.4 us
    transpose x6, local copies, waits for them, and re-layouts, transform(): jnp.einsum('ky,ayz->akz', cas_values, values_field.reshape(batch_size * g...  12.1 us
  transfers between devices with their start and end apart: 7, of which 6 were waited for; matrix products, arithmetic and copies ran while one was open for 3% of the time, Pallas kernels for 0%

commit v1 on v0

v1 whole, which is shorter than its diff:
```python
import functools

import jax
import jax.numpy as jnp
from jax import lax
from jax.experimental import pallas as pl
from jax.experimental.pallas import tpu as pltpu
from jax.sharding import PartitionSpec as P

NG = 64
STEPS = 3
LANES = 128
HALF = LANES // 2
screen_scale = 0.05


def passed_along(block, axis, distance):
    devices = range(lax.axis_size(axis))
    route = [((i - distance) % len(devices), i) for i in devices]
    return lax.ppermute(block, axis, route)


def cas_table(grid_points):
    grid_index = jnp.arange(grid_points, dtype=jnp.int32)
    product = grid_index[:, None] * grid_index[None, :] % grid_points
    phase_angle = 2.0 * jnp.pi / grid_points * product.astype(jnp.float32)
    return jnp.cos(phase_angle) + jnp.sin(phase_angle)


def screened_kernel(grid_points):
    def squares(index):
        folded = jnp.where(index <= grid_points // 2, index, index - grid_points).astype(jnp.float32)
        return folded * folded

    shape = (grid_points * grid_points // 2, 2 * grid_points)
    row = lax.broadcasted_iota(jnp.int32, shape, 0)
    lane = lax.broadcasted_iota(jnp.int32, shape, 1)
    k_squared = (
        squares(row % grid_points)
        + squares(2 * (row // grid_points) + lane // grid_points)
        + squares(lane % grid_points)
    )
    safe_square = jnp.maximum(k_squared, 1.0)
    screened = (
        4.0
        * jnp.pi
        / (screen_scale * safe_square)
        * (1.0 - jnp.exp(-screen_scale * safe_square / (4.0 * jnp.pi)))
    )
    return jnp.where(k_squared > 0.5, screened, jnp.ones_like(screened))


def high_low(value):
    high = value.astype(jnp.bfloat16)
    return high, (value - high.astype(jnp.float32)).astype(jnp.bfloat16)


def dot(a, b):
    return lax.dot_general(a, b, (((1,), (0,)), ((), ())), preferred_element_type=jnp.float32)


def swapped(first, second, low_half):
    return (
        jnp.where(low_half, first, pltpu.roll(second, HALF, 1)),
        jnp.where(low_half, pltpu.roll(first, HALF, 1), second),
    )


def left_weights(table):
    high, low = high_low(table)
    return jnp.concatenate([high, high, low], axis=1)


def lane_weights(table):
    high, low = high_low(table)
    return jnp.concatenate(
        [jnp.concatenate([high, low], axis=1), jnp.concatenate([high, jnp.zeros_like(low)], axis=1)],
        axis=0,
    )


def from_left(weights, value):
    high, low = high_low(value)
    return dot(weights, jnp.concatenate([high, low, high], axis=0))


def along_lanes(value, weights):
    high, low = high_low(value)
    both = dot(jnp.concatenate([high, low], axis=1), weights)
    return both[:, :LANES] + both[:, LANES:]


def low_mask(rows):
    return lax.broadcasted_iota(jnp.int32, (rows, LANES), 1) < HALF


def spectrum_body(own, visiting, kernel, forward, backward, paired, out):
    plane = NG // 2
    pairs = NG // 2
    mask = low_mask(plane)
    w_forward = left_weights(forward[...])
    w_backward = left_weights(backward[...])
    w_lanes = lane_weights(paired[...])

    def planes(step, _):
        at = pl.multiple_of(step * (4 * plane), 4 * plane)
        density = own[pl.ds(at, 4 * plane), :] * visiting[pl.ds(at, 4 * plane), :]
        along_z = along_lanes(density, w_lanes)
        blocks = []
        for half in range(2):
            base = half * 2 * plane
            even, odd = swapped(along_z[base : base + plane], along_z[base + plane : base + 2 * plane], mask)
            blocks.append(jnp.concatenate([even, odd], axis=0))
        along_y = from_left(w_forward, jnp.concatenate(blocks, axis=1))
        out[pl.ds(at, 2 * plane), :] = along_y[:, :LANES]
        out[pl.ds(at + 2 * plane, 2 * plane), :] = along_y[:, LANES:]
        return 0

    lax.fori_loop(0, NG // 4, planes, 0, unroll=2)

    def columns(step, _):
        blocks = []
        for part in range(2):
            row = 4 * step + 2 * part
            first = out[pl.ds(row, pairs, stride=NG), :]
            second = out[pl.ds(row + 1, pairs, stride=NG), :]
            blocks.append(jnp.concatenate(swapped(first, second, mask), axis=0))
        along_x = from_left(w_forward, jnp.concatenate(blocks, axis=1))
        at = pl.multiple_of(step * (2 * NG), 2 * NG)
        weight = jnp.concatenate([kernel[pl.ds(at, NG), :], kernel[pl.ds(at + NG, NG), :]], axis=1)
        returned = from_left(w_backward, along_x * weight)
        for part in range(2):
            block = returned[:, part * LANES : (part + 1) * LANES]
            first, second = swapped(block[:plane], block[plane:], mask)
            row = 4 * step + 2 * part
            out[pl.ds(row, pairs, stride=NG), :] = first
            out[pl.ds(row + 1, pairs, stride=NG), :] = second
        return 0

    lax.fori_loop(0, NG // 4, columns, 0, unroll=2)


def spectrum(own, visiting, kernel, forward, backward, paired):
    rows = own.shape[0]
    return pl.pallas_call(
        spectrum_body,
        out_shape=jax.ShapeDtypeStruct((rows, LANES), jnp.float32),
        in_specs=[pl.BlockSpec(memory_space=pltpu.VMEM)] * 6,
        out_specs=pl.BlockSpec(memory_space=pltpu.VMEM),
        compiler_params=pltpu.CompilerParams(vmem_limit_bytes=24 << 20),
        cost_estimate=pl.CostEstimate(flops=rows * LANES * NG * 24, bytes_accessed=16 * rows * LANES, transcendentals=0),
        name="spectrum",
    )(own, visiting, kernel, forward, backward, paired)


def term_body(chosen, spectral, visiting, scale, backward, paired, out):
    plane = NG // 2
    mask = low_mask(plane)
    w_backward = left_weights(backward[...])
    w_lanes = lane_weights(paired[...])
    factor = scale[0]

    def planes(step, _):
        at = pl.multiple_of(step * (4 * plane), 4 * plane)
        pair = jnp.concatenate(
            [spectral[pl.ds(at, 2 * plane), :], spectral[pl.ds(at + 2 * plane, 2 * plane), :]], axis=1
        )
        along_y = from_left(w_backward, pair)
        blocks = []
        for half in range(2):
            block = along_y[:, half * LANES : (half + 1) * LANES]
            blocks.extend(swapped(block[:plane], block[plane:], mask))
        potential = along_lanes(jnp.concatenate(blocks, axis=0), w_lanes)
        out[pl.ds(at, 4 * plane), :] = potential * (visiting[pl.ds(at, 4 * plane), :] * factor)
        return 0

    lax.fori_loop(0, spectral.shape[0] // (4 * plane), planes, 0, unroll=2)


def term(slabs, slab_rows, spectral, visiting, scale, backward, paired):
    count = slabs.shape[0]
    slab = pl.BlockSpec((slab_rows, LANES), lambda i, chosen: (chosen[i], 0))
    whole = pl.BlockSpec(memory_space=pltpu.VMEM)
    cells = count * slab_rows * LANES
    return pl.pallas_call(
        term_body,
        out_shape=jax.ShapeDtypeStruct((count * slab_rows, LANES), jnp.float32),
        grid_spec=pltpu.PrefetchScalarGridSpec(
            num_scalar_prefetch=1,
            grid=(count,),
            in_specs=[slab, slab, pl.BlockSpec(memory_space=pltpu.SMEM), whole, whole],
            out_specs=pl.BlockSpec((slab_rows, LANES), lambda i, chosen: (i, 0)),
        ),
        compiler_params=pltpu.CompilerParams(vmem_limit_bytes=24 << 20),
        cost_estimate=pl.CostEstimate(flops=cells * NG * 12, bytes_accessed=12 * cells, transcendentals=0),
        name="term",
    )(slabs, spectral, visiting, scale, backward, paired)


def position_block(orbital_block, amount):
    bit_count = (lax.axis_size("blk") - 1).bit_length()
    for bit_level in range(bit_count):
        moved_block = passed_along(orbital_block, "blk", 1 << bit_level)
        orbital_block = jnp.where(amount // (1 << bit_level) % 2 == 1, moved_block, orbital_block)
    return orbital_block


def displacement_order(blocks):
    order = []
    for distance in range(1, blocks // 2 + 1):
        order += [distance] if 2 * distance == blocks else [distance, blocks - distance]
    return order + [0]


def shared_visits(orbitals, offsets, replica):
    blocks, replicas = lax.axis_size("blk"), lax.axis_size("rep")
    order = displacement_order(blocks)
    met = (offsets[:, None] + jnp.arange(STEPS, dtype=jnp.int32)[None, :]) % blocks
    visits = []
    for slot in range(blocks // replicas):
        chosen = order[slot * replicas : (slot + 1) * replicas]
        route = [
            ((b - chosen[r]) % blocks * replicas + r, b * replicas + r)
            for b in range(blocks)
            for r in range(replicas)
            if chosen[r] != 0
        ]
        displacement = jnp.asarray(chosen, jnp.int32)[replica]
        moved = lax.ppermute(orbitals, ("blk", "rep"), route)
        if 0 in chosen:
            moved = jnp.where(displacement == 0, orbitals, moved)
        weight = jnp.sum((met == displacement).astype(jnp.float32))
        visits.append((moved, weight))
    return visits


def stepped_visits(orbitals, offsets, replica):
    blocks = lax.axis_size("blk")
    first = position_block(orbitals, (offsets[replica] + STEPS // 2) % blocks)
    visits = [first]
    for distance in range(1, STEPS // 2 + 1):
        visits.append(passed_along(first, "blk", -distance))
        visits.append(passed_along(first, "blk", distance))
    return [(visit, jnp.ones((), jnp.float32)) for visit in visits]


def local(orbitals, offsets):
    blocks, replicas = lax.axis_size("blk"), lax.axis_size("rep")
    replica = lax.axis_index("rep")
    cells = orbitals.shape[1]
    rows = cells // LANES
    slab_rows = rows // replicas
    table = cas_table(NG)
    forward = table.reshape(NG, NG // 2, 2).transpose(0, 2, 1).reshape(NG, NG)
    backward = forward.T
    paired = jnp.kron(jnp.eye(2, dtype=jnp.float32), table)
    kernel = screened_kernel(NG)
    own = orbitals.reshape(rows, LANES)

    if blocks % replicas == 0 and blocks // replicas < STEPS:
        visits = shared_visits(orbitals, offsets, replica)
    else:
        visits = stepped_visits(orbitals, offsets, replica)

    quarter = lax.dynamic_slice_in_dim(orbitals, replica * (cells // replicas), cells // replicas, 1)
    slab_orbitals = lax.all_to_all(quarter, "blk", split_axis=1, concat_axis=0, tiled=True)

    terms = []
    for visit, weight in visits:
        visiting = visit.reshape(rows, LANES)
        spectral = spectrum(own, visiting, kernel, forward, backward, paired)
        terms.append((spectral, visiting, (weight / float(NG**3)).reshape(1)))

    def summed(slabs):
        total = None
        for spectral, visiting, scale in terms:
            part = term(slabs, slab_rows, spectral, visiting, scale, backward, paired)
            total = part if total is None else total + part
        return total

    if replicas == 4:
        low, high = replica % 2, replica // 2
        sent = summed(jnp.stack([1 - low, 3 - low]))
        kept_far = summed((2 * (1 - high) + low).reshape(1))
        kept = summed((2 * high + low).reshape(1))
        met = lax.ppermute(sent, "rep", [(r, r ^ 1) for r in range(replicas)]).reshape(2, slab_rows, LANES)
        far = kept_far + jnp.where(high == 0, met[1], met[0])
        near = kept + jnp.where(high == 0, met[0], met[1])
        exchanged = near + lax.ppermute(far, "rep", [(r, r ^ 2) for r in range(replicas)])
        exchanged = exchanged.reshape(1, cells // replicas)
    else:
        whole = summed(jnp.arange(replicas, dtype=jnp.int32)).reshape(1, cells)
        exchanged = lax.psum_scatter(whole, "rep", scatter_dimension=1, tiled=True)

    slab_exchanged = lax.all_to_all(exchanged, "blk", split_axis=1, concat_axis=0, tiled=True)
    partial_value = jnp.sum(slab_orbitals[:, None, :] * slab_exchanged[None, :, :], axis=2) / float(NG**3)
    gram_rows = lax.psum_scatter(partial_value, "blk", scatter_dimension=0, tiled=True)
    margin = lax.psum(gram_rows, "rep")
    return (exchanged, margin)


def solution(mesh):
    placed = (P(("groups", "blk"), None), P("groups"))
    return jax.shard_map(
        local,
        mesh=mesh,
        in_specs=placed,
        out_specs=(P(("groups", "blk"), "rep"), P(("groups", "blk"), None)),
        check_vma=False,
    )
```

time: 331 us -> 94 us (0.28)
  waiting for transfers between devices: 149 us -> 32.2 us
  matrix products: 64 us -> 0 us
  local copies, waits for them, and re-layouts: 45.4 us -> 3.74 us
  Pallas kernels: 0 us -> 14.8 us
  between operations: 15.8 us -> 2.1 us
  other arithmetic: 21.3 us -> 9.41 us
    ppermute x4 -> x3, waiting for transfers between devices: 111 us -> 21.1 us  [the longest x1 19 us: shared_visits(): moved = lax.ppermute(orbitals, ('blk', 'rep'), route)]
    dot_general x19 -> x0, matrix products: 64 us -> none  [the longest x6 28.7 us: transform(): jnp.einsum('ky,ayz->akz', cas_values, values_field.reshape(batch_size * g...]
    unnamed x2 -> x0, waiting for transfers between devices: 29.9 us -> none
    reshape x15 -> x0, local copies, waits for them, and re-layouts: 23.9 us -> none  [the longest x6 12.4 us: transform(): values_field.reshape(batch_size * grid_points, grid_points, grid_points)]
    pallas_call x0 -> x4, Pallas kernels: none -> 14.8 us  [the longest x1 10 us: spectrum(): pl.pallas_call(spectrum_body, out_shape=jax.ShapeDtypeStruct((rows, LANES...]
    mul x3 -> x2, other arithmetic: 14.4 us -> 0.11 us  [the longest x1 0.1 us: local(): paired = jnp.kron(jnp.eye(2, dtype=jnp.float32), table)]
    transpose x6 -> x0, local copies, waits for them, and re-layouts: 12.1 us -> none  [transform(): jnp.einsum('ky,ayz->akz', cas_values, values_field.reshape(batch_size * g...]
    all_to_all x1, waiting for transfers between devices: 0.01 us -> 5.55 us  [local(): lax.all_to_all(quarter, 'blk', split_axis=1, concat_axis=0, tiled=True)]
  transfers between devices with their start and end apart: 7 -> 5, of which waited for: 6 -> 5; matrix products, arithmetic and copies ran while one was open for 3% -> 9% of each run, Pallas kernels for 0% -> 2%
where the time goes in v1:
time: 94 us; the launch traced here: 93.6 us
  waiting for transfers between devices  32.2 us (34%)
  blocking collectives  16.5 us (18%)
  starting transfers between devices  14.8 us (16%)
  Pallas kernels  14.8 us (16%)
  other arithmetic  9.41 us (10%)
  local copies, waits for them, and re-layouts  3.74 us (4%)
  between operations  2.1 us (2%)
    ppermute x1, waiting for transfers between devices, shared_visits(): moved = lax.ppermute(orbitals, ('blk', 'rep'), route)  19 us
    unnamed x1, blocking collectives  10.3 us
    pallas_call x1, Pallas kernels, spectrum(): pl.pallas_call(spectrum_body, out_shape=jax.ShapeDtypeStruct((rows, LANES...  10 us
    psum x1, blocking collectives, local(): margin = lax.psum(gram_rows, 'rep')  6.27 us
    all_to_all x1, waiting for transfers between devices, local(): lax.all_to_all(exchanged, 'blk', split_axis=1, concat_axis=0, tiled=True)  5.57 us
    all_to_all x1, waiting for transfers between devices, local(): lax.all_to_all(quarter, 'blk', split_axis=1, concat_axis=0, tiled=True)  5.55 us
    ppermute x1, starting transfers between devices, shared_visits(): moved = lax.ppermute(orbitals, ('blk', 'rep'), route)  5.09 us
    pallas_call x3, Pallas kernels, term(): pl.pallas_call(term_body, out_shape=jax.ShapeDtypeStruct((count * slab_ro...  4.77 us
  transfers between devices with their start and end apart: 5, of which 5 were waited for; matrix products, arithmetic and copies ran while one was open for 9% of the time, Pallas kernels for 2%

profile of v1, /device:TPU:0, one launch (start us, length us, event | category | flops | bytes accessed | tf_op | source)
XLA Modules:
  0.0 93.6 jit_solution(15023946059540025774)
XLA Ops:
  0.7 5.1 %collective-permute-start = (f32[1,262144]{1,0:T(1,128)}, f32[1,262144]{1,0:T(1,128)S(1)}, u32[]{:S(2)}, u32[]{:S(2)}) collective-permute-start(f32[1,262144]{1,0:T(1,128)} %param.3), channel_id=1, source_target_pairs={{12,0},{5,1},{10,2},{0,4},{9,5},{14,6},{4,8},{13,9},{2,10},{8,12},... | collective-permute-start | bytes 3145736 | tf_op jit(solution)/shard_map/ppermute | solution.py:229
  6.0 0.6 dynamic_slice.6
  7.6 2.0 %convert_reduce_fusion = f32[]{:T(128)} fusion(s32[]{:T(128)} %bitcast.2, s32[4]{0:T(128)} %param.4), kind=kLoop, calls=%fused_computation.64 | loop fusion | flops 179 | bytes 24 | tf_op jit(solution)/shard_map/reduce_sum | solution.py:232
  10.6 1.7 %multiply_select_fusion.kernel = f32[2048,128]{1,0:T(8,128)S(1)} fusion(s32[128]{0:T(128)S(1)} %get-tuple-element.13, s32[128]{0:T(128)S(1)} %get-tuple-element.14, s32[128]{0:T(128)S(1)} %get-tuple-element.12, s32[128]{0:T(128)S(1)} %get-tuple-element.15, s32[2048]{0:T(1024)S(1)} %get-tuple-element.4, s32[2048]{0:T(1024)S(1)} %get-tuple-element.7, ...), kind=kLoop, calls=%fused_computation.13 | loop fusion | flops 8126464 | bytes 1087744 | tf_op jit(solution)/shard_map/jit(_where)/select_n | solution.py:50
  12.3 19.0 %collective-permute-done = f32[1,262144]{1,0:T(1,128)S(1)} collective-permute-done((f32[1,262144]{1,0:T(1,128)}, f32[1,262144]{1,0:T(1,128)S(1)}, u32[]{:S(2)}, u32[]{:S(2)}) %collective-permute-start) | collective-permute-done | bytes 1048608 | tf_op jit(solution)/shard_map/ppermute | solution.py:229
  31.3 1.1 %broadcast_select_fusion = f32[1,262144]{1,0:T(1,128)S(1)} fusion(f32[1,262144]{1,0:T(1,128)S(1)} %copy-done, f32[1,262144]{1,0:T(1,128)S(1)} %collective-permute-done, pred[]{:T(512)S(6)} %eq.35), kind=kLoop, calls=%fused_computation.3 | loop fusion | flops 262144 | bytes 3145729 | tf_op jit(solution)/shard_map/jit(_where)/select_n | solution.py:231
  32.4 10.0 %spectrum.1.spectral = f32[2048,128]{1,0:T(8,128)S(1)} custom-call(f32[2048,128]{1,0:T(8,128)S(1)} %bitcast.22, f32[2048,128]{1,0:T(8,128)S(1)} %bitcast.18, f32[2048,128]{1,0:T(8,128)S(1)} %multiply_select_fusion.kernel, f32[64,64]{1,0:T(8,128)S(1)} %get-tuple-element.3.forward, f32[64,64]{1,0:T(8,128)S(1)} %get-tuple-element.2.backward, ...), custom_call_target="tpu_custom_call" | custom-call | flops 402653184 | bytes 4194304 | tf_op jit(solution)/shard_map/spectrum/pallas_call | solution.py:145
  42.4 3.0 %term.4 = f32[1024,128]{1,0:T(8,128)} custom-call(s32[2]{0:T(128)S(1)} %pad_add_fusion.chosen, f32[2048,128]{1,0:T(8,128)S(1)} %spectrum.1.spectral, f32[2048,128]{1,0:T(8,128)S(1)} %bitcast.19, f32[1]{0:T(128)} %bitcast.4.scale, f32[64,64]{1,0:T(8,128)S(1)} %get-tuple-element.2.backward, f32[128,128]{1,0:T(8,128)S(1)} %mul.260.paired), custom_call_target="tpu_custom_call" | custom-call | flops 100663296 | bytes 1572864 | tf_op jit(solution)/shard_map/term/pallas_call | solution.py:185
  45.5 0.9 term.5
  46.3 1.4 %collective-permute-done.1 = f32[1024,128]{1,0:T(8,128)} collective-permute-done((f32[1024,128]{1,0:T(8,128)}, f32[1024,128]{1,0:T(8,128)}, u32[]{:S(2)}, u32[]{:S(2)}) %collective-permute-start.1) | collective-permute-done | bytes 524320 | tf_op jit(solution)/shard_map/ppermute | solution.py:286
  47.7 1.8 %select_add_fusion = f32[512,128]{1,0:T(8,128)} fusion(f32[512,128]{1,0:T(8,128)S(1)} %term.5, f32[1024,128]{1,0:T(8,128)} %collective-permute-done.1, pred[]{:T(512)S(6)} %eq.39), kind=kLoop, calls=%fused_computation.16 | loop fusion | flops 131072 | bytes 1048577 | tf_op jit(solution)/shard_map/add | solution.py:287
  49.5 1.5 %collective-permute-start.2 = (f32[512,128]{1,0:T(8,128)}, f32[512,128]{1,0:T(8,128)S(1)}, u32[]{:S(2)}, u32[]{:S(2)}) collective-permute-start(f32[512,128]{1,0:T(8,128)} %select_add_fusion), channel_id=1, source_target_pairs={{0,2},{1,3},{2,0},{3,1},{4,6},{5,7},{6,4},{7,5},{8,10},{9,11},{10,... | collective-permute-start | bytes 786440 | tf_op jit(solution)/shard_map/ppermute | solution.py:289
  51.0 0.7 constant_dynamic-slice_fusion.1
  51.7 4.8 %all-to-all-start = ((f32[1,4,16384]{2,0,1:T(1,128)}), f32[1,4,16384]{2,0,1:T(1,128)S(1)}, u32[]{:S(2)}, u32[]{:S(2)}) async-start(f32[1,4,16384]{2,0,1:T(1,128)} %bitcast.9), calls=%async_computation | async-start | bytes 524288 | tf_op jit(solution)/shard_map/all_to_all | solution.py:266
  56.4 0.9 term.3
  57.3 0.7 collective-permute-done.2
  58.0 1.8 %add_add_fusion = f32[512,128]{1,0:T(8,128)} fusion(f32[512,128]{1,0:T(8,128)S(1)} %collective-permute-done.2, f32[512,128]{1,0:T(8,128)S(1)} %term.3, f32[1024,128]{1,0:T(8,128)} %collective-permute-done.1, pred[]{:T(512)S(6)} %eq.39), kind=kLoop, calls=%fused_computation.17 | loop fusion | flops 196608 | bytes 1310721 | tf_op jit(solution)/shard_map/add | solution.py:289
  59.8 5.6 %all-to-all-done = f32[1,4,16384]{2,0,1:T(1,128)S(1)} async-done(((f32[1,4,16384]{2,0,1:T(1,128)}), f32[1,4,16384]{2,0,1:T(1,128)S(1)}, u32[]{:S(2)}, u32[]{:S(2)}) %all-to-all-start) | async-done | bytes 262176 | tf_op jit(solution)/shard_map/all_to_all | solution.py:266
  65.4 3.4 %all-to-all-start.1 = ((f32[1,4,16384]{2,0,1:T(1,128)}), f32[1,4,16384]{2,0,1:T(1,128)S(1)}, u32[]{:S(2)}, u32[]{:S(2)}) async-start(f32[1,4,16384]{2,0,1:T(1,128)} %bitcast.10), calls=%async_computation.1 | async-start | bytes 524288 | tf_op jit(solution)/shard_map/all_to_all | solution.py:295
  68.8 0.6 copy-done.1
  70.2 5.6 %all-to-all-done.1 = f32[1,4,16384]{2,0,1:T(1,128)S(1)} async-done(((f32[1,4,16384]{2,0,1:T(1,128)}), f32[1,4,16384]{2,0,1:T(1,128)S(1)}, u32[]{:S(2)}, u32[]{:S(2)}) %all-to-all-start.1) | async-done | bytes 262176 | tf_op jit(solution)/shard_map/all_to_all | solution.py:295
  76.3 10.3 %all-reduce = f32[4,4]{1,0:T(4,128)S(1)} all-reduce(f32[4,4]{1,0:T(4,128)S(1)} %broadcast_multiply_fusion.1), channel_id=2, replica_groups=mesh['groups'=2,'blk'=4,'rep'=4] {'blk'}, use_global_device_ids=true, to_apply=%region_2.3.clone | all-reduce | flops 16 | bytes 128
  86.6 0.6 constant_dynamic-slice_fusion
  87.3 6.3 %psum.7 = f32[1,4]{1,0:T(1,128)} all-reduce(f32[1,4]{1,0:T(1,128)S(1)} %constant_dynamic-slice_fusion), channel_id=1, replica_groups=mesh['groups'=2,'blk'=4,'rep'=4] {'rep'}, use_global_device_ids=true, to_apply=%region_3.4 | all-reduce | flops 4 | bytes 32 | tf_op jit(solution)/shard_map/psum | solution.py:298
  (25 shorter events, 2.2 us)
Async XLA Ops:
  0.6 5.4 %copy-start.2 = (s32[4]{0:T(128)S(1)}, s32[4]{0:T(128)}, u32[]{:S(2)}) copy-start(s32[4]{0:T(128)} %constant.136.clone) | copy-start | bytes 52
  0.6 30.6 %copy-start = (f32[1,262144]{1,0:T(1,128)S(1)}, f32[1,262144]{1,0:T(1,128)}, u32[]{:S(2)}) copy-start(f32[1,262144]{1,0:T(1,128)} %param.3) | copy-start | bytes 3145732
  0.7 30.6 %collective-permute-start = (f32[1,262144]{1,0:T(1,128)}, f32[1,262144]{1,0:T(1,128)S(1)}, u32[]{:S(2)}, u32[]{:S(2)}) collective-permute-start(f32[1,262144]{1,0:T(1,128)} %param.3), channel_id=1, source_target_pairs={{12,0},{5,1},{10,2},{0,4},{9,5},{14,6},{4,8},{13,9},{2,10},{8,12},... | collective-permute-start | bytes 3145736 | tf_op jit(solution)/shard_map/ppermute | solution.py:229
  45.5 2.3 %collective-permute-start.1 = (f32[1024,128]{1,0:T(8,128)}, f32[1024,128]{1,0:T(8,128)}, u32[]{:S(2)}, u32[]{:S(2)}) collective-permute-start(f32[1024,128]{1,0:T(8,128)} %term.4), channel_id=1, source_target_pairs={{0,1},{1,0},{2,3},{3,2},{4,5},{5,4},{6,7},{7,6},{8,9},{9,8},{10,11... | collective-permute-start | bytes 1572872 | tf_op jit(solution)/shard_map/ppermute | solution.py:286
  49.5 8.6 %collective-permute-start.2 = (f32[512,128]{1,0:T(8,128)}, f32[512,128]{1,0:T(8,128)S(1)}, u32[]{:S(2)}, u32[]{:S(2)}) collective-permute-start(f32[512,128]{1,0:T(8,128)} %select_add_fusion), channel_id=1, source_target_pairs={{0,2},{1,3},{2,0},{3,1},{4,6},{5,7},{6,4},{7,5},{8,10},{9,11},{10,... | collective-permute-start | bytes 786440 | tf_op jit(solution)/shard_map/ppermute | solution.py:289
  51.7 13.7 %all-to-all-start = ((f32[1,4,16384]{2,0,1:T(1,128)}), f32[1,4,16384]{2,0,1:T(1,128)S(1)}, u32[]{:S(2)}, u32[]{:S(2)}) async-start(f32[1,4,16384]{2,0,1:T(1,128)} %bitcast.9), calls=%async_computation | async-start | bytes 524288 | tf_op jit(solution)/shard_map/all_to_all | solution.py:266
  65.4 10.4 %all-to-all-start.1 = ((f32[1,4,16384]{2,0,1:T(1,128)}), f32[1,4,16384]{2,0,1:T(1,128)S(1)}, u32[]{:S(2)}, u32[]{:S(2)}) async-start(f32[1,4,16384]{2,0,1:T(1,128)} %bitcast.10), calls=%async_computation.1 | async-start | bytes 524288 | tf_op jit(solution)/shard_map/all_to_all | solution.py:295
  68.8 0.7 copy-start.1

commit v2 on v1

v2 whole, which is shorter than its diff:
```python
import functools

import jax
import jax.numpy as jnp
from jax import lax
from jax.experimental import pallas as pl
from jax.experimental.pallas import tpu as pltpu
from jax.sharding import PartitionSpec as P

NG = 64
STEPS = 3
LANES = 128
HALF = LANES // 2
PITCH = NG + 1
MET = (3, 1, 2, 0)
SENT = (3, 1, 2, 1)
screen_scale = 0.05


def passed_along(block, axis, distance):
    devices = range(lax.axis_size(axis))
    route = [((i - distance) % len(devices), i) for i in devices]
    return lax.ppermute(block, axis, route)


def cas_table(grid_points):
    grid_index = jnp.arange(grid_points, dtype=jnp.int32)
    product = grid_index[:, None] * grid_index[None, :] % grid_points
    phase_angle = 2.0 * jnp.pi / grid_points * product.astype(jnp.float32)
    return jnp.cos(phase_angle) + jnp.sin(phase_angle)


def screened_kernel(grid_points):
    def squares(index):
        folded = jnp.where(index <= grid_points // 2, index, index - grid_points).astype(jnp.float32)
        return folded * folded

    shape = (grid_points * grid_points // 2, 2 * grid_points)
    row = lax.broadcasted_iota(jnp.int32, shape, 0)
    lane = lax.broadcasted_iota(jnp.int32, shape, 1)
    k_squared = (
        squares(row % grid_points)
        + squares(2 * (row // grid_points) + lane // grid_points)
        + squares(lane % grid_points)
    )
    safe_square = jnp.maximum(k_squared, 1.0)
    screened = (
        4.0
        * jnp.pi
        / (screen_scale * safe_square)
        * (1.0 - jnp.exp(-screen_scale * safe_square / (4.0 * jnp.pi)))
    )
    return jnp.where(k_squared > 0.5, screened, jnp.ones_like(screened))


def high_low(value):
    high = value.astype(jnp.bfloat16)
    return high, (value - high.astype(jnp.float32)).astype(jnp.bfloat16)


def dot(a, b):
    return lax.dot_general(a, b, (((1,), (0,)), ((), ())), preferred_element_type=jnp.float32)


def swapped(first, second, low_half):
    return (
        jnp.where(low_half, first, pltpu.roll(second, HALF, 1)),
        jnp.where(low_half, pltpu.roll(first, HALF, 1), second),
    )


def left_weights(table):
    high, low = high_low(table)
    return jnp.concatenate([high, high, low], axis=1)


def lane_weights(table):
    high, low = high_low(table)
    return jnp.concatenate(
        [jnp.concatenate([high, low], axis=1), jnp.concatenate([high, jnp.zeros_like(low)], axis=1)],
        axis=0,
    )


def from_left(weights, value):
    high, low = high_low(value)
    return dot(weights, jnp.concatenate([high, low, high], axis=0))


def along_lanes(value, weights):
    high, low = high_low(value)
    both = dot(jnp.concatenate([high, low], axis=1), weights)
    return both[:, :LANES] + both[:, LANES:]


def low_mask(rows):
    return lax.broadcasted_iota(jnp.int32, (rows, LANES), 1) < HALF


def spectrum_body(same, own, *refs):
    *pieces, kernel, forward, backward, paired, out = refs
    alone = same[0] == 1
    plane = NG // 2
    pairs = NG // 2
    mask = low_mask(plane)
    w_forward = left_weights(forward[...])
    w_backward = left_weights(backward[...])
    w_lanes = lane_weights(paired[...])

    def planes(piece, first_row, step, _):
        at = pl.multiple_of(step * (4 * plane), 4 * plane)
        mine = own[pl.ds(at, 4 * plane), :]
        density = mine * jnp.where(alone, mine, piece[pl.ds(at - first_row, 4 * plane), :])
        along_z = along_lanes(density, w_lanes)
        blocks = []
        for half in range(2):
            base = half * 2 * plane
            even, odd = swapped(along_z[base : base + plane], along_z[base + plane : base + 2 * plane], mask)
            blocks.append(jnp.concatenate([even, odd], axis=0))
        along_y = from_left(w_forward, jnp.concatenate(blocks, axis=1))
        out[pl.ds(step * (2 * PITCH), NG), :] = along_y[:, :LANES]
        out[pl.ds(step * (2 * PITCH) + PITCH, NG), :] = along_y[:, LANES:]
        return 0

    each = NG // 4 // len(pieces)
    for index, piece in enumerate(pieces):
        first_row = index * each * 4 * plane
        lax.fori_loop(
            index * each, (index + 1) * each, functools.partial(planes, piece, first_row), 0, unroll=each
        )

    def columns(step, _):
        blocks = []
        for part in range(2):
            row = 4 * step + 2 * part
            first = out[pl.ds(row, pairs, stride=PITCH), :]
            second = out[pl.ds(row + 1, pairs, stride=PITCH), :]
            blocks.append(jnp.concatenate(swapped(first, second, mask), axis=0))
        along_x = from_left(w_forward, jnp.concatenate(blocks, axis=1))
        at = pl.multiple_of(step * (2 * NG), 2 * NG)
        weight = jnp.concatenate([kernel[pl.ds(at, NG), :], kernel[pl.ds(at + NG, NG), :]], axis=1)
        returned = from_left(w_backward, along_x * weight)
        for part in range(2):
            block = returned[:, part * LANES : (part + 1) * LANES]
            first, second = swapped(block[:plane], block[plane:], mask)
            row = 4 * step + 2 * part
            out[pl.ds(row, pairs, stride=PITCH), :] = first
            out[pl.ds(row + 1, pairs, stride=PITCH), :] = second
        return 0

    lax.fori_loop(0, NG // 4, columns, 0, unroll=16)


def spectrum(same, own, pieces, kernel, forward, backward, paired):
    rows = own.shape[0]
    vmem = pl.BlockSpec(memory_space=pltpu.VMEM)
    return pl.pallas_call(
        spectrum_body,
        out_shape=jax.ShapeDtypeStruct((NG // 2 * PITCH, LANES), jnp.float32),
        in_specs=[pl.BlockSpec(memory_space=pltpu.SMEM)] + [vmem] * (5 + len(pieces)),
        out_specs=vmem,
        compiler_params=pltpu.CompilerParams(vmem_limit_bytes=24 << 20),
        cost_estimate=pl.CostEstimate(
            flops=rows * LANES * NG * 24, bytes_accessed=16 * rows * LANES, transcendentals=0
        ),
        name="spectrum",
    )(same, own, *pieces, kernel, forward, backward, paired)


def term_body(chosen, same, spectral, own, *refs):
    *pieces, backward, paired, out = refs
    plane = NG // 2
    mask = low_mask(plane)
    w_backward = left_weights(backward[...])
    w_lanes = lane_weights(paired[...])
    slab_rows = out.shape[0]
    slab = chosen[pl.program_id(0)]
    each = own.shape[0] // len(pieces)
    alone = same[0] == 1

    def partner(at):
        row = pl.multiple_of(slab * slab_rows, slab_rows) + at
        value = pieces[0][pl.ds(row % each, 4 * plane), :]
        for index in range(1, len(pieces)):
            value = jnp.where(row // each == index, pieces[index][pl.ds(row % each, 4 * plane), :], value)
        return jnp.where(alone, own[pl.ds(row, 4 * plane), :], value)

    def planes(step, _):
        at = pl.multiple_of(step * (4 * plane), 4 * plane)
        row = step * (2 * PITCH)
        pair = jnp.concatenate([spectral[pl.ds(row, NG), :], spectral[pl.ds(row + PITCH, NG), :]], axis=1)
        along_y = from_left(w_backward, pair)
        blocks = []
        for half in range(2):
            block = along_y[:, half * LANES : (half + 1) * LANES]
            blocks.extend(swapped(block[:plane], block[plane:], mask))
        potential = along_lanes(jnp.concatenate(blocks, axis=0), w_lanes)
        out[pl.ds(at, 4 * plane), :] = potential * (partner(at) * (1.0 / NG**3))
        return 0

    lax.fori_loop(0, slab_rows // (4 * plane), planes, 0, unroll=4)


def term(slabs, slab_rows, same, spectral, own, pieces, backward, paired):
    count = slabs.shape[0]
    pitched = pl.BlockSpec((slab_rows // NG * PITCH, LANES), lambda i, chosen: (chosen[i], 0))
    whole = pl.BlockSpec(memory_space=pltpu.VMEM)
    cells = count * slab_rows * LANES
    return pl.pallas_call(
        term_body,
        out_shape=jax.ShapeDtypeStruct((count * slab_rows, LANES), jnp.float32),
        grid_spec=pltpu.PrefetchScalarGridSpec(
            num_scalar_prefetch=1,
            grid=(count,),
            in_specs=[pl.BlockSpec(memory_space=pltpu.SMEM), pitched, whole] + [whole] * (2 + len(pieces)),
            out_specs=pl.BlockSpec((slab_rows, LANES), lambda i, chosen: (i, 0)),
        ),
        compiler_params=pltpu.CompilerParams(vmem_limit_bytes=24 << 20),
        cost_estimate=pl.CostEstimate(flops=cells * NG * 12, bytes_accessed=12 * cells, transcendentals=0),
        name="term",
    )(slabs, same, spectral, own, *pieces, backward, paired)


def blend_body(weights, kept, met, *refs, first):
    *more, out = refs
    rows = out.shape[0]
    at = 0 if first else rows
    value = weights[0] * kept[at : at + rows, :] + weights[1] * met[at : at + rows, :]
    out[...] = value + more[0][...] if more else value


def blend(weights, kept, met, *more):
    rows = kept.shape[0] // 2
    vmem = pl.BlockSpec(memory_space=pltpu.VMEM)
    return pl.pallas_call(
        functools.partial(blend_body, first=not more),
        out_shape=jax.ShapeDtypeStruct((rows, LANES), jnp.float32),
        in_specs=[pl.BlockSpec(memory_space=pltpu.SMEM)] + [vmem] * (2 + len(more)),
        out_specs=vmem,
        compiler_params=pltpu.CompilerParams(vmem_limit_bytes=16 << 20),
        cost_estimate=pl.CostEstimate(flops=4 * rows * LANES, bytes_accessed=16 * rows * LANES, transcendentals=0),
        name="blend",
    )(weights, kept, met, *more)


def gram_body(places, factors, kept, met, own, *refs):
    *stores, out = refs
    visits, nears, evens, odds = stores[0:2], stores[2:4], stores[4:6], stores[6:8]
    slab_rows = kept.shape[0] // 2
    chunk = 64
    parity = places[6]

    def folded(value):
        return jnp.sum(value.reshape(chunk // 8, 8, LANES), axis=0)

    totals = (jnp.zeros((8, LANES), jnp.float32),) * 8
    for side in range(2):
        term_row = pl.multiple_of(places[4 + side], slab_rows)
        half_row = pl.multiple_of(parity * slab_rows, slab_rows)

        def step(index, totals, side=side, term_row=term_row, half_row=half_row):
            at = pl.multiple_of(index * chunk, chunk)
            terms = (kept[pl.ds(term_row + at, chunk), :], met[pl.ds(term_row + at, chunk), :])
            orbitals = (
                own[pl.ds(side * 2 * slab_rows + half_row + at, chunk), :],
                visits[side][pl.ds(half_row + at, chunk), :],
                nears[side][pl.ds(half_row + at, chunk), :],
                evens[side][pl.ds(at, chunk), :] + odds[side][pl.ds(at, chunk), :],
            )
            return tuple(
                totals[4 * t + o] + folded(terms[t] * orbitals[o]) for t in range(2) for o in range(4)
            )

        totals = lax.fori_loop(0, slab_rows // chunk, step, totals, unroll=2)
    lane = lax.broadcasted_iota(jnp.int32, (8, LANES), 1)
    result = jnp.zeros((8, LANES), jnp.float32)
    for o in range(4):
        value = jnp.sum(factors[o] * totals[o] + factors[4 + o] * totals[4 + o], axis=(0, 1), keepdims=True)
        result = jnp.where(lane == places[o], value, result)
    out[...] = result


def gram(places, factors, kept, met, own, *stores):
    rows = kept.shape[0]
    smem = pl.BlockSpec(memory_space=pltpu.SMEM)
    vmem = pl.BlockSpec(memory_space=pltpu.VMEM)
    return pl.pallas_call(
        gram_body,
        out_shape=jax.ShapeDtypeStruct((8, LANES), jnp.float32),
        in_specs=[smem, smem] + [vmem] * (3 + len(stores)),
        out_specs=vmem,
        compiler_params=pltpu.CompilerParams(vmem_limit_bytes=24 << 20),
        cost_estimate=pl.CostEstimate(flops=16 * rows * LANES, bytes_accessed=24 * rows * LANES, transcendentals=0),
        name="gram",
    )(places, factors, kept, met, own, *stores)


def position_block(orbital_block, amount):
    bit_count = (lax.axis_size("blk") - 1).bit_length()
    for bit_level in range(bit_count):
        moved_block = passed_along(orbital_block, "blk", 1 << bit_level)
        orbital_block = jnp.where(amount // (1 << bit_level) % 2 == 1, moved_block, orbital_block)
    return orbital_block


def stepped(orbitals, offsets, tables):
    blocks, replicas = lax.axis_size("blk"), lax.axis_size("rep")
    replica = lax.axis_index("rep")
    cells = orbitals.shape[1]
    rows = cells // LANES
    kernel, forward, backward, paired = tables
    first = position_block(orbitals, (offsets[replica] + STEPS // 2) % blocks)
    visits = [first]
    for distance in range(1, STEPS // 2 + 1):
        visits.append(passed_along(first, "blk", -distance))
        visits.append(passed_along(first, "blk", distance))
    own = orbitals.reshape(rows, LANES)
    apart = jnp.zeros((1,), jnp.int32)
    slabs = jnp.arange(replicas, dtype=jnp.int32)
    whole = jnp.zeros((rows, LANES), jnp.float32)
    for visit in visits:
        pieces = [visit.reshape(rows, LANES)]
        spectral = spectrum(apart, own, pieces, kernel, forward, backward, paired)
        whole = whole + term(slabs, rows // replicas, apart, spectral, own, pieces, backward, paired)
    exchanged = lax.psum_scatter(whole.reshape(1, cells), "rep", scatter_dimension=1, tiled=True)
    quarter = lax.dynamic_slice_in_dim(orbitals, replica * (cells // replicas), cells // replicas, 1)
    slab_orbitals = lax.all_to_all(quarter, "blk", split_axis=1, concat_axis=0, tiled=True)
    slab_exchanged = lax.all_to_all(exchanged, "blk", split_axis=1, concat_axis=0, tiled=True)
    partial_value = lax.dot_general(
        slab_orbitals, slab_exchanged, (((1,), (1,)), ((), ())), precision=lax.Precision.HIGHEST
    ) / float(NG**3)
    gram_rows = lax.psum_scatter(partial_value, "blk", scatter_dimension=0, tiled=True)
    return exchanged, lax.psum(gram_rows, "rep")


def folded(orbitals, offsets, tables):
    blocks, replicas = lax.axis_size("blk"), lax.axis_size("rep")
    block, replica = lax.axis_index("blk"), lax.axis_index("rep")
    low, high = replica % 2, replica // 2
    cells = orbitals.shape[1]
    rows = cells // LANES
    slab_rows = rows // replicas
    kernel, forward, backward, paired = tables
    own = orbitals.reshape(rows, LANES)
    met_by = jnp.asarray(MET, jnp.int32)
    sent_to = jnp.asarray(SENT, jnp.int32)
    same = (met_by[replica] == 0).astype(jnp.int32).reshape(1)

    def along_blocks(value):
        route = [((b ^ SENT[r]) * replicas + r, b * replicas + r) for b in range(blocks) for r in range(replicas)]
        return lax.ppermute(value, ("blk", "rep"), route)

    def replica_swap(value, bit):
        return lax.ppermute(value, "rep", [(r, r ^ bit) for r in range(replicas)])

    def from_even(value, to_odd):
        return lax.ppermute(value, "rep", [(r, (r ^ 2) + to_odd) for r in range(0, replicas, 2)])

    pieces, nears, evens, odds = [], [], [], []
    for side in range(2):
        piece = along_blocks(own[side * rows // 2 : (side + 1) * rows // 2])
        pieces.append(piece)
    for piece in pieces:
        evens.append(from_even(piece[:slab_rows], 0))
        odds.append(from_even(piece[slab_rows:], 1))
        nears.append(replica_swap(piece, 1))

    spectral = spectrum(same, own, pieces, kernel, forward, backward, paired)
    far_side, near_side = 2 * (1 - high), 2 * high
    sent = term(
        jnp.stack([far_side + 1 - low, near_side + 1 - low]), slab_rows, same, spectral, own, pieces, backward, paired
    )
    kept = term(jnp.stack([far_side + low, near_side + low]), slab_rows, same, spectral, own, pieces, backward, paired)
    met = replica_swap(sent, 1)

    occurs = (offsets[:, None] + jnp.arange(STEPS, dtype=jnp.int32)[None, :]) % blocks
    counts = jnp.sum((occurs[:, :, None] == jnp.arange(blocks, dtype=jnp.int32)).astype(jnp.float32), axis=(0, 1))
    partners = block ^ jnp.stack([met_by[replica], met_by[replica ^ 1]])
    weights = counts[(block - partners) % blocks]
    far = blend(weights, kept, met)
    arrived = replica_swap(far, 2)
    exchanged = blend(weights, kept, met, arrived).reshape(1, cells // replicas)

    others = block ^ jnp.stack(
        [jnp.zeros_like(block), sent_to[replica], sent_to[replica ^ 1], sent_to[(replica ^ 2) // 2 * 2]]
    )
    factors = counts[(others[None, :] - partners[:, None]) % blocks].reshape(-1) / float(NG**3)
    places = jnp.concatenate([others, jnp.stack([(1 - high) * slab_rows, high * slab_rows, low])])
    rows_of = gram(places.astype(jnp.int32), factors, kept, met, own, *pieces, *nears, *evens, *odds)
    rows_of = rows_of + replica_swap(rows_of, 1)
    rows_of = rows_of + replica_swap(rows_of, 2)
    return exchanged, rows_of[:1, :blocks]


def local(orbitals, offsets):
    blocks, replicas = lax.axis_size("blk"), lax.axis_size("rep")
    table = cas_table(NG)
    forward = table.reshape(NG, NG // 2, 2).transpose(0, 2, 1).reshape(NG, NG)
    paired = jnp.kron(jnp.eye(2, dtype=jnp.float32), table)
    tables = screened_kernel(NG), forward, forward.T, paired
    if blocks == replicas == len(MET):
        return folded(orbitals, offsets, tables)
    return stepped(orbitals, offsets, tables)


def solution(mesh):
    placed = (P(("groups", "blk"), None), P("groups"))
    return jax.shard_map(
        local,
        mesh=mesh,
        in_specs=placed,
        out_specs=(P(("groups", "blk"), "rep"), P(("groups", "blk"), None)),
        check_vma=False,
    )
```

time: 94 us -> 71 us (0.76)
  blocking collectives: 16.5 us -> 0 us
  waiting for transfers between devices: 32.2 us -> 21.7 us
  starting transfers between devices: 14.8 us -> 19.7 us
  local copies, waits for them, and re-layouts: 3.74 us -> 6.52 us
  other arithmetic: 9.41 us -> 7.55 us
  Pallas kernels: 14.8 us -> 13.5 us
    ppermute x3 -> x12, starting transfers between devices: 6.59 us -> 19.7 us  [the longest x4 9.96 us: from_even(): lax.ppermute(value, 'rep', [(r, (r ^ 2) + to_odd) for r in range(0, repli...]
    all_to_all x2 -> x0, waiting for transfers between devices: 11.1 us -> none  [the longest x1 5.57 us: local(): lax.all_to_all(exchanged, 'blk', split_axis=1, concat_axis=0, tiled=True)]
    unnamed x1 -> x0, blocking collectives: 10.3 us -> none
    all_to_all x2 -> x0, starting transfers between devices: 8.16 us -> none  [the longest x1 4.76 us: local(): lax.all_to_all(quarter, 'blk', split_axis=1, concat_axis=0, tiled=True)]
    psum x1 -> x0, blocking collectives: 6.27 us -> none  [local(): margin = lax.psum(gram_rows, 'rep')]
    add x2, other arithmetic: 3.55 us -> 0.01 us  [the longest x1 0.01 us: folded(): rows_of = rows_of + replica_swap(rows_of, 1)]
    slice x0 -> x4, local copies, waits for them, and re-layouts: none -> 3.45 us  [the longest x2 1.65 us: folded(): odds.append(from_even(piece[slab_rows:], 1))]
    xor x0 -> x2, other arithmetic: none -> 3.37 us  [the longest x1 1.94 us: folded(): block ^ jnp.stack([jnp.zeros_like(block), sent_to[replica], sent_to[repli...]
  transfers between devices with their start and end apart: 5 -> 12, of which waited for: 5 -> 5; matrix products, arithmetic and copies ran while one was open for 9% -> 17% of each run, Pallas kernels for 2% -> 7%
where the time goes in v2:
time: 71 us; the launch traced here: 70.5 us
  waiting for transfers between devices  21.7 us (31%)
  starting transfers between devices  19.7 us (28%)
  Pallas kernels  13.5 us (19%)
  other arithmetic  7.55 us (11%)
  local copies, waits for them, and re-layouts  6.52 us (9%)
  between operations  1.58 us (2%)
    ppermute x2, waiting for transfers between devices, along_blocks(): return lax.ppermute(value, ('blk', 'rep'), route)  14.3 us
    ppermute x4, starting transfers between devices, from_even(): lax.ppermute(value, 'rep', [(r, (r ^ 2) + to_odd) for r in range(0, repli...  9.96 us
    ppermute x2, starting transfers between devices, along_blocks(): return lax.ppermute(value, ('blk', 'rep'), route)  5.22 us
    pallas_call x2, Pallas kernels, term(): pl.pallas_call(term_body, out_shape=jax.ShapeDtypeStruct((count * slab_ro...  4.71 us
    ppermute x6, starting transfers between devices, replica_swap(): return lax.ppermute(value, 'rep', [(r, r ^ bit) for r in range(replicas)])  4.48 us
    ppermute x6, waiting for transfers between devices, replica_swap(): return lax.ppermute(value, 'rep', [(r, r ^ bit) for r in range(replicas)])  4.01 us
    pallas_call x1, Pallas kernels, spectrum(): pl.pallas_call(spectrum_body, out_shape=jax.ShapeDtypeStruct((NG // 2 * P...  3.84 us
    ppermute x4, waiting for transfers between devices, from_even(): lax.ppermute(value, 'rep', [(r, (r ^ 2) + to_odd) for r in range(0, repli...  3.45 us
  transfers between devices with their start and end apart: 12, of which 5 were waited for; matrix products, arithmetic and copies ran while one was open for 17% of the time, Pallas kernels for 7%

profile of v2, /device:TPU:0, one launch (start us, length us, event | category | flops | bytes accessed | tf_op | source)
XLA Modules:
  0.0 70.5 jit_solution(2699978096748544487)
XLA Ops:
  0.7 1.3 %fusion.37 = (f32[1,131072]{1,0:T(1,128)S(1)}, f32[1,131072]{1,0:T(1,128)S(1)}) fusion(f32[1,262144]{1,0:T(1,128)} %param.4), kind=kLoop, calls=%fused_computation.92 | loop fusion | bytes 2097152 | tf_op jit(solution)/shard_map/slice | solution.py:361
  2.0 5.1 %collective-permute-start = (f32[1024,128]{1,0:T(8,128)S(1)}, f32[1024,128]{1,0:T(8,128)S(1)}, u32[]{:S(2)}, u32[]{:S(2)}) collective-permute-start(f32[1024,128]{1,0:T(8,128)S(1)} %bitcast.22), channel_id=1, source_target_pairs={{12,0},{5,1},{10,2},{7,3},{8,4},{1,5},{14,6},{3,7},{4,8},{13,9},{2... | collective-permute-start | bytes 1572872 | tf_op jit(solution)/shard_map/ppermute | solution.py:351
  8.8 1.4 %add_xor_fusion.2 = s32[2]{0:T(128)S(1)} fusion(s32[1]{0:T(128)} %get-tuple-element.15, s32[1]{0:T(128)} %get-tuple-element.16, s32[]{:T(128)S(6)} %axis_index.23), kind=kLoop, calls=%fused_computation.88 | loop fusion | flops 4 | bytes 20 | tf_op jit(solution)/shard_map/xor | solution.py:378
  10.3 1.9 %add_xor_fusion.1 = s32[4]{0:T(128)S(1)} fusion(s32[1]{0:T(128)} %get-tuple-element.9, s32[1]{0:T(128)} %get-tuple-element.10, s32[1]{0:T(128)} %get-tuple-element.8, s32[1]{0:T(128)} %constant.154.clone.1, s32[]{:T(128)S(6)} %axis_index.23), kind=kLoop, calls=%fused_computation.86 | loop fusion | flops 16 | bytes 36 | tf_op jit(solution)/shard_map/xor | solution.py:384
  12.3 1.4 %fusion.35 = s32[2]{0:T(128)S(1)} fusion(s32[1,1]{0,1:T(1,128)} %bitcast.1, s32[1,1]{0,1:T(1,128)} %bitcast, s32[]{:T(128)S(6)} %axis_index.23), kind=kLoop, calls=%fused_computation.81 | loop fusion | flops 34 | bytes 20 | tf_op jit(solution)/shard_map/select_n | solution.py:379
  14.6 1.7 %multiply_select_fusion.refs_2_ = f32[2048,128]{1,0:T(8,128)S(1)} fusion(s32[128]{0:T(128)S(1)} %get-tuple-element.26, s32[128]{0:T(128)S(1)} %get-tuple-element.27, s32[128]{0:T(128)S(1)} %get-tuple-element.25, s32[128]{0:T(128)S(1)} %get-tuple-element.28, s32[2048]{0:T(1024)S(1)} %get-tuple-element.17, s32[2048]{0:T(1024)S(1)} %get-tuple-element.20, ...), kind=kLoop, calls=%fused_computation.13 | loop fusion | flops 8126464 | bytes 1087744 | tf_op jit(solution)/shard_map/jit(_where)/select_n | solution.py:53
  16.3 3.6 %collective-permute-done.refs_0_ = f32[1024,128]{1,0:T(8,128)S(1)} collective-permute-done((f32[1024,128]{1,0:T(8,128)S(1)}, f32[1024,128]{1,0:T(8,128)S(1)}, u32[]{:S(2)}, u32[]{:S(2)}) %collective-permute-start) | collective-permute-done | bytes 524320 | tf_op jit(solution)/shard_map/ppermute | solution.py:351
  19.9 10.6 %collective-permute-done.1.refs_1_ = f32[1024,128]{1,0:T(8,128)S(1)} collective-permute-done((f32[1024,128]{1,0:T(8,128)S(1)}, f32[1024,128]{1,0:T(8,128)S(1)}, u32[]{:S(2)}, u32[]{:S(2)}) %collective-permute-start.1) | collective-permute-done | bytes 524320 | tf_op jit(solution)/shard_map/ppermute | solution.py:351
  30.5 3.8 %spectrum.1.spectral = f32[2080,128]{1,0:T(8,128)S(1)} custom-call(s32[1]{0:T(128)S(6)} %convert_element_type.51.same, f32[2048,128]{1,0:T(8,128)S(1)} %bitcast.17, f32[1024,128]{1,0:T(8,128)S(1)} %collective-permute-done.refs_0_, f32[1024,128]{1,0:T(8,128)S(1)} %collective-permute-done.1.refs_1_, f32[2048,128]{1,0:T(8,128)S(1)} %multiply_select_fusion.refs_2_, ...), custom_call_target="tpu_custom_call" | custom-call | flops 402653184 | bytes 4194304 | tf_op jit(solution)/shard_map/spectrum/pallas_call | solution.py:157
  34.4 2.7 %term.3 = f32[1024,128]{1,0:T(8,128)} custom-call(s32[2]{0:T(128)S(1)} %pad_add_fusion.1.chosen, s32[1]{0:T(128)S(6)} %convert_element_type.51.same, f32[2080,128]{1,0:T(8,128)S(1)} %spectrum.1.spectral, f32[2048,128]{1,0:T(8,128)S(1)} %bitcast.18, f32[1024,128]{1,0:T(8,128)S(1)} %collective-permute-done.refs_0_, ...), custom_call_target="tpu_custom_call" | custom-call | flops 100663296 | bytes 1572864 | tf_op jit(solution)/shard_map/term/pallas_call | solution.py:209
  37.9 2.3 %collective-permute-start.6 = (f32[512,128]{1,0:T(8,128)}, f32[512,128]{1,0:T(8,128)S(1)}, u32[]{:S(2)}, u32[]{:S(2)}) collective-permute-start(f32[512,128]{1,0:T(8,128)} %get-tuple-element.7), channel_id=1, source_target_pairs={{0,2},{2,0},{4,6},{6,4},{8,10},{10,8},{12,14},{14,12},{16,18},{18,... | collective-permute-start | bytes 786440 | tf_op jit(solution)/shard_map/ppermute | solution.py:357
  40.2 0.8 %fusion.38 = (f32[512,128]{1,0:T(8,128)}, f32[512,128]{1,0:T(8,128)}) fusion(f32[1024,128]{1,0:T(8,128)S(1)} %collective-permute-done.1.refs_1_), kind=kLoop, calls=%fused_computation.93 | loop fusion | bytes 1048576 | tf_op jit(solution)/shard_map/slice | solution.py:365
  41.1 3.5 %collective-permute-start.7 = (f32[512,128]{1,0:T(8,128)}, f32[512,128]{1,0:T(8,128)}, u32[]{:S(2)}, u32[]{:S(2)}) collective-permute-start(f32[512,128]{1,0:T(8,128)} %get-tuple-element.5), channel_id=1, source_target_pairs={{0,2},{2,0},{4,6},{6,4},{8,10},{10,8},{12,14},{14,12},{16,18},{18,... | collective-permute-start | bytes 786440 | tf_op jit(solution)/shard_map/ppermute | solution.py:357
  45.9 2.0 %term.2.kept = f32[1024,128]{1,0:T(8,128)S(1)} custom-call(s32[2]{0:T(128)S(1)} %pad_add_fusion.chosen, s32[1]{0:T(128)S(6)} %convert_element_type.51.same, f32[2080,128]{1,0:T(8,128)S(1)} %spectrum.1.spectral, f32[2048,128]{1,0:T(8,128)S(1)} %bitcast.19, f32[1024,128]{1,0:T(8,128)S(1)} %collective-permute-done.refs_0_, ...), custom_call_target="tpu_custom_call" | custom-call | flops 100663296 | bytes 1572864 | tf_op jit(solution)/shard_map/term/pallas_call | solution.py:209
  47.9 2.0 %collective-permute-start.8 = (f32[512,128]{1,0:T(8,128)}, f32[512,128]{1,0:T(8,128)S(1)}, u32[]{:S(2)}, u32[]{:S(2)}) collective-permute-start(f32[512,128]{1,0:T(8,128)} %get-tuple-element.6), channel_id=1, source_target_pairs={{0,3},{2,1},{4,7},{6,5},{8,11},{10,9},{12,15},{14,13},{16,19},{18,... | collective-permute-start | bytes 786440 | tf_op jit(solution)/shard_map/ppermute | solution.py:357
  50.0 1.1 %blend.2 = f32[512,128]{1,0:T(8,128)S(1)} custom-call(f32[2]{0:T(128)S(1)} %gather_fusion, f32[1024,128]{1,0:T(8,128)S(1)} %term.2.kept, f32[1024,128]{1,0:T(8,128)} %collective-permute-done.2.met), custom_call_target="tpu_custom_call" | custom-call | flops 262144 | bytes 1048576 | tf_op jit(solution)/shard_map/blend/pallas_call | solution.py:235
  51.8 2.1 %collective-permute-start.9 = (f32[512,128]{1,0:T(8,128)}, f32[512,128]{1,0:T(8,128)}, u32[]{:S(2)}, u32[]{:S(2)}) collective-permute-start(f32[512,128]{1,0:T(8,128)} %get-tuple-element.4), channel_id=1, source_target_pairs={{0,3},{2,1},{4,7},{6,5},{8,11},{10,9},{12,15},{14,13},{16,19},{18,... | collective-permute-start | bytes 786440 | tf_op jit(solution)/shard_map/ppermute | solution.py:357
  54.0 1.6 %collective-permute-start.3 = (f32[512,128]{1,0:T(8,128)S(1)}, f32[512,128]{1,0:T(8,128)}, u32[]{:S(2)}, u32[]{:S(2)}) collective-permute-start(f32[512,128]{1,0:T(8,128)S(1)} %blend.2), channel_id=1, source_target_pairs={{0,2},{1,3},{2,0},{3,1},{4,6},{5,7},{6,4},{7,5},{8,10},{9,11},{10,... | collective-permute-start | bytes 786440 | tf_op jit(solution)/shard_map/ppermute | solution.py:354
  56.3 3.4 %collective-permute-done.9.refs_7_ = f32[512,128]{1,0:T(8,128)} collective-permute-done((f32[512,128]{1,0:T(8,128)}, f32[512,128]{1,0:T(8,128)}, u32[]{:S(2)}, u32[]{:S(2)}) %collective-permute-start.9) | collective-permute-done | bytes 262176 | tf_op jit(solution)/shard_map/ppermute | solution.py:357
  59.8 2.0 %gram.1 = f32[8,128]{1,0:T(8,128)S(1)} custom-call(s32[7]{0:T(128)S(1)} %pad_add_fusion.2.places, f32[8]{0:T(128)S(1)} %broadcast_multiply_fusion.1.factors, f32[1024,128]{1,0:T(8,128)S(1)} %copy-done.2, f32[1024,128]{1,0:T(8,128)} %collective-permute-done.2.met, f32[2048,128]{1,0:T(8,128)S(1)} %bitcast.20, f32[1024,128]{1,0:T(8,128)S(1)} %collective-permute-done.refs_0_, ...), custom_call_target="tpu_custom_call" | custom-call | flops 2097152 | bytes 3145728 | tf_op jit(solution)/shard_map/gram/pallas_call | solution.py:287
  61.8 1.9 %collective-permute-start.10 = (f32[8,128]{1,0:T(8,128)S(1)}, f32[8,128]{1,0:T(8,128)S(1)}, u32[]{:S(2)}, u32[]{:S(2)}) collective-permute-start(f32[8,128]{1,0:T(8,128)S(1)} %gram.1), channel_id=1, source_target_pairs={{0,1},{1,0},{2,3},{3,2},{4,5},{5,4},{6,7},{7,6},{8,9},{9,8},{10,11... | collective-permute-start | bytes 12296 | tf_op jit(solution)/shard_map/ppermute | solution.py:354
  63.7 0.8 %collective-permute-done.10 = f32[8,128]{1,0:T(8,128)S(1)} collective-permute-done((f32[8,128]{1,0:T(8,128)S(1)}, f32[8,128]{1,0:T(8,128)S(1)}, u32[]{:S(2)}, u32[]{:S(2)}) %collective-permute-start.10) | collective-permute-done | bytes 4128 | tf_op jit(solution)/shard_map/ppermute | solution.py:354
  65.0 3.2 %collective-permute-done.11 = f32[8,128]{1,0:T(8,128)S(1)} collective-permute-done((f32[8,128]{1,0:T(8,128)S(1)}, f32[8,128]{1,0:T(8,128)S(1)}, u32[]{:S(2)}, u32[]{:S(2)}) %collective-permute-start.11) | collective-permute-done | bytes 4128 | tf_op jit(solution)/shard_map/ppermute | solution.py:354
  68.7 1.9 %blend.3 = f32[512,128]{1,0:T(8,128)} custom-call(f32[2]{0:T(128)S(1)} %gather_fusion, f32[1024,128]{1,0:T(8,128)S(1)} %copy-done.2, f32[1024,128]{1,0:T(8,128)} %collective-permute-done.2.met, f32[512,128]{1,0:T(8,128)} %collective-permute-done.3.refs_0_), custom_call_target="tpu_custom_call" | custom-call | flops 262144 | bytes 1048576 | tf_op jit(solution)/shard_map/blend/pallas_call | solution.py:235
  (54 shorter events, 6.5 us)
Async XLA Ops:
  0.6 7.5 %copy-start.3 = (s32[4]{0:T(128)S(1)}, s32[4]{0:T(128)}, u32[]{:S(2)}) copy-start(s32[4]{0:T(128)} %constant.169.clone) | copy-start | bytes 52
  0.6 7.5 %copy-start.4 = (s32[4]{0:T(128)S(1)}, s32[4]{0:T(128)}, u32[]{:S(2)}) copy-start(s32[4]{0:T(128)} %constant.168.clone) | copy-start | bytes 52
  0.7 7.2 %copy-start.5 = (s32[4]{0:T(128)S(1)}, s32[4]{0:T(128)}, u32[]{:S(2)}) copy-start(s32[4]{0:T(128)} %param.5) | copy-start | bytes 52
  2.0 28.6 %copy-start = (f32[1,262144]{1,0:T(1,128)S(1)}, f32[1,262144]{1,0:T(1,128)}, u32[]{:S(2)}) copy-start(f32[1,262144]{1,0:T(1,128)} %param.4) | copy-start | bytes 3145732
  2.0 17.9 %collective-permute-start = (f32[1024,128]{1,0:T(8,128)S(1)}, f32[1024,128]{1,0:T(8,128)S(1)}, u32[]{:S(2)}, u32[]{:S(2)}) collective-permute-start(f32[1024,128]{1,0:T(8,128)S(1)} %bitcast.22), channel_id=1, source_target_pairs={{12,0},{5,1},{10,2},{7,3},{8,4},{1,5},{14,6},{3,7},{4,8},{13,9},{2... | collective-permute-start | bytes 1572872 | tf_op jit(solution)/shard_map/ppermute | solution.py:351
  7.1 23.4 %collective-permute-start.1 = (f32[1024,128]{1,0:T(8,128)S(1)}, f32[1024,128]{1,0:T(8,128)S(1)}, u32[]{:S(2)}, u32[]{:S(2)}) collective-permute-start(f32[1024,128]{1,0:T(8,128)S(1)} %bitcast.21), channel_id=1, source_target_pairs={{12,0},{5,1},{10,2},{7,3},{8,4},{1,5},{14,6},{3,7},{4,8},{13,9},{2... | collective-permute-start | bytes 1572872 | tf_op jit(solution)/shard_map/ppermute | solution.py:351
  37.1 10.8 %collective-permute-start.2 = (f32[1024,128]{1,0:T(8,128)}, f32[1024,128]{1,0:T(8,128)}, u32[]{:S(2)}, u32[]{:S(2)}) collective-permute-start(f32[1024,128]{1,0:T(8,128)} %term.3), channel_id=1, source_target_pairs={{0,1},{1,0},{2,3},{3,2},{4,5},{5,4},{6,7},{7,6},{8,9},{9,8},{10,11... | collective-permute-start | bytes 1572872 | tf_op jit(solution)/shard_map/ppermute | solution.py:354
  37.9 13.9 %collective-permute-start.6 = (f32[512,128]{1,0:T(8,128)}, f32[512,128]{1,0:T(8,128)S(1)}, u32[]{:S(2)}, u32[]{:S(2)}) collective-permute-start(f32[512,128]{1,0:T(8,128)} %get-tuple-element.7), channel_id=1, source_target_pairs={{0,2},{2,0},{4,6},{6,4},{8,10},{10,8},{12,14},{14,12},{16,18},{18,... | collective-permute-start | bytes 786440 | tf_op jit(solution)/shard_map/ppermute | solution.py:357
  41.1 12.9 %collective-permute-start.7 = (f32[512,128]{1,0:T(8,128)}, f32[512,128]{1,0:T(8,128)}, u32[]{:S(2)}, u32[]{:S(2)}) collective-permute-start(f32[512,128]{1,0:T(8,128)} %get-tuple-element.5), channel_id=1, source_target_pairs={{0,2},{2,0},{4,6},{6,4},{8,10},{10,8},{12,14},{14,12},{16,18},{18,... | collective-permute-start | bytes 786440 | tf_op jit(solution)/shard_map/ppermute | solution.py:357
  45.3 14.4 %collective-permute-start.4 = (f32[1024,128]{1,0:T(8,128)S(1)}, f32[1024,128]{1,0:T(8,128)}, u32[]{:S(2)}, u32[]{:S(2)}) collective-permute-start(f32[1024,128]{1,0:T(8,128)S(1)} %collective-permute-done.refs_0_), channel_id=1, source_target_pairs={{0,1},{1,0},{2,3},{3,2},{4,5},{5,4},{6,7},{7,6},{8,9},{9,8},{10,11... | collective-permute-start | bytes 1572872 | tf_op jit(solution)/shard_map/ppermute | solution.py:354
  45.3 14.4 %collective-permute-start.5 = (f32[1024,128]{1,0:T(8,128)S(1)}, f32[1024,128]{1,0:T(8,128)}, u32[]{:S(2)}, u32[]{:S(2)}) collective-permute-start(f32[1024,128]{1,0:T(8,128)S(1)} %collective-permute-done.1.refs_1_), channel_id=1, source_target_pairs={{0,1},{1,0},{2,3},{3,2},{4,5},{5,4},{6,7},{7,6},{8,9},{9,8},{10,11... | collective-permute-start | bytes 1572872 | tf_op jit(solution)/shard_map/ppermute | solution.py:354
  47.9 8.4 %collective-permute-start.8 = (f32[512,128]{1,0:T(8,128)}, f32[512,128]{1,0:T(8,128)S(1)}, u32[]{:S(2)}, u32[]{:S(2)}) collective-permute-start(f32[512,128]{1,0:T(8,128)} %get-tuple-element.6), channel_id=1, source_target_pairs={{0,3},{2,1},{4,7},{6,5},{8,11},{10,9},{12,15},{14,13},{16,19},{18,... | collective-permute-start | bytes 786440 | tf_op jit(solution)/shard_map/ppermute | solution.py:357
  51.0 0.8 %copy-start.1 = (f32[1024,128]{1,0:T(8,128)}, f32[1024,128]{1,0:T(8,128)S(1)}, u32[]{:S(2)}) copy-start(f32[1024,128]{1,0:T(8,128)S(1)} %term.2.kept) | copy-start | bytes 1572868
  51.8 7.9 %copy-start.2 = (f32[1024,128]{1,0:T(8,128)S(1)}, f32[1024,128]{1,0:T(8,128)}, u32[]{:S(2)}) copy-start(f32[1024,128]{1,0:T(8,128)} %copy-done.1) | copy-start | bytes 1572868
  51.8 7.9 %collective-permute-start.9 = (f32[512,128]{1,0:T(8,128)}, f32[512,128]{1,0:T(8,128)}, u32[]{:S(2)}, u32[]{:S(2)}) collective-permute-start(f32[512,128]{1,0:T(8,128)} %get-tuple-element.4), channel_id=1, source_target_pairs={{0,3},{2,1},{4,7},{6,5},{8,11},{10,9},{12,15},{14,13},{16,19},{18,... | collective-permute-start | bytes 786440 | tf_op jit(solution)/shard_map/ppermute | solution.py:357
  54.0 14.7 %collective-permute-start.3 = (f32[512,128]{1,0:T(8,128)S(1)}, f32[512,128]{1,0:T(8,128)}, u32[]{:S(2)}, u32[]{:S(2)}) collective-permute-start(f32[512,128]{1,0:T(8,128)S(1)} %blend.2), channel_id=1, source_target_pairs={{0,2},{1,3},{2,0},{3,1},{4,6},{5,7},{6,4},{7,5},{8,10},{9,11},{10,... | collective-permute-start | bytes 786440 | tf_op jit(solution)/shard_map/ppermute | solution.py:354
  61.8 2.8 %collective-permute-start.10 = (f32[8,128]{1,0:T(8,128)S(1)}, f32[8,128]{1,0:T(8,128)S(1)}, u32[]{:S(2)}, u32[]{:S(2)}) collective-permute-start(f32[8,128]{1,0:T(8,128)S(1)} %gram.1), channel_id=1, source_target_pairs={{0,1},{1,0},{2,3},{3,2},{4,5},{5,4},{6,7},{7,6},{8,9},{9,8},{10,11... | collective-permute-start | bytes 12296 | tf_op jit(solution)/shard_map/ppermute | solution.py:354
  64.6 3.6 %collective-permute-start.11 = (f32[8,128]{1,0:T(8,128)S(1)}, f32[8,128]{1,0:T(8,128)S(1)}, u32[]{:S(2)}, u32[]{:S(2)}) collective-permute-start(f32[8,128]{1,0:T(8,128)S(1)} %add.220), channel_id=1, source_target_pairs={{0,2},{1,3},{2,0},{3,1},{4,6},{5,7},{6,4},{7,5},{8,10},{9,11},{10,... | collective-permute-start | bytes 12296 | tf_op jit(solution)/shard_map/ppermute | solution.py:354

commit v3 on v2

v3 whole, which is shorter than its diff:
```python
import functools

import jax
import jax.numpy as jnp
from jax import lax
from jax.experimental import pallas as pl
from jax.experimental.pallas import tpu as pltpu
from jax.sharding import PartitionSpec as P


NG = 64
STEPS = 3
LANES = 128
HALF = LANES // 2
PITCH = NG + 1
MET = (3, 1, 2, 0)
SENT = (3, 1, 2, 1)
SAME, LOW, HIGH, FAR_SENT, NEAR_SENT, FAR_KEPT, NEAR_KEPT, OWN, OTHERS = 0, 1, 2, 3, 4, 5, 6, 7, 9
screen_scale = 0.05


def passed_along(block, axis, distance):
    devices = range(lax.axis_size(axis))
    route = [((i - distance) % len(devices), i) for i in devices]
    return lax.ppermute(block, axis, route)


def cas_table(grid_points):
    grid_index = jnp.arange(grid_points, dtype=jnp.int32)
    product = grid_index[:, None] * grid_index[None, :] % grid_points
    phase_angle = 2.0 * jnp.pi / grid_points * product.astype(jnp.float32)
    return jnp.cos(phase_angle) + jnp.sin(phase_angle)


def screened_kernel(grid_points):
    def squares(index):
        folded = jnp.where(index <= grid_points // 2, index, index - grid_points).astype(jnp.float32)
        return folded * folded

    shape = (grid_points * grid_points // 2, 2 * grid_points)
    row = lax.broadcasted_iota(jnp.int32, shape, 0)
    lane = lax.broadcasted_iota(jnp.int32, shape, 1)
    k_squared = (
        squares(row % grid_points)
        + squares(2 * (row // grid_points) + lane // grid_points)
        + squares(lane % grid_points)
    )
    safe_square = jnp.maximum(k_squared, 1.0)
    screened = (
        4.0
        * jnp.pi
        / (screen_scale * safe_square)
        * (1.0 - jnp.exp(-screen_scale * safe_square / (4.0 * jnp.pi)))
    )
    return jnp.where(k_squared > 0.5, screened, jnp.ones_like(screened))


def high_low(value):
    high = value.astype(jnp.bfloat16)
    return high, (value - high.astype(jnp.float32)).astype(jnp.bfloat16)


def dot(a, b):
    return lax.dot_general(a, b, (((1,), (0,)), ((), ())), preferred_element_type=jnp.float32)


def swapped(first, second, low_half):
    return (
        jnp.where(low_half, first, pltpu.roll(second, HALF, 1)),
        jnp.where(low_half, pltpu.roll(first, HALF, 1), second),
    )


def left_weights(table):
    high, low = high_low(table)
    return jnp.concatenate([high, high, low], axis=1)


def lane_weights(table):
    high, low = high_low(table)
    return jnp.concatenate(
        [jnp.concatenate([high, low], axis=1), jnp.concatenate([high, jnp.zeros_like(low)], axis=1)],
        axis=0,
    )


def from_left(weights, value):
    high, low = high_low(value)
    return dot(weights, jnp.concatenate([high, low, high], axis=0))


def along_lanes(value, weights):
    high, low = high_low(value)
    both = dot(jnp.concatenate([high, low], axis=1), weights)
    return both[:, :LANES] + both[:, LANES:]


def low_mask(rows):
    return lax.broadcasted_iota(jnp.int32, (rows, LANES), 1) < HALF


def kernel_call(body, shape, spaces, flops, cells, **more):
    memory = {"s": pltpu.SMEM, "v": pltpu.VMEM}
    return pl.pallas_call(
        body,
        out_shape=jax.ShapeDtypeStruct(shape, jnp.float32),
        in_specs=[pl.BlockSpec(memory_space=memory[space]) for space in spaces],
        out_specs=pl.BlockSpec(memory_space=pltpu.VMEM),
        compiler_params=pltpu.CompilerParams(vmem_limit_bytes=24 << 20),
        cost_estimate=pl.CostEstimate(flops=flops, bytes_accessed=4 * cells, transcendentals=0),
        **more,
    )


def planes_body(places, factors, own, visiting, forward, paired, out, *, first_row):
    plane = NG // 2
    mask = low_mask(plane)
    w_forward = left_weights(forward[...])
    w_lanes = lane_weights(paired[...])
    alone = places[SAME] == 1

    def planes(step, _):
        at = pl.multiple_of(step * (4 * plane), 4 * plane)
        mine = own[pl.ds(first_row + at, 4 * plane), :]
        density = mine * jnp.where(alone, mine, visiting[pl.ds(at, 4 * plane), :])
        along_z = along_lanes(density, w_lanes)
        blocks = []
        for half in range(2):
            base = half * 2 * plane
            even, odd = swapped(along_z[base : base + plane], along_z[base + plane : base + 2 * plane], mask)
            blocks.append(jnp.concatenate([even, odd], axis=0))
        along_y = from_left(w_forward, jnp.concatenate(blocks, axis=1))
        out[pl.ds(step * (2 * PITCH), NG), :] = along_y[:, :LANES]
        out[pl.ds(step * (2 * PITCH) + PITCH, NG), :] = along_y[:, LANES:]
        return 0

    steps = visiting.shape[0] // (4 * plane)
    lax.fori_loop(0, steps, planes, 0, unroll=steps)


def columns_body(head, kernel, forward, backward, tail, out):
    plane = NG // 2
    pairs = NG // 4
    mask = low_mask(plane)
    w_forward = left_weights(forward[...])
    w_backward = left_weights(backward[...])

    def columns(step, _):
        blocks = []
        for part in range(2):
            row = 4 * step + 2 * part
            first, second = (
                jnp.concatenate([half[pl.ds(row + odd, pairs, stride=PITCH), :] for half in (head, tail)], axis=0)
                for odd in range(2)
            )
            blocks.append(jnp.concatenate(swapped(first, second, mask), axis=0))
        along_x = from_left(w_forward, jnp.concatenate(blocks, axis=1))
        at = pl.multiple_of(step * (2 * NG), 2 * NG)
        weight = jnp.concatenate([kernel[pl.ds(at, NG), :], kernel[pl.ds(at + NG, NG), :]], axis=1)
        returned = from_left(w_backward, along_x * weight)
        for part in range(2):
            block = returned[:, part * LANES : (part + 1) * LANES]
            row = 4 * step + 2 * part
            for odd, value in enumerate(swapped(block[:plane], block[plane:], mask)):
                out[pl.ds(row + odd, plane, stride=PITCH), :] = value
        return 0

    lax.fori_loop(0, NG // 4, columns, 0, unroll=NG // 4)


def last_body(places, factors, head, own, visiting, kernel, forward, backward, paired, out, tail, *, first_row):
    planes_body(places, factors, own, visiting, forward, paired, tail, first_row=first_row)
    columns_body(head, kernel, forward, backward, tail, out)


def first_planes(places, factors, own, visiting, forward, paired):
    rows = visiting.shape[0]
    return kernel_call(
        functools.partial(planes_body, first_row=0),
        (rows // NG * PITCH, LANES),
        "ssvvvv",
        rows * LANES * NG * 4,
        3 * rows * LANES,
    )(places, factors, own, visiting, forward, paired)


def spectrum(places, factors, head, own, visiting, kernel, forward, backward, paired):
    rows = visiting.shape[0]
    return kernel_call(
        functools.partial(last_body, first_row=rows),
        (2 * rows // NG * PITCH, LANES),
        "ssvvvvvvv",
        rows * LANES * NG * 20,
        12 * rows * LANES,
        scratch_shapes=[pltpu.VMEM((rows // NG * PITCH, LANES), jnp.float32)],
    )(places, factors, head, own, visiting, kernel, forward, backward, paired)


def term_body(places, spectral, own, even, odd, backward, paired, out, *, which):
    plane = NG // 2
    mask = low_mask(plane)
    w_backward = left_weights(backward[...])
    w_lanes = lane_weights(paired[...])
    slab_rows = out.shape[0]
    start = places[which] * slab_rows
    half_rows = even.shape[0]
    alone = places[SAME] == 1
    later = start >= half_rows
    inside = start % half_rows

    def planes(step, _):
        at = step * (4 * plane)
        row = (start // NG + 2 * step) * PITCH
        pair = jnp.concatenate([spectral[pl.ds(row, NG), :], spectral[pl.ds(row + PITCH, NG), :]], axis=1)
        along_y = from_left(w_backward, pair)
        blocks = []
        for half in range(2):
            block = along_y[:, half * LANES : (half + 1) * LANES]
            blocks.extend(swapped(block[:plane], block[plane:], mask))
        potential = along_lanes(jnp.concatenate(blocks, axis=0), w_lanes)
        near = pl.multiple_of(inside + at, 4 * plane)
        visiting = jnp.where(later, odd[pl.ds(near, 4 * plane), :], even[pl.ds(near, 4 * plane), :])
        partner = jnp.where(alone, own[pl.ds(pl.multiple_of(start + at, 4 * plane), 4 * plane), :], visiting)
        out[pl.ds(pl.multiple_of(at, 4 * plane), 4 * plane), :] = potential * (partner * (1.0 / NG**3))
        return 0

    steps = slab_rows // (4 * plane)
    lax.fori_loop(0, steps, planes, 0, unroll=steps)


def term(which, slab_rows, places, spectral, own, pieces, backward, paired):
    cells = slab_rows * LANES
    return kernel_call(
        functools.partial(term_body, which=which), (slab_rows, LANES), "svvvvvv", cells * NG * 12, 4 * cells
    )(places, spectral, own, *pieces, backward, paired)


def blend_body(factors, kept, met, *refs):
    *more, out = refs
    value = factors[0] * kept[...] + factors[1] * met[...]
    out[...] = value + more[0][...] if more else value


def blend(factors, kept, met, *more):
    cells = kept.size
    return kernel_call(blend_body, kept.shape, "svv" + "v" * len(more), 4 * cells, 4 * cells)(factors, kept, met, *more)


def pick_body(places, mine, near, out):
    out[...] = jnp.where(places[LOW] == 0, mine[...], near[...])


def blocks_call(body, places, arrays, indices, shape, block, flops, scalars=()):
    def spec(index):
        return pl.BlockSpec(block, lambda i, held: (held[int(index)] if isinstance(index, str) else index, 0))

    return pl.pallas_call(
        body,
        out_shape=jax.ShapeDtypeStruct(shape, jnp.float32),
        grid_spec=pltpu.PrefetchScalarGridSpec(
            num_scalar_prefetch=1,
            grid=(1,),
            in_specs=[pl.BlockSpec(memory_space=pltpu.SMEM) for _ in scalars] + [spec(index) for index in indices],
            out_specs=pl.BlockSpec(shape, lambda i, held: (0, 0)),
        ),
        compiler_params=pltpu.CompilerParams(vmem_limit_bytes=24 << 20),
        cost_estimate=pl.CostEstimate(
            flops=flops, bytes_accessed=4 * block[0] * block[1] * len(arrays), transcendentals=0
        ),
    )(places, *scalars, *arrays)


def pick(places, mine, near):
    rows = mine.shape[0] // 2
    return blocks_call(
        pick_body, places, (mine, near), (str(LOW), str(LOW)), (rows, LANES), (rows, LANES), rows * LANES
    )


def gram_body(places, factors, *refs):
    *stores, out = refs
    far, near, sides = stores[0:2], stores[2:4], (stores[4:8], stores[8:12])
    rows = far[0].shape[0]
    chunk = 64

    def folded_rows(value):
        return jnp.sum(value.reshape(chunk // 8, 8, LANES), axis=0)

    totals = (jnp.zeros((8, LANES), jnp.float32),) * 8
    for side in range(2):
        is_near = places[HIGH] == side

        def step(index, totals, side=side, is_near=is_near):
            at = pl.ds(pl.multiple_of(index * chunk, chunk), chunk)
            terms = [jnp.where(is_near, near[t][at, :], far[t][at, :]) for t in range(2)]
            orbitals = [store[at, :] for store in sides[side]]
            return tuple(
                totals[4 * t + o] + folded_rows(terms[t] * orbitals[o]) for t in range(2) for o in range(4)
            )

        totals = lax.fori_loop(0, rows // chunk, step, totals, unroll=2)
    lane = lax.broadcasted_iota(jnp.int32, (8, LANES), 1)
    result = jnp.zeros((8, LANES), jnp.float32)
    for o in range(4):
        value = jnp.sum(factors[2 + o] * totals[o] + factors[6 + o] * totals[4 + o], axis=(0, 1), keepdims=True)
        result = jnp.where(lane == places[OTHERS + o], value, result)
    out[...] = result


def gram(places, factors, far, near, own, pieces, nears, moved):
    rows = far[0].shape[0]
    arrays = list(far) + list(near)
    indices = [0] * 4
    for side in range(2):
        arrays += [own, pieces[side], nears[side], moved[side]]
        indices += [str(OWN + side), str(LOW), str(LOW), 0]
    return blocks_call(gram_body, places, arrays, indices, (8, LANES), (rows, LANES), 32 * rows * LANES, (factors,))


def position_block(orbital_block, amount):
    bit_count = (lax.axis_size("blk") - 1).bit_length()
    for bit_level in range(bit_count):
        moved_block = passed_along(orbital_block, "blk", 1 << bit_level)
        orbital_block = jnp.where(amount // (1 << bit_level) % 2 == 1, moved_block, orbital_block)
    return orbital_block


def stepped(orbitals, offsets, tables):
    blocks, replicas = lax.axis_size("blk"), lax.axis_size("rep")
    replica = lax.axis_index("rep")
    cells = orbitals.shape[1]
    rows = cells // LANES
    kernel, forward, backward, paired = tables
    first = position_block(orbitals, (offsets[replica] + STEPS // 2) % blocks)
    visits = [first]
    for distance in range(1, STEPS // 2 + 1):
        visits.append(passed_along(first, "blk", -distance))
        visits.append(passed_along(first, "blk", distance))
    own = orbitals.reshape(rows, LANES)
    slab_rows = rows // replicas
    places = jnp.zeros((OTHERS,), jnp.int32)
    factors = jnp.zeros((2,), jnp.float32)
    whole = jnp.zeros((rows, LANES), jnp.float32)
    for visit in visits:
        visit = visit.reshape(rows, LANES)
        pieces = visit[: rows // 2], visit[rows // 2 :]
        head = first_planes(places, factors, own, pieces[0], forward, paired)
        spectral = spectrum(places, factors, head, own, pieces[1], kernel, forward, backward, paired)
        slabs = [
            term(FAR_SENT, slab_rows, places.at[FAR_SENT].set(r), spectral, own, pieces, backward, paired)
            for r in range(replicas)
        ]
        whole = whole + jnp.concatenate(slabs, axis=0)
    exchanged = lax.psum_scatter(whole.reshape(1, cells), "rep", scatter_dimension=1, tiled=True)
    quarter = lax.dynamic_slice_in_dim(orbitals, replica * (cells // replicas), cells // replicas, 1)
    slab_orbitals = lax.all_to_all(quarter, "blk", split_axis=1, concat_axis=0, tiled=True)
    slab_exchanged = lax.all_to_all(exchanged, "blk", split_axis=1, concat_axis=0, tiled=True)
    partial_value = lax.dot_general(
        slab_orbitals, slab_exchanged, (((1,), (1,)), ((), ())), precision=lax.Precision.HIGHEST
    ) / float(NG**3)
    gram_rows = lax.psum_scatter(partial_value, "blk", scatter_dimension=0, tiled=True)
    return exchanged, lax.psum(gram_rows, "rep")


def folded(orbitals, offsets, tables):
    blocks, replicas = lax.axis_size("blk"), lax.axis_size("rep")
    block, replica = lax.axis_index("blk"), lax.axis_index("rep")
    low, high = replica % 2, replica // 2
    cells = orbitals.shape[1]
    rows = cells // LANES
    slab_rows = rows // replicas
    kernel, forward, backward, paired = tables
    own = orbitals.reshape(rows, LANES)
    met_by = jnp.asarray(MET, jnp.int32)
    sent_to = jnp.asarray(SENT, jnp.int32)

    partners = block ^ jnp.stack([met_by[replica], met_by[replica ^ 1]])
    others = block ^ jnp.stack(
        [jnp.zeros_like(block), sent_to[replica], sent_to[replica ^ 1], sent_to[(replica ^ 2) // 2 * 2]]
    )
    far_side, near_side = 2 * (1 - high), 2 * high
    sides = [far_side + 1 - low, near_side + 1 - low, far_side + low, near_side + low, low, 2 + low]
    same = (met_by[replica] == 0).astype(jnp.int32)
    places = jnp.concatenate([jnp.stack([same, low, high] + sides), others]).astype(jnp.int32)
    apart = jnp.concatenate([block - partners, (others[None, :] - partners[:, None]).reshape(-1)])
    occurs = offsets[:, None] + jnp.arange(STEPS, dtype=jnp.int32)[None, :]
    hits = (occurs[None] - apart[:, None, None]) % blocks == 0
    factors = jnp.sum(hits.astype(jnp.float32), axis=(1, 2))
    factors = factors * jnp.where(jnp.arange(apart.shape[0]) < 2, 1.0, 1.0 / NG**3)

    def along_blocks(value):
        route = [((b ^ SENT[r]) * replicas + r, b * replicas + r) for b in range(blocks) for r in range(replicas)]
        return lax.ppermute(value, ("blk", "rep"), route)

    def replica_swap(value, bit):
        return lax.ppermute(value, "rep", [(r, r ^ bit) for r in range(replicas)])

    piece_a = along_blocks(own[: rows // 2])
    piece_b = along_blocks(own[rows // 2 :])
    near_a = replica_swap(piece_a, 1)
    moved_a = replica_swap(pick(places, piece_a, near_a), 2)
    head = first_planes(places, factors, own, piece_a, forward, paired)
    near_b = replica_swap(piece_b, 1)
    spectral = spectrum(places, factors, head, own, piece_b, kernel, forward, backward, paired)
    picked_b = pick(places, piece_b, near_b)
    moved_b = replica_swap(picked_b, 2)

    pieces = piece_a, piece_b
    terms = {}
    for which in (FAR_SENT, FAR_KEPT, NEAR_SENT, NEAR_KEPT):
        terms[which] = term(which, slab_rows, places, spectral, own, pieces, backward, paired)
    met_far = replica_swap(terms[FAR_SENT], 1)
    met_near = replica_swap(terms[NEAR_SENT], 1)
    arrived = replica_swap(blend(factors, terms[FAR_KEPT], met_far), 2)
    near_sum = blend(factors, terms[NEAR_KEPT], met_near, arrived)
    row = gram(
        places,
        factors,
        (terms[FAR_KEPT], met_far),
        (terms[NEAR_KEPT], met_near),
        own,
        pieces,
        (near_a, near_b),
        (moved_a, moved_b),
    )
    row = row + replica_swap(row, 1)
    row = row + replica_swap(row, 2)
    return near_sum.reshape(1, cells // replicas), row[:1, :blocks]


def local(orbitals, offsets):
    blocks, replicas = lax.axis_size("blk"), lax.axis_size("rep")
    table = cas_table(NG)
    forward = table.reshape(NG, NG // 2, 2).transpose(0, 2, 1).reshape(NG, NG)
    paired = jnp.kron(jnp.eye(2, dtype=jnp.float32), table)
    tables = screened_kernel(NG), forward, forward.T, paired
    if is_folded(blocks, replicas):
        return folded(orbitals, offsets, tables)
    return stepped(orbitals, offsets, tables)


def is_folded(blocks, replicas):
    return blocks == replicas == len(MET)


def solution(mesh):
    placed = (P(("groups", "blk"), None), P("groups"))
    step = jax.shard_map(
        local,
        mesh=mesh,
        in_specs=placed,
        out_specs=(P(("groups", "blk"), "rep"), P(("groups", "blk"), None)),
        check_vma=False,
    )
    if not is_folded(mesh.shape["blk"], mesh.shape["rep"]):
        return step
    return step
```

time: 71 us -> 65.6 us (0.924)
  starting transfers between devices: 19.7 us -> 8.9 us
  waiting for transfers between devices: 21.7 us -> 27.7 us
  Pallas kernels: 13.5 us -> 17.4 us
  local copies, waits for them, and re-layouts: 6.52 us -> 3.87 us
  other arithmetic: 7.55 us -> 5.95 us
    ppermute x4 -> x0, starting transfers between devices: 9.96 us -> none  [from_even(): lax.ppermute(value, 'rep', [(r, (r ^ 2) + to_odd) for r in range(0, repli...]
    ppermute x6 -> x9, waiting for transfers between devices: 4.01 us -> 10.6 us  [replica_swap(): return lax.ppermute(value, 'rep', [(r, r ^ bit) for r in range(replicas)])]
    pallas_call x6 -> x11, Pallas kernels: 13.5 us -> 17.4 us  [the longest x3 5.2 us: blocks_call(): pl.pallas_call(body, out_shape=jax.ShapeDtypeStruct(shape, jnp.float32),...]
    ppermute x4 -> x0, waiting for transfers between devices: 3.45 us -> none  [from_even(): lax.ppermute(value, 'rep', [(r, (r ^ 2) + to_odd) for r in range(0, repli...]
    ppermute x2, waiting for transfers between devices: 14.3 us -> 17.1 us  [along_blocks(): return lax.ppermute(value, ('blk', 'rep'), route)]
    select_n x3 -> x0, other arithmetic: 1.54 us -> none  [the longest x1 1.44 us: folded(): weights = counts[(block - partners) % blocks]]
    sub x0 -> x2, other arithmetic: none -> 1.44 us  [the longest x1 1.37 us: folded(): block - partners]
    xor x1 -> x0, other arithmetic: 1.43 us -> none  [folded(): partners = block ^ jnp.stack([met_by[replica], met_by[replica ^ 1]])]
  transfers between devices with their start and end apart: 12 -> 11, of which waited for: 5 -> 7; matrix products, arithmetic and copies ran while one was open for 17% -> 11% of each run, Pallas kernels for 7% -> 27%
where the time goes in v3:
time: 65.6 us; the launch traced here: 65.3 us
  waiting for transfers between devices  27.7 us (42%)
  Pallas kernels  17.4 us (27%)
  starting transfers between devices  8.9 us (14%)
  other arithmetic  5.95 us (9%)
  local copies, waits for them, and re-layouts  3.87 us (6%)
  between operations  1.52 us (2%)
    ppermute x2, waiting for transfers between devices, along_blocks(): return lax.ppermute(value, ('blk', 'rep'), route)  17.1 us
    ppermute x9, waiting for transfers between devices, replica_swap(): return lax.ppermute(value, 'rep', [(r, r ^ bit) for r in range(replicas)])  10.6 us
    pallas_call x3, Pallas kernels, blocks_call(): pl.pallas_call(body, out_shape=jax.ShapeDtypeStruct(shape, jnp.float32),...  5.2 us
    ppermute x2, starting transfers between devices, along_blocks(): return lax.ppermute(value, ('blk', 'rep'), route)  5.1 us
    pallas_call x4, Pallas kernels, term(): kernel_call(functools.partial(term_body, which=which), (slab_rows, LANES)...  5.01 us
    ppermute x9, starting transfers between devices, replica_swap(): return lax.ppermute(value, 'rep', [(r, r ^ bit) for r in range(replicas)])  3.8 us
    pallas_call x1, Pallas kernels, spectrum(): kernel_call(functools.partial(last_body, first_row=rows), (2 * rows // NG...  3.13 us
    slice x1, local copies, waits for them, and re-layouts, folded(): piece_b = along_blocks(own[rows // 2:])  2.28 us
  transfers between devices with their start and end apart: 11, of which 7 were waited for; matrix products, arithmetic and copies ran while one was open for 11% of the time, Pallas kernels for 27%

profile of v3, /device:TPU:0, one launch (start us, length us, event | category | flops | bytes accessed | tf_op | source)
XLA Modules:
  0.0 65.3 jit_solution(6645184263877340676)
XLA Ops:
  0.7 2.3 %fusion.35 = (f32[1,131072]{1,0:T(1,128)}, f32[1,131072]{1,0:T(1,128)}) fusion(f32[1,262144]{1,0:T(1,128)} %param.4), kind=kLoop, calls=%fused_computation.78 | loop fusion | bytes 2097152 | tf_op jit(solution)/shard_map/slice | solution.py:399
  2.9 5.1 %collective-permute-start = (f32[1024,128]{1,0:T(8,128)}, f32[1024,128]{1,0:T(8,128)S(1)}, u32[]{:S(2)}, u32[]{:S(2)}) collective-permute-start(f32[1024,128]{1,0:T(8,128)} %bitcast.8), channel_id=1, source_target_pairs={{12,0},{5,1},{10,2},{7,3},{8,4},{1,5},{14,6},{3,7},{4,8},{13,9},{2... | collective-permute-start | bytes 1572872 | tf_op jit(solution)/shard_map/ppermute | solution.py:393
  8.3 0.7 %fusion.36 = (s32[1]{0:T(128)}, s32[1]{0:T(128)}, s32[1]{0:T(128)}, s32[1]{0:T(128)}, s32[1]{0:T(128)}) fusion(s32[4]{0:T(128)S(1)} %copy-done.2, s32[]{:T(128)S(6)} %select_n.105, s32[]{:T(128)S(6)} %select_n.106, s32[4]{0:T(128)S(1)} %copy-done.1, s32[]{:T(128)S(6)} %select_n.108), kind=kLoop, calls=%fused_computation.79 | loop fusion | bytes 52 | tf_op jit(solution)/shard_map/dynamic_slice | solution.py:377
  9.0 1.4 %broadcast_subtract_fusion.1 = (s32[2]{0:T(128)S(1)}, s32[2]{0:T(128)S(1)}) fusion(s32[]{:T(128)S(6)} %axis_index.23, s32[1]{0:T(128)} %get-tuple-element.9, s32[1]{0:T(128)} %get-tuple-element.8), kind=kLoop, calls=%fused_computation.77 | loop fusion | flops 6 | bytes 28 | tf_op jit(solution)/shard_map/sub | solution.py:385
  10.3 2.0 %add_xor_fusion.1 = s32[4]{0:T(128)S(1)} fusion(s32[1]{0:T(128)} %get-tuple-element.14, s32[1]{0:T(128)} %get-tuple-element.13, s32[1]{0:T(128)} %get-tuple-element.15, s32[1]{0:T(128)} %constant.131.clone.1, s32[]{:T(128)S(6)} %axis_index.23), kind=kLoop, calls=%fused_computation.72 | loop fusion | flops 16 | bytes 36 | tf_op jit(solution)/shard_map/xor | solution.py:378
  12.8 1.7 %multiply_select_fusion.kernel = f32[2048,128]{1,0:T(8,128)S(1)} fusion(s32[128]{0:T(128)S(1)} %get-tuple-element.25, s32[128]{0:T(128)S(1)} %get-tuple-element.26, s32[128]{0:T(128)S(1)} %get-tuple-element.24, s32[128]{0:T(128)S(1)} %get-tuple-element.27, s32[2048]{0:T(1024)S(1)} %get-tuple-element.16, s32[2048]{0:T(1024)S(1)} %get-tuple-element.19, ...), kind=kLoop, calls=%fused_computation.11 | loop fusion | flops 8126464 | bytes 1087744 | tf_op jit(solution)/shard_map/jit(_where)/select_n | solution.py:55
  14.5 6.5 %collective-permute-done.visiting.even.mine.refs_5_ = f32[1024,128]{1,0:T(8,128)S(1)} collective-permute-done((f32[1024,128]{1,0:T(8,128)}, f32[1024,128]{1,0:T(8,128)S(1)}, u32[]{:S(2)}, u32[]{:S(2)}) %collective-permute-start) | collective-permute-done | bytes 524320 | tf_op jit(solution)/shard_map/ppermute | solution.py:393
  21.0 10.6 %collective-permute-done.1.visiting.odd.mine.refs_9_ = f32[1024,128]{1,0:T(8,128)S(1)} collective-permute-done((f32[1024,128]{1,0:T(8,128)}, f32[1024,128]{1,0:T(8,128)S(1)}, u32[]{:S(2)}, u32[]{:S(2)}) %collective-permute-start.1) | collective-permute-done | bytes 524320 | tf_op jit(solution)/shard_map/ppermute | solution.py:393
  32.9 2.2 %shard_map.59.head = f32[1040,128]{1,0:T(8,128)S(1)} custom-call(s32[13]{0:T(128)S(1)} %concatenate.15.places, f32[10]{0:T(128)S(1)} %fusion.34.factors, f32[2048,128]{1,0:T(8,128)S(1)} %bitcast.11, f32[1024,128]{1,0:T(8,128)S(1)} %collective-permute-done.visiting.even.mine.refs_5_, f32[64,64]{1,0:T(8,128)S(1)} %get-tuple-element.7.forward, ...), custom_call_target="tpu_custom_call" | custom-call | flops 33554432 | bytes 1572864 | tf_op jit(solution)/shard_map/pallas_call | solution.py:178
  35.1 3.1 %shard_map.60.spectral = f32[2080,128]{1,0:T(8,128)S(1)} custom-call(s32[13]{0:T(128)S(1)} %concatenate.15.places, f32[10]{0:T(128)S(1)} %fusion.34.factors, f32[1040,128]{1,0:T(8,128)S(1)} %shard_map.59.head, f32[2048,128]{1,0:T(8,128)S(1)} %bitcast.12, f32[1024,128]{1,0:T(8,128)S(1)} %collective-permute-done.1.visiting.odd.mine.refs_9_, ...), custom_call_target="tpu_custom_call" | custom-call | flops 167772160 | bytes 6291456 | tf_op jit(solution)/shard_map/pallas_call | solution.py:189
  38.3 1.3 %shard_map.64 = f32[512,128]{1,0:T(8,128)S(1)} custom-call(s32[13]{0:T(128)S(1)} %concatenate.15.places, f32[2080,128]{1,0:T(8,128)S(1)} %shard_map.60.spectral, f32[2048,128]{1,0:T(8,128)S(1)} %bitcast.13, f32[1024,128]{1,0:T(8,128)S(1)} %collective-permute-done.visiting.even.mine.refs_5_, f32[1024,128]{1,0:T(8,128)S(1)} %collective-permute-done.1.visiting.odd.mine.refs_9_, ...), custom_call_target="tpu_custom_call" | custom-call | flops 50331648 | bytes 1048576 | tf_op jit(solution)/shard_map/pallas_call | solution.py:233
  40.1 1.3 %shard_map.62 = f32[512,128]{1,0:T(8,128)S(1)} custom-call(s32[13]{0:T(128)S(1)} %concatenate.15.places, f32[2080,128]{1,0:T(8,128)S(1)} %shard_map.60.spectral, f32[2048,128]{1,0:T(8,128)S(1)} %bitcast.14, f32[1024,128]{1,0:T(8,128)S(1)} %collective-permute-done.visiting.even.mine.refs_5_, f32[1024,128]{1,0:T(8,128)S(1)} %collective-permute-done.1.visiting.odd.mine.refs_9_, ...), custom_call_target="tpu_custom_call" | custom-call | flops 50331648 | bytes 1048576 | tf_op jit(solution)/shard_map/pallas_call | solution.py:233
  41.4 1.5 %shard_map.67 = f32[512,128]{1,0:T(8,128)S(1)} custom-call(s32[13]{0:T(128)S(1)} %concatenate.15.places, f32[1024,128]{1,0:T(8,128)S(1)} %collective-permute-done.visiting.even.mine.refs_5_, f32[1024,128]{1,0:T(8,128)} %collective-permute-done.5.near.refs_6_), custom_call_target="tpu_custom_call" | custom-call | flops 65536 | bytes 524288 | tf_op jit(solution)/shard_map/pallas_call | solution.py:257
  43.5 1.5 %shard_map.68 = f32[512,128]{1,0:T(8,128)S(1)} custom-call(s32[13]{0:T(128)S(1)} %concatenate.15.places, f32[1024,128]{1,0:T(8,128)S(1)} %collective-permute-done.1.visiting.odd.mine.refs_9_, f32[1024,128]{1,0:T(8,128)} %collective-permute-done.7.near.refs_10_), custom_call_target="tpu_custom_call" | custom-call | flops 65536 | bytes 524288 | tf_op jit(solution)/shard_map/pallas_call | solution.py:257
  45.0 1.7 %collective-permute-start.8 = (f32[512,128]{1,0:T(8,128)S(1)}, f32[512,128]{1,0:T(8,128)S(1)}, u32[]{:S(2)}, u32[]{:S(2)}) collective-permute-start(f32[512,128]{1,0:T(8,128)S(1)} %shard_map.68), channel_id=1, source_target_pairs={{0,2},{1,3},{2,0},{3,1},{4,6},{5,7},{6,4},{7,5},{8,10},{9,11},{10,... | collective-permute-start | bytes 786440 | tf_op jit(solution)/shard_map/ppermute | solution.py:396
  46.6 1.3 %shard_map.63.kept.refs_0_ = f32[512,128]{1,0:T(8,128)S(1)} custom-call(s32[13]{0:T(128)S(1)} %concatenate.15.places, f32[2080,128]{1,0:T(8,128)S(1)} %shard_map.60.spectral, f32[2048,128]{1,0:T(8,128)S(1)} %bitcast.15, f32[1024,128]{1,0:T(8,128)S(1)} %collective-permute-done.visiting.even.mine.refs_5_, ...), custom_call_target="tpu_custom_call" | custom-call | flops 50331648 | bytes 1048576 | tf_op jit(solution)/shard_map/pallas_call | solution.py:233
  47.9 0.6 shard_map.65
  49.0 1.3 %shard_map.61.kept.refs_2_ = f32[512,128]{1,0:T(8,128)S(1)} custom-call(s32[13]{0:T(128)S(1)} %concatenate.15.places, f32[2080,128]{1,0:T(8,128)S(1)} %shard_map.60.spectral, f32[2048,128]{1,0:T(8,128)S(1)} %bitcast.16, f32[1024,128]{1,0:T(8,128)S(1)} %collective-permute-done.visiting.even.mine.refs_5_, ...), custom_call_target="tpu_custom_call" | custom-call | flops 50331648 | bytes 1048576 | tf_op jit(solution)/shard_map/pallas_call | solution.py:233
  50.3 1.9 %collective-permute-done.6.refs_7_ = f32[512,128]{1,0:T(8,128)S(1)} collective-permute-done((f32[512,128]{1,0:T(8,128)S(1)}, f32[512,128]{1,0:T(8,128)S(1)}, u32[]{:S(2)}, u32[]{:S(2)}) %collective-permute-start.6) | collective-permute-done | bytes 262176 | tf_op jit(solution)/shard_map/ppermute | solution.py:396
  52.2 5.6 %collective-permute-done.8.refs_11_ = f32[512,128]{1,0:T(8,128)S(1)} collective-permute-done((f32[512,128]{1,0:T(8,128)S(1)}, f32[512,128]{1,0:T(8,128)S(1)}, u32[]{:S(2)}, u32[]{:S(2)}) %collective-permute-start.8) | collective-permute-done | bytes 262176 | tf_op jit(solution)/shard_map/ppermute | solution.py:396
  57.8 2.1 %shard_map.69 = f32[8,128]{1,0:T(8,128)S(1)} custom-call(s32[13]{0:T(128)S(1)} %concatenate.15.places, f32[10]{0:T(128)S(1)} %fusion.34.factors, f32[512,128]{1,0:T(8,128)S(1)} %shard_map.63.kept.refs_0_, f32[512,128]{1,0:T(8,128)S(1)} %collective-permute-done.3.met.refs_1_, f32[512,128]{1,0:T(8,128)S(1)} %shard_map.61.kept.refs_2_, ...), custom_call_target="tpu_custom_call" | custom-call | flops 2097152 | bytes 3145728 | tf_op jit(solution)/shard_map/pallas_call | solution.py:257
  60.1 1.2 %collective-permute-done.9 = f32[8,128]{1,0:T(8,128)S(1)} collective-permute-done((f32[8,128]{1,0:T(8,128)S(1)}, f32[8,128]{1,0:T(8,128)S(1)}, u32[]{:S(2)}, u32[]{:S(2)}) %collective-permute-start.9) | collective-permute-done | bytes 4128 | tf_op jit(solution)/shard_map/ppermute | solution.py:396
  61.6 1.3 %collective-permute-done.4.refs_0_ = f32[512,128]{1,0:T(8,128)S(1)} collective-permute-done((f32[512,128]{1,0:T(8,128)S(1)}, f32[512,128]{1,0:T(8,128)S(1)}, u32[]{:S(2)}, u32[]{:S(2)}) %collective-permute-start.4) | collective-permute-done | bytes 262176 | tf_op jit(solution)/shard_map/ppermute | solution.py:396
  63.0 1.3 %shard_map.66 = f32[512,128]{1,0:T(8,128)} custom-call(f32[10]{0:T(128)S(1)} %fusion.34.factors, f32[512,128]{1,0:T(8,128)S(1)} %shard_map.61.kept.refs_2_, f32[512,128]{1,0:T(8,128)S(1)} %collective-permute-done.2.met.refs_3_, f32[512,128]{1,0:T(8,128)S(1)} %collective-permute-done.4.refs_0_), custom_call_target="tpu_custom_call" | custom-call | flops 262144 | bytes 1048576 | tf_op jit(solution)/shard_map/pallas_call | solution.py:246
  (45 shorter events, 4.5 us)
Async XLA Ops:
  0.6 7.7 %copy-start.1 = (s32[4]{0:T(128)S(1)}, s32[4]{0:T(128)}, u32[]{:S(2)}) copy-start(s32[4]{0:T(128)} %constant.149.clone) | copy-start | bytes 52
  0.6 7.7 %copy-start.2 = (s32[4]{0:T(128)S(1)}, s32[4]{0:T(128)}, u32[]{:S(2)}) copy-start(s32[4]{0:T(128)} %constant.148.clone) | copy-start | bytes 52
  0.7 11.9 %copy-start.3 = (s32[4]{0:T(128)S(1)}, s32[4]{0:T(128)}, u32[]{:S(2)}) copy-start(s32[4]{0:T(128)} %param.5) | copy-start | bytes 52
  2.9 30.0 %copy-start = (f32[1,262144]{1,0:T(1,128)S(1)}, f32[1,262144]{1,0:T(1,128)}, u32[]{:S(2)}) copy-start(f32[1,262144]{1,0:T(1,128)} %param.4) | copy-start | bytes 3145732
  2.9 18.1 %collective-permute-start = (f32[1024,128]{1,0:T(8,128)}, f32[1024,128]{1,0:T(8,128)S(1)}, u32[]{:S(2)}, u32[]{:S(2)}) collective-permute-start(f32[1024,128]{1,0:T(8,128)} %bitcast.8), channel_id=1, source_target_pairs={{12,0},{5,1},{10,2},{7,3},{8,4},{1,5},{14,6},{3,7},{4,8},{13,9},{2... | collective-permute-start | bytes 1572872 | tf_op jit(solution)/shard_map/ppermute | solution.py:393
  8.0 23.6 %collective-permute-start.1 = (f32[1024,128]{1,0:T(8,128)}, f32[1024,128]{1,0:T(8,128)S(1)}, u32[]{:S(2)}, u32[]{:S(2)}) collective-permute-start(f32[1024,128]{1,0:T(8,128)} %bitcast.9), channel_id=1, source_target_pairs={{12,0},{5,1},{10,2},{7,3},{8,4},{1,5},{14,6},{3,7},{4,8},{13,9},{2... | collective-permute-start | bytes 1572872 | tf_op jit(solution)/shard_map/ppermute | solution.py:393
  21.0 20.4 %collective-permute-start.5 = (f32[1024,128]{1,0:T(8,128)S(1)}, f32[1024,128]{1,0:T(8,128)}, u32[]{:S(2)}, u32[]{:S(2)}) collective-permute-start(f32[1024,128]{1,0:T(8,128)S(1)} %collective-permute-done.visiting.even.mine.refs_5_), channel_id=1, source_target_pairs={{0,1},{1,0},{2,3},{3,2},{4,5},{5,4},{6,7},{7,6},{8,9},{9,8},{10,11... | collective-permute-start | bytes 1572872 | tf_op jit(solution)/shard_map/ppermute | solution.py:396
  31.7 11.8 %collective-permute-start.7 = (f32[1024,128]{1,0:T(8,128)S(1)}, f32[1024,128]{1,0:T(8,128)}, u32[]{:S(2)}, u32[]{:S(2)}) collective-permute-start(f32[1024,128]{1,0:T(8,128)S(1)} %collective-permute-done.1.visiting.odd.mine.refs_9_), channel_id=1, source_target_pairs={{0,1},{1,0},{2,3},{3,2},{4,5},{5,4},{6,7},{7,6},{8,9},{9,8},{10,11... | collective-permute-start | bytes 1572872 | tf_op jit(solution)/shard_map/ppermute | solution.py:396
  39.5 8.4 %collective-permute-start.3 = (f32[512,128]{1,0:T(8,128)S(1)}, f32[512,128]{1,0:T(8,128)S(1)}, u32[]{:S(2)}, u32[]{:S(2)}) collective-permute-start(f32[512,128]{1,0:T(8,128)S(1)} %shard_map.64), channel_id=1, source_target_pairs={{0,1},{1,0},{2,3},{3,2},{4,5},{5,4},{6,7},{7,6},{8,9},{9,8},{10,11... | collective-permute-start | bytes 786440 | tf_op jit(solution)/shard_map/ppermute | solution.py:396
  41.3 8.9 %collective-permute-start.2 = (f32[512,128]{1,0:T(8,128)S(1)}, f32[512,128]{1,0:T(8,128)S(1)}, u32[]{:S(2)}, u32[]{:S(2)}) collective-permute-start(f32[512,128]{1,0:T(8,128)S(1)} %shard_map.62), channel_id=1, source_target_pairs={{0,1},{1,0},{2,3},{3,2},{4,5},{5,4},{6,7},{7,6},{8,9},{9,8},{10,11... | collective-permute-start | bytes 786440 | tf_op jit(solution)/shard_map/ppermute | solution.py:396
  43.0 9.2 %collective-permute-start.6 = (f32[512,128]{1,0:T(8,128)S(1)}, f32[512,128]{1,0:T(8,128)S(1)}, u32[]{:S(2)}, u32[]{:S(2)}) collective-permute-start(f32[512,128]{1,0:T(8,128)S(1)} %shard_map.67), channel_id=1, source_target_pairs={{0,2},{1,3},{2,0},{3,1},{4,6},{5,7},{6,4},{7,5},{8,10},{9,11},{10,... | collective-permute-start | bytes 786440 | tf_op jit(solution)/shard_map/ppermute | solution.py:396
  45.0 12.8 %collective-permute-start.8 = (f32[512,128]{1,0:T(8,128)S(1)}, f32[512,128]{1,0:T(8,128)S(1)}, u32[]{:S(2)}, u32[]{:S(2)}) collective-permute-start(f32[512,128]{1,0:T(8,128)S(1)} %shard_map.68), channel_id=1, source_target_pairs={{0,2},{1,3},{2,0},{3,1},{4,6},{5,7},{6,4},{7,5},{8,10},{9,11},{10,... | collective-permute-start | bytes 786440 | tf_op jit(solution)/shard_map/ppermute | solution.py:396
  48.5 14.5 %collective-permute-start.4 = (f32[512,128]{1,0:T(8,128)S(1)}, f32[512,128]{1,0:T(8,128)S(1)}, u32[]{:S(2)}, u32[]{:S(2)}) collective-permute-start(f32[512,128]{1,0:T(8,128)S(1)} %shard_map.65), channel_id=1, source_target_pairs={{0,2},{1,3},{2,0},{3,1},{4,6},{5,7},{6,4},{7,5},{8,10},{9,11},{10,... | collective-permute-start | bytes 786440 | tf_op jit(solution)/shard_map/ppermute | solution.py:396
  60.0 1.2 %collective-permute-start.9 = (f32[8,128]{1,0:T(8,128)S(1)}, f32[8,128]{1,0:T(8,128)S(1)}, u32[]{:S(2)}, u32[]{:S(2)}) collective-permute-start(f32[8,128]{1,0:T(8,128)S(1)} %shard_map.69), channel_id=1, source_target_pairs={{0,1},{1,0},{2,3},{3,2},{4,5},{5,4},{6,7},{7,6},{8,9},{9,8},{10,11... | collective-permute-start | bytes 12296 | tf_op jit(solution)/shard_map/ppermute | solution.py:396
  61.2 3.6 %collective-permute-start.10 = (f32[8,128]{1,0:T(8,128)S(1)}, f32[8,128]{1,0:T(8,128)S(1)}, u32[]{:S(2)}, u32[]{:S(2)}) collective-permute-start(f32[8,128]{1,0:T(8,128)S(1)} %add.194), channel_id=1, source_target_pairs={{0,2},{1,3},{2,0},{3,1},{4,6},{5,7},{6,4},{7,5},{8,10},{9,11},{10,... | collective-permute-start | bytes 12296 | tf_op jit(solution)/shard_map/ppermute | solution.py:396

commit v4 on v3

v4 whole, which is shorter than its diff:
```python
import functools

import jax
import jax.numpy as jnp
from jax import lax
from jax.experimental import pallas as pl
from jax.experimental.pallas import tpu as pltpu
from jax.sharding import PartitionSpec as P


NG = 64
STEPS = 3
LANES = 128
HALF = LANES // 2
PITCH = NG + 1
GROUP = 256
MET = (3, 1, 2, 0)
SENT = (3, 1, 2, 1)
SENT_A = (3, 3, 2, 2)
SENT_B = (1, 1, 1, 1)
SLABS = len(MET)
SAME, LOW, HIGH, FAR_SENT, NEAR_SENT, FAR_KEPT, NEAR_KEPT, OWN, OTHERS = 0, 1, 2, 3, 4, 5, 6, 7, 9
screen_scale = 0.05


def passed_along(block, axis, distance):
    devices = range(lax.axis_size(axis))
    route = [((i - distance) % len(devices), i) for i in devices]
    return lax.ppermute(block, axis, route)


def cas_table(grid_points):
    grid_index = jnp.arange(grid_points, dtype=jnp.int32)
    product = grid_index[:, None] * grid_index[None, :] % grid_points
    phase_angle = 2.0 * jnp.pi / grid_points * product.astype(jnp.float32)
    return jnp.cos(phase_angle) + jnp.sin(phase_angle)


def screened_kernel(grid_points):
    def squares(index):
        folded = jnp.where(index <= grid_points // 2, index, index - grid_points).astype(jnp.float32)
        return folded * folded

    shape = (grid_points * grid_points // 2, 2 * grid_points)
    row = lax.broadcasted_iota(jnp.int32, shape, 0)
    lane = lax.broadcasted_iota(jnp.int32, shape, 1)
    k_squared = (
        squares(row % grid_points)
        + squares(2 * (row // grid_points) + lane // grid_points)
        + squares(lane % grid_points)
    )
    safe_square = jnp.maximum(k_squared, 1.0)
    screened = (
        4.0
        * jnp.pi
        / (screen_scale * safe_square)
        * (1.0 - jnp.exp(-screen_scale * safe_square / (4.0 * jnp.pi)))
    )
    return jnp.where(k_squared > 0.5, screened, jnp.ones_like(screened))


def high_low(value):
    high = value.astype(jnp.bfloat16)
    return high, (value - high.astype(jnp.float32)).astype(jnp.bfloat16)


def dot(a, b):
    return lax.dot_general(a, b, (((1,), (0,)), ((), ())), preferred_element_type=jnp.float32)


def swapped(first, second, low_half):
    return (
        jnp.where(low_half, first, pltpu.roll(second, HALF, 1)),
        jnp.where(low_half, pltpu.roll(first, HALF, 1), second),
    )


def left_weights(table):
    high, low = high_low(table)
    return jnp.concatenate([high, high, low], axis=1)


def lane_weights(table):
    high, low = high_low(table)
    return jnp.concatenate(
        [jnp.concatenate([high, low], axis=1), jnp.concatenate([high, jnp.zeros_like(low)], axis=1)],
        axis=0,
    )


def from_left(weights, value):
    high, low = high_low(value)
    return dot(weights, jnp.concatenate([high, low, high], axis=0))


def along_lanes(value, weights):
    high, low = high_low(value)
    both = dot(jnp.concatenate([high, low], axis=1), weights)
    return both[:, :LANES] + both[:, LANES:]


def low_mask(rows):
    return lax.broadcasted_iota(jnp.int32, (rows, LANES), 1) < HALF


def kernel_call(body, shape, spaces, flops, cells, **more):
    memory = {"s": pltpu.SMEM, "v": pltpu.VMEM}
    return pl.pallas_call(
        body,
        out_shape=jax.ShapeDtypeStruct(shape, jnp.float32),
        in_specs=[pl.BlockSpec(memory_space=memory[space]) for space in spaces],
        out_specs=pl.BlockSpec(memory_space=pltpu.VMEM),
        compiler_params=pltpu.CompilerParams(vmem_limit_bytes=24 << 20),
        cost_estimate=pl.CostEstimate(flops=flops, bytes_accessed=4 * cells, transcendentals=0),
        **more,
    )


def weights_body(forward, backward, paired, left_y, left_back, lanes):
    left_y[...] = left_weights(forward[...])
    left_back[...] = left_weights(backward[...])
    lanes[...] = lane_weights(paired[...])


def prepared_weights(forward, backward, paired):
    vmem = pl.BlockSpec(memory_space=pltpu.VMEM)
    shapes = (NG, 3 * NG), (NG, 3 * NG), (2 * LANES, 2 * LANES)
    return pl.pallas_call(
        weights_body,
        out_shape=[jax.ShapeDtypeStruct(shape, jnp.bfloat16) for shape in shapes],
        in_specs=[vmem] * 3,
        out_specs=[vmem] * 3,
        name="weights",
    )(forward, backward, paired)


def planes_body(own, visit_at, alone, left_y, lanes, along_z, out, *, first_row):
    plane = NG // 2
    mask = low_mask(plane)
    w_forward = left_y[...]
    w_lanes = lanes[...]
    rows = along_z.shape[0]
    for at in range(0, rows, GROUP):
        mine = own[first_row + at : first_row + at + GROUP, :]
        density = mine * jnp.where(alone, mine, visit_at(at))
        along_z[at : at + GROUP, :] = along_lanes(density, w_lanes)

    def step_planes(step, _):
        at = step * (4 * plane)
        blocks = []
        for half in range(2):
            base = at + half * 2 * plane
            lines = [along_z[pl.ds(pl.multiple_of(base + odd * plane, plane), plane), :] for odd in range(2)]
            blocks.append(jnp.concatenate(swapped(*lines, mask), axis=0))
        along_y = from_left(w_forward, jnp.concatenate(blocks, axis=1))
        out[pl.ds(step * (2 * PITCH), NG), :] = along_y[:, :LANES]
        out[pl.ds(step * (2 * PITCH) + PITCH, NG), :] = along_y[:, LANES:]
        return 0

    steps = rows // (4 * plane)
    lax.fori_loop(0, steps, step_planes, 0, unroll=steps)


def first_body(places, factors, own, visiting, left_y, lanes, out, along_z):
    def visit_at(at):
        return visiting[at : at + GROUP, :]

    planes_body(own, visit_at, places[SAME] == 1, left_y, lanes, along_z, out, first_row=0)


def spectrum_body(
    places, factors, own, head, low_even, low_odd, high_even, high_odd, kernel, left_y, left_back, lanes, out, late,
    tail, along_z,
):
    plane = NG // 2
    pairs = NG // 4
    mask = low_mask(plane)
    slab_rows = low_even.shape[0]
    even = places[LOW] == 0

    def visit_at(at):
        inside = slice(at % slab_rows, at % slab_rows + GROUP)
        by_parity = (low_even, low_odd) if at < slab_rows else (high_even, high_odd)
        value = jnp.where(even, by_parity[0][inside, :], by_parity[1][inside, :])
        late[at : at + GROUP, :] = value
        return value

    planes_body(own, visit_at, places[SAME] == 1, left_y, lanes, along_z, tail, first_row=2 * slab_rows)
    w_forward = left_y[...]
    w_backward = left_back[...]

    def columns(step, _):
        blocks = []
        for part in range(2):
            row = 4 * step + 2 * part
            first, second = (
                jnp.concatenate([half[pl.ds(row + odd, pairs, stride=PITCH), :] for half in (head, tail)], axis=0)
                for odd in range(2)
            )
            blocks.append(jnp.concatenate(swapped(first, second, mask), axis=0))
        along_x = from_left(w_forward, jnp.concatenate(blocks, axis=1))
        at = pl.multiple_of(step * (2 * NG), 2 * NG)
        weight = jnp.concatenate([kernel[pl.ds(at, NG), :], kernel[pl.ds(at + NG, NG), :]], axis=1)
        returned = from_left(w_backward, along_x * weight)
        for part in range(2):
            block = returned[:, part * LANES : (part + 1) * LANES]
            row = 4 * step + 2 * part
            for odd, value in enumerate(swapped(block[:plane], block[plane:], mask)):
                out[pl.ds(row + odd, plane, stride=PITCH), :] = value
        return 0

    lax.fori_loop(0, NG // 4, columns, 0, unroll=NG // 4)


def first_planes(places, factors, own, visiting, weights):
    left_y, _, lanes = weights
    rows = visiting.shape[0]
    return kernel_call(
        first_body,
        (rows // NG * PITCH, LANES),
        "ssvvvv",
        rows * LANES * NG * 4,
        4 * rows * LANES,
        scratch_shapes=[pltpu.VMEM((rows, LANES), jnp.float32)],
    )(places, factors, own, visiting, left_y, lanes)


def spectrum(places, factors, own, head, quarters, kernel, weights):
    rows = own.shape[0]
    smem = pl.BlockSpec(memory_space=pltpu.SMEM)
    vmem = pl.BlockSpec(memory_space=pltpu.VMEM)
    half = rows // 2
    return pl.pallas_call(
        spectrum_body,
        out_shape=[
            jax.ShapeDtypeStruct((rows // NG * PITCH, LANES), jnp.float32),
            jax.ShapeDtypeStruct((half, LANES), jnp.float32),
        ],
        in_specs=[smem] * 2 + [vmem] * 10,
        out_specs=[vmem] * 2,
        scratch_shapes=[
            pltpu.VMEM((half // NG * PITCH, LANES), jnp.float32),
            pltpu.VMEM((half, LANES), jnp.float32),
        ],
        compiler_params=pltpu.CompilerParams(vmem_limit_bytes=24 << 20),
        cost_estimate=pl.CostEstimate(
            flops=rows * LANES * NG * 10, bytes_accessed=24 * rows * LANES, transcendentals=0
        ),
        name="spectrum",
    )(places, factors, own, head, *quarters, kernel, *weights)


def term_body(places, spectral, own, even, odd, left_back, lanes, out, back_y, *, which):
    plane = NG // 2
    mask = low_mask(plane)
    w_backward = left_back[...]
    w_lanes = lanes[...]
    slab_rows = out.shape[0]
    start = places[which] * slab_rows
    half_rows = even.shape[0]
    alone = places[SAME] == 1
    later = start >= half_rows
    inside = start % half_rows

    def step_planes(step, _):
        at = step * (4 * plane)
        row = (start // NG + 2 * step) * PITCH
        pair = jnp.concatenate([spectral[pl.ds(row, NG), :], spectral[pl.ds(row + PITCH, NG), :]], axis=1)
        along_y = from_left(w_backward, pair)
        for half in range(2):
            block = along_y[:, half * LANES : (half + 1) * LANES]
            for second, value in enumerate(swapped(block[:plane], block[plane:], mask)):
                line = pl.multiple_of(at + (2 * half + second) * plane, plane)
                back_y[pl.ds(line, plane), :] = value
        return 0

    steps = slab_rows // (4 * plane)
    lax.fori_loop(0, steps, step_planes, 0, unroll=steps)
    for at in range(0, slab_rows, GROUP):
        potential = along_lanes(back_y[at : at + GROUP, :], w_lanes)
        near = pl.ds(pl.multiple_of(inside + at, 8), GROUP)
        visiting = jnp.where(later, odd[near, :], even[near, :])
        partner = jnp.where(alone, own[pl.ds(pl.multiple_of(start + at, 8), GROUP), :], visiting)
        out[at : at + GROUP, :] = potential * (partner * (1.0 / NG**3))


def term(which, slab_rows, places, spectral, own, pieces, weights):
    cells = slab_rows * LANES
    return kernel_call(
        functools.partial(term_body, which=which),
        (slab_rows, LANES),
        "svvvvvv",
        cells * NG * 12,
        4 * cells,
        scratch_shapes=[pltpu.VMEM((slab_rows, LANES), jnp.float32)],
    )(places, spectral, own, *pieces, weights[1], weights[2])


def blend_body(factors, kept, met, out):
    out[...] = factors[0] * kept[...] + factors[1] * met[...]


def blend(factors, kept, met):
    return kernel_call(blend_body, kept.shape, "svv", 3 * kept.size, 3 * kept.size)(factors, kept, met)


def join_body(first, second, out):
    out[...] = first[...] + second[...]


def join(first, second):
    return kernel_call(join_body, first.shape, "vv", first.size, 3 * first.size)(first, second)


def pick_body(places, mine, near, out):
    rows = out.shape[0]
    out[...] = jnp.where(places[LOW] == 0, mine[:rows, :], near[rows:, :])


def pick(places, mine, near):
    rows = mine.shape[0] // 2
    return kernel_call(pick_body, (rows, LANES), "svv", rows * LANES, 3 * rows * LANES)(places, mine, near)


def seat_body(offsets, places, factors, *, blocks, replicas):
    block, replica = lax.axis_index("blk"), lax.axis_index("rep")
    low, high = replica % 2, replica // 2

    def listed(numbers, index):
        value = jnp.int32(numbers[0])
        for other in range(1, len(numbers)):
            value = jnp.where(index == other, jnp.int32(numbers[other]), value)
        return value

    partners = [block ^ listed(MET, replica), block ^ listed(MET, replica ^ 1)]
    others = [
        block,
        block ^ listed(SENT, replica),
        block ^ listed(SENT, replica ^ 1),
        block ^ listed(SENT, (replica ^ 2) // 2 * 2),
    ]
    far, near = 2 * (1 - high), 2 * high
    same = (listed(MET, replica) == 0).astype(jnp.int32)
    slabs = [far + 1 - low, near + 1 - low, far + low, near + low, low, 2 + low]
    for index, value in enumerate([same, low, high] + slabs + others):
        places[index] = value.astype(jnp.int32)
    shifts = [(offsets[r] + step) % blocks for r in range(replicas) for step in range(STEPS)]
    apart = [(block - partner, 1.0) for partner in partners]
    apart += [(other - partner, 1.0 / NG**3) for partner in partners for other in others]
    for index, (distance, scale) in enumerate(apart):
        wanted = (distance + blocks) % blocks
        hits = jnp.int32(0)
        for shift in shifts:
            hits += (shift == wanted).astype(jnp.int32)
        factors[index] = hits.astype(jnp.float32) * scale


def seat(offsets, blocks, replicas):
    smem = pl.BlockSpec(memory_space=pltpu.SMEM)
    return pl.pallas_call(
        functools.partial(seat_body, blocks=blocks, replicas=replicas),
        out_shape=[
            jax.ShapeDtypeStruct((OTHERS + 4,), jnp.int32),
            jax.ShapeDtypeStruct((10,), jnp.float32),
        ],
        in_specs=[smem],
        out_specs=[smem] * 2,
        name="seat",
    )(offsets)


def gram_body(places, factors, far, met_far, near, met_near, own, *refs):
    piece_a, near_a, moved_a, late_a, late_b, moved_b, out = refs
    even = places[LOW] == 0
    rows = far.shape[0]
    chunk = 64

    def folded_rows(value):
        return jnp.sum(value.reshape(chunk // 8, 8, LANES), axis=0)

    totals = (jnp.zeros((8, LANES), jnp.float32),) * 8
    for side in range(2):
        is_near = places[HIGH] == side
        parity_row = places[LOW] * rows
        own_row = places[OWN + side] * rows

        def step(index, totals, side=side, is_near=is_near, parity_row=parity_row, own_row=own_row):
            inside = index * chunk
            at = pl.ds(pl.multiple_of(inside, chunk), chunk)
            half = pl.ds(pl.multiple_of(parity_row + inside, chunk), chunk)
            mine = pl.ds(pl.multiple_of(own_row + inside, chunk), chunk)
            terms = (
                jnp.where(is_near, near[at, :], far[at, :]),
                jnp.where(is_near, met_near[at, :], met_far[at, :]),
            )
            if side == 0:
                orbitals = (own[mine, :], piece_a[half, :], near_a[half, :], moved_a[at, :])
            else:
                of_a, of_b = late_a[at, :], late_b[at, :]
                orbitals = (own[mine, :], jnp.where(even, of_a, of_b), jnp.where(even, of_b, of_a), moved_b[at, :])
            return tuple(
                totals[4 * t + o] + folded_rows(terms[t] * orbitals[o]) for t in range(2) for o in range(4)
            )

        totals = lax.fori_loop(0, rows // chunk, step, totals, unroll=4)
    lane = lax.broadcasted_iota(jnp.int32, (8, LANES), 1)
    result = jnp.zeros((8, LANES), jnp.float32)
    for o in range(4):
        value = jnp.sum(factors[2 + o] * totals[o] + factors[6 + o] * totals[4 + o], axis=(0, 1), keepdims=True)
        result = jnp.where(lane == places[OTHERS + o], value, result)
    out[...] = result


def gram(places, factors, far, near, own, *stores):
    cells = far[0].size
    return kernel_call(
        gram_body, (8, LANES), "ssvvvvv" + "v" * len(stores), 32 * cells, 12 * cells
    )(places, factors, *far, *near, own, *stores)


def position_block(orbital_block, amount):
    bit_count = (lax.axis_size("blk") - 1).bit_length()
    for bit_level in range(bit_count):
        moved_block = passed_along(orbital_block, "blk", 1 << bit_level)
        orbital_block = jnp.where(amount // (1 << bit_level) % 2 == 1, moved_block, orbital_block)
    return orbital_block


def stepped(orbitals, offsets, tables):
    blocks, replicas = lax.axis_size("blk"), lax.axis_size("rep")
    replica = lax.axis_index("rep")
    cells = orbitals.shape[1]
    rows = cells // LANES
    weights = prepared_weights(*tables)
    kernel = screened_kernel(NG)
    first = position_block(orbitals, (offsets[replica] + STEPS // 2) % blocks)
    visits = [first]
    for distance in range(1, STEPS // 2 + 1):
        visits.append(passed_along(first, "blk", -distance))
        visits.append(passed_along(first, "blk", distance))
    own = orbitals.reshape(rows, LANES)
    places = jnp.zeros((OTHERS,), jnp.int32)
    factors = jnp.zeros((2,), jnp.float32)
    whole = jnp.zeros((rows, LANES), jnp.float32)
    for visit in visits:
        visit = visit.reshape(rows, LANES)
        pieces = visit[: rows // 2], visit[rows // 2 :]
        head = first_planes(places, factors, own, pieces[0], weights)
        quarters = [pieces[1][at : at + rows // SLABS] for at in (0, 0, rows // SLABS, rows // SLABS)]
        spectral, _ = spectrum(places, factors, own, head, quarters, kernel, weights)
        slabs = [
            term(FAR_SENT, rows // SLABS, places.at[FAR_SENT].set(slab), spectral, own, pieces, weights)
            for slab in range(SLABS)
        ]
        whole = whole + jnp.concatenate(slabs, axis=0)
    exchanged = lax.psum_scatter(whole.reshape(1, cells), "rep", scatter_dimension=1, tiled=True)
    quarter = lax.dynamic_slice_in_dim(orbitals, replica * (cells // replicas), cells // replicas, 1)
    slab_orbitals = lax.all_to_all(quarter, "blk", split_axis=1, concat_axis=0, tiled=True)
    slab_exchanged = lax.all_to_all(exchanged, "blk", split_axis=1, concat_axis=0, tiled=True)
    partial_value = lax.dot_general(
        slab_orbitals, slab_exchanged, (((1,), (1,)), ((), ())), precision=lax.Precision.HIGHEST
    ) / float(NG**3)
    gram_rows = lax.psum_scatter(partial_value, "blk", scatter_dimension=0, tiled=True)
    return exchanged, lax.psum(gram_rows, "rep")


def folded(orbitals, offsets, tables):
    blocks, replicas = lax.axis_size("blk"), lax.axis_size("rep")
    replica = lax.axis_index("rep")
    cells = orbitals.shape[1]
    rows = cells // LANES
    slab_rows = rows // replicas
    weights = prepared_weights(*tables)
    own = orbitals.reshape(rows, LANES)
    low = replica % 2
    places, factors = seat(offsets, blocks, replicas)

    def along_blocks(value, sent):
        route = [((b ^ sent[r]) * replicas + r, b * replicas + r) for b in range(blocks) for r in range(replicas)]
        return lax.ppermute(value, ("blk", "rep"), route)

    def replica_swap(value, bit):
        return lax.ppermute(value, "rep", [(r, r ^ bit) for r in range(replicas)])

    def slab_of(index):
        return lax.dynamic_slice_in_dim(own, index * slab_rows, slab_rows, 0)

    piece_a = along_blocks(own[: 2 * slab_rows], SENT)
    late_b = along_blocks(slab_of(3 - low), SENT_B)
    late_a = along_blocks(slab_of(2 + low), SENT_A)

    near_a = replica_swap(piece_a, 1)

    moved_a = replica_swap(pick(places, piece_a, near_a), 2)
    kernel = screened_kernel(NG)
    head = first_planes(places, factors, own, piece_a, weights)
    near_late_b = replica_swap(late_b, 1)
    near_late_a = replica_swap(late_a, 1)
    moved_b = replica_swap(late_a, 2)
    quarters = late_a, late_b, near_late_a, near_late_b
    spectral, piece_b = spectrum(places, factors, own, head, quarters, kernel, weights)
    pieces = piece_a, piece_b
    terms = {}
    for which in (FAR_SENT, FAR_KEPT, NEAR_SENT, NEAR_KEPT):
        terms[which] = term(which, slab_rows, places, spectral, own, pieces, weights)
    met_far = replica_swap(terms[FAR_SENT], 1)
    met_near = replica_swap(terms[NEAR_SENT], 1)

    arrived = replica_swap(blend(factors, terms[FAR_KEPT], met_far), 2)
    row = gram(
        places,
        factors,
        (terms[FAR_KEPT], met_far),
        (terms[NEAR_KEPT], met_near),
        own,
        piece_a,
        near_a,
        moved_a,
        late_a,
        near_late_b,
        moved_b,
    )
    near_sum = blend(factors, terms[NEAR_KEPT], met_near)
    row = row + replica_swap(row, 1)
    other = replica_swap(row, 2)
    margin = row[:1, :blocks] + other[:1, :blocks]
    exchanged = join(near_sum, arrived)
    return exchanged.reshape(1, cells // replicas), margin


def local(orbitals, offsets):
    blocks, replicas = lax.axis_size("blk"), lax.axis_size("rep")
    table = cas_table(NG)
    forward = table.reshape(NG, NG // 2, 2).transpose(0, 2, 1).reshape(NG, NG)
    paired = jnp.kron(jnp.eye(2, dtype=jnp.float32), table)
    tables = forward, forward.T, paired
    if is_folded(blocks, replicas):
        return folded(orbitals, offsets, tables)
    return stepped(orbitals, offsets, tables)


def is_folded(blocks, replicas):
    return blocks == replicas == len(MET)


def solution(mesh):
    placed = (P(("groups", "blk"), None), P("groups"))
    step = jax.shard_map(
        local,
        mesh=mesh,
        in_specs=placed,
        out_specs=(P(("groups", "blk"), "rep"), P(("groups", "blk"), None)),
        check_vma=False,
    )
    if not is_folded(mesh.shape["blk"], mesh.shape["rep"]):
        return step
    return step
```

time: 65.6 us -> 65.4 us (level)
  waiting for transfers between devices: 27.7 us -> 31.6 us
  other arithmetic: 5.95 us -> 3.43 us
  Pallas kernels: 17.4 us -> 14.9 us
  local copies, waits for them, and re-layouts: 3.87 us -> 5.01 us
  between operations: 1.52 us -> 0.83 us
    ppermute x2 -> x3, waiting for transfers between devices: 17.1 us -> 20.2 us  [along_blocks(): return lax.ppermute(value, ('blk', 'rep'), route)]
    unnamed x8 -> x16, local copies, waits for them, and re-layouts: 0.02 us -> 3 us
    slice x2 -> x1, local copies, waits for them, and re-layouts: 2.79 us -> 0.03 us  [folded(): piece_a = along_blocks(own[:2 * slab_rows], SENT)]
    xor x1 -> x0, other arithmetic: 2.01 us -> none  [folded(): block ^ jnp.stack([jnp.zeros_like(block), sent_to[replica], sent_to[repli...]
    pallas_call x7 -> x9, Pallas kernels: 12.4 us -> 10.7 us  [the longest x1 2.62 us: spectrum(): pl.pallas_call(spectrum_body, out_shape=[jax.ShapeDtypeStruct((rows // NG...]
    sub x2 -> x0, other arithmetic: 1.44 us -> none  [the longest x1 1.37 us: folded(): block - partners]
    ppermute x2 -> x3, starting transfers between devices: 5.1 us -> 6.11 us  [along_blocks(): return lax.ppermute(value, ('blk', 'rep'), route)]
    pallas_call x4, Pallas kernels: 5.01 us -> 4.12 us  [term(): kernel_call(functools.partial(term_body, which=which), (slab_rows, LANES)...]
  transfers between devices with their start and end apart: 11 -> 13, of which waited for: 7 -> 8; matrix products, arithmetic and copies ran while one was open for 11% -> 6% of each run, Pallas kernels for 27% -> 23%
where the time goes in v4:
time: 65.4 us; the launch traced here: 65.1 us
  waiting for transfers between devices  31.6 us (48%)
  Pallas kernels  14.9 us (23%)
  starting transfers between devices  9.35 us (14%)
  local copies, waits for them, and re-layouts  5.01 us (8%)
  other arithmetic  3.43 us (5%)
  between operations  0.83 us (1%)
    ppermute x3, waiting for transfers between devices, along_blocks(): return lax.ppermute(value, ('blk', 'rep'), route)  20.2 us
    ppermute x10, waiting for transfers between devices, replica_swap(): return lax.ppermute(value, 'rep', [(r, r ^ bit) for r in range(replicas)])  11.4 us
    ppermute x3, starting transfers between devices, along_blocks(): return lax.ppermute(value, ('blk', 'rep'), route)  6.11 us
    pallas_call x4, Pallas kernels, term(): kernel_call(functools.partial(term_body, which=which), (slab_rows, LANES)...  4.12 us
    ppermute x10, starting transfers between devices, replica_swap(): return lax.ppermute(value, 'rep', [(r, r ^ bit) for r in range(replicas)])  3.25 us
    unnamed x16, local copies, waits for them, and re-layouts  3 us
    pallas_call x1, Pallas kernels, spectrum(): pl.pallas_call(spectrum_body, out_shape=[jax.ShapeDtypeStruct((rows // NG...  2.62 us
    select_n x1, other arithmetic, screened_kernel(): return jnp.where(k_squared > 0.5, screened, jnp.ones_like(screened))  1.7 us
  transfers between devices with their start and end apart: 13, of which 8 were waited for; matrix products, arithmetic and copies ran while one was open for 6% of the time, Pallas kernels for 23%

profile of v4, /device:TPU:0, one launch (start us, length us, event | category | flops | bytes accessed | tf_op | source)
XLA Modules:
  0.0 65.1 jit_solution(10759437015067494141)
XLA Ops:
  0.7 1.2 %constant_dynamic-slice_fusion = (f32[512,128]{1,0:T(8,128)S(1)}, f32[512,128]{1,0:T(8,128)S(1)}) fusion(f32[2048,128]{1,0:T(8,128)} %bitcast.3, s32[]{:T(128)S(6)} %select_n.67, s32[]{:T(128)S(6)} %select_n.66), kind=kLoop, calls=%fused_computation.61 | loop fusion | bytes 1048584 | tf_op jit(solution)/shard_map/dynamic_slice | solution.py:486
  1.8 5.1 %collective-permute-start.1 = (f32[512,128]{1,0:T(8,128)S(1)}, f32[512,128]{1,0:T(8,128)S(1)}, u32[]{:S(2)}, u32[]{:S(2)}) collective-permute-start(f32[512,128]{1,0:T(8,128)S(1)} %get-tuple-element.17), channel_id=1, source_target_pairs={{12,0},{13,1},{10,2},{11,3},{8,4},{9,5},{14,6},{15,7},{4,8},{5,9},... | collective-permute-start | bytes 786440 | tf_op jit(solution)/shard_map/ppermute | solution.py:480
  7.0 1.0 %collective-permute-start = (f32[1024,128]{1,0:T(8,128)S(1)}, f32[1024,128]{1,0:T(8,128)S(1)}, u32[]{:S(2)}, u32[]{:S(2)}) collective-permute-start(f32[1024,128]{1,0:T(8,128)S(1)} %bitcast.11), channel_id=1, source_target_pairs={{12,0},{5,1},{10,2},{7,3},{8,4},{1,5},{14,6},{3,7},{4,8},{13,9},{2... | collective-permute-start | bytes 1572872 | tf_op jit(solution)/shard_map/ppermute | solution.py:480
  8.0 1.7 %multiply_select_fusion.kernel = f32[2048,128]{1,0:T(8,128)S(1)} fusion(s32[128]{0:T(128)S(1)} %get-tuple-element.29, s32[128]{0:T(128)S(1)} %get-tuple-element.30, s32[128]{0:T(128)S(1)} %get-tuple-element.28, s32[128]{0:T(128)S(1)} %get-tuple-element.31, s32[2048]{0:T(1024)S(1)} %get-tuple-element.22, s32[2048]{0:T(1024)S(1)} %get-tuple-element.25, ...), kind=kLoop, calls=%fused_computation.11 | loop fusion | flops 8126464 | bytes 1087744 | tf_op jit(solution)/shard_map/jit(_where)/select_n | solution.py:59
  10.0 4.2 %collective-permute-done.1.low_even.refs_3_ = f32[512,128]{1,0:T(8,128)S(1)} collective-permute-done((f32[512,128]{1,0:T(8,128)S(1)}, f32[512,128]{1,0:T(8,128)S(1)}, u32[]{:S(2)}, u32[]{:S(2)}) %collective-permute-start.1) | collective-permute-done | bytes 262176 | tf_op jit(solution)/shard_map/ppermute | solution.py:480
  14.2 5.1 %collective-permute-done.2.low_odd = f32[512,128]{1,0:T(8,128)} collective-permute-done((f32[512,128]{1,0:T(8,128)S(1)}, f32[512,128]{1,0:T(8,128)}, u32[]{:S(2)}, u32[]{:S(2)}) %collective-permute-start.2) | collective-permute-done | bytes 262176 | tf_op jit(solution)/shard_map/ppermute | solution.py:480
  19.3 10.9 %collective-permute-done.visiting.even.mine.refs_0_ = f32[1024,128]{1,0:T(8,128)S(1)} collective-permute-done((f32[1024,128]{1,0:T(8,128)S(1)}, f32[1024,128]{1,0:T(8,128)S(1)}, u32[]{:S(2)}, u32[]{:S(2)}) %collective-permute-start) | collective-permute-done | bytes 524320 | tf_op jit(solution)/shard_map/ppermute | solution.py:480
  31.0 1.4 %seat.1 = (s32[13]{0:T(128)}, f32[10]{0:T(128)}) custom-call(s32[4]{0:T(128)} %offsets.1), custom_call_target="tpu_custom_call" | custom-call | tf_op jit(solution)/shard_map/seat/pallas_call | solution.py:360
  32.4 0.9 %sine_add_fusion.1 = (f32[64,64]{1,0:T(8,128)}, f32[64,64]{1,0:T(8,128)}) fusion(s32[64]{0:T(128)S(1)} %mul.125), kind=kLoop, calls=%fused_computation.34 | loop fusion | flops 122880 | bytes 33024 | tf_op jit(solution)/shard_map/add | solution.py:36
  33.3 1.6 %weights.1 = (bf16[64,192]{1,0:T(8,128)(2,1)}, bf16[64,192]{1,0:T(8,128)(2,1)}, bf16[256,256]{1,0:T(8,128)(2,1)}) custom-call(f32[64,64]{1,0:T(8,128)} %get-tuple-element.19.forward, f32[64,64]{1,0:T(8,128)} %get-tuple-element.18.backward, f32[128,128]{1,0:T(8,128)} %mul.141.paired), custom_call_target="tpu_custom_call" | custom-call | tf_op jit(solution)/shard_map/weights/pallas_call | solution.py:128
  35.0 0.9 %copy-done.1 = bf16[256,256]{1,0:T(8,128)(2,1)S(1)} copy-done((bf16[256,256]{1,0:T(8,128)(2,1)S(1)}, bf16[256,256]{1,0:T(8,128)(2,1)}, u32[]{:S(2)}) %copy-start.1) | copy-done | bytes 131096
  37.9 1.1 %shard_map.41.head = f32[1040,128]{1,0:T(8,128)S(1)} custom-call(s32[13]{0:T(128)S(1)} %copy-done.5, f32[10]{0:T(128)S(1)} %copy-done.7, f32[2048,128]{1,0:T(8,128)S(1)} %bitcast.4, f32[1024,128]{1,0:T(8,128)S(1)} %collective-permute-done.visiting.even.mine.refs_0_, bf16[64,192]{1,0:T(8,128)(2,1)S(1)} %copy-done.4, bf16[256,256]{1,0:T(8,128)(2,1)S(1)} %copy-done.1), custom_call_target="tpu_custom_call" | custom-call | flops 33554432 | bytes 2097152 | tf_op jit(solution)/shard_map/pallas_call | solution.py:218
  39.1 2.6 %spectrum.1 = (f32[2080,128]{1,0:T(8,128)S(1)}, f32[1024,128]{1,0:T(8,128)S(1)}) custom-call(s32[13]{0:T(128)S(1)} %copy-done.5, f32[10]{0:T(128)S(1)} %copy-done.7, f32[2048,128]{1,0:T(8,128)S(1)} %bitcast.5, f32[1040,128]{1,0:T(8,128)S(1)} %shard_map.41.head, f32[512,128]{1,0:T(8,128)S(1)} %collective-permute-done.1.low_even.refs_3_, ...), custom_call_target="tpu_custom_call" | custom-call | flops 167772160 | bytes 6291456 | tf_op jit(solution)/shard_map/spectrum/pallas_call | solution.py:233
  41.8 1.0 %shard_map.46 = f32[512,128]{1,0:T(8,128)S(1)} custom-call(s32[13]{0:T(128)S(1)} %copy-done.5, f32[2080,128]{1,0:T(8,128)S(1)} %get-tuple-element.14.spectral, f32[2048,128]{1,0:T(8,128)S(1)} %bitcast.6, f32[1024,128]{1,0:T(8,128)S(1)} %collective-permute-done.visiting.even.mine.refs_0_, f32[1024,128]{1,0:T(8,128)S(1)} %get-tuple-element.15.odd, ...), custom_call_target="tpu_custom_call" | custom-call | flops 50331648 | bytes 1048576 | tf_op jit(solution)/shard_map/pallas_call | solution.py:289
  43.5 1.0 %shard_map.43 = f32[512,128]{1,0:T(8,128)S(1)} custom-call(s32[13]{0:T(128)S(1)} %copy-done.5, f32[2080,128]{1,0:T(8,128)S(1)} %get-tuple-element.14.spectral, f32[2048,128]{1,0:T(8,128)S(1)} %bitcast.7, f32[1024,128]{1,0:T(8,128)S(1)} %collective-permute-done.visiting.even.mine.refs_0_, f32[1024,128]{1,0:T(8,128)S(1)} %get-tuple-element.15.odd, ...), custom_call_target="tpu_custom_call" | custom-call | flops 50331648 | bytes 1048576 | tf_op jit(solution)/shard_map/pallas_call | solution.py:289
  45.3 1.9 %collective-permute-start.9 = (f32[512,128]{1,0:T(8,128)S(1)}, f32[512,128]{1,0:T(8,128)S(1)}, u32[]{:S(2)}, u32[]{:S(2)}) collective-permute-start(f32[512,128]{1,0:T(8,128)S(1)} %shard_map.49), channel_id=1, source_target_pairs={{0,2},{1,3},{2,0},{3,1},{4,6},{5,7},{6,4},{7,5},{8,10},{9,11},{10,... | collective-permute-start | bytes 786440 | tf_op jit(solution)/shard_map/ppermute | solution.py:483
  47.2 1.0 %shard_map.45.kept.far = f32[512,128]{1,0:T(8,128)S(1)} custom-call(s32[13]{0:T(128)S(1)} %copy-done.5, f32[2080,128]{1,0:T(8,128)S(1)} %get-tuple-element.14.spectral, f32[2048,128]{1,0:T(8,128)S(1)} %bitcast.8, f32[1024,128]{1,0:T(8,128)S(1)} %collective-permute-done.visiting.even.mine.refs_0_, f32[1024,128]{1,0:T(8,128)S(1)} %get-tuple-element.15.odd, ...), custom_call_target="tpu_custom_call" | custom-call | flops 50331648 | bytes 1048576 | tf_op jit(solution)/shard_map/pallas_call | solution.py:289
  49.1 1.0 %shard_map.42.kept.near = f32[512,128]{1,0:T(8,128)S(1)} custom-call(s32[13]{0:T(128)S(1)} %copy-done.6, f32[2080,128]{1,0:T(8,128)S(1)} %get-tuple-element.14.spectral, f32[2048,128]{1,0:T(8,128)S(1)} %bitcast.9, f32[1024,128]{1,0:T(8,128)S(1)} %collective-permute-done.visiting.even.mine.refs_0_, f32[1024,128]{1,0:T(8,128)S(1)} %get-tuple-element.15.odd, ...), custom_call_target="tpu_custom_call" | custom-call | flops 50331648 | bytes 1048576 | tf_op jit(solution)/shard_map/pallas_call | solution.py:289
  50.1 2.4 %collective-permute-done.10.refs_5_ = f32[512,128]{1,0:T(8,128)S(1)} collective-permute-done((f32[512,128]{1,0:T(8,128)S(1)}, f32[512,128]{1,0:T(8,128)S(1)}, u32[]{:S(2)}, u32[]{:S(2)}) %collective-permute-start.10) | collective-permute-done | bytes 262176 | tf_op jit(solution)/shard_map/ppermute | solution.py:483
  52.6 5.6 %collective-permute-done.9.refs_2_ = f32[512,128]{1,0:T(8,128)S(1)} collective-permute-done((f32[512,128]{1,0:T(8,128)S(1)}, f32[512,128]{1,0:T(8,128)S(1)}, u32[]{:S(2)}, u32[]{:S(2)}) %collective-permute-start.9) | collective-permute-done | bytes 262176 | tf_op jit(solution)/shard_map/ppermute | solution.py:483
  58.2 1.5 %shard_map.50 = f32[8,128]{1,0:T(8,128)S(1)} custom-call(s32[13]{0:T(128)S(1)} %copy-done.6, f32[10]{0:T(128)S(1)} %copy-done.7, f32[512,128]{1,0:T(8,128)S(1)} %shard_map.45.kept.far, f32[512,128]{1,0:T(8,128)S(1)} %collective-permute-done.6.met.met_far, f32[512,128]{1,0:T(8,128)S(1)} %shard_map.42.kept.near, ...), custom_call_target="tpu_custom_call" | custom-call | flops 2097152 | bytes 3145728 | tf_op jit(solution)/shard_map/pallas_call | solution.py:416
  59.8 1.2 %collective-permute-done.11 = f32[8,128]{1,0:T(8,128)S(1)} collective-permute-done((f32[8,128]{1,0:T(8,128)S(1)}, f32[8,128]{1,0:T(8,128)S(1)}, u32[]{:S(2)}, u32[]{:S(2)}) %collective-permute-start.11) | collective-permute-done | bytes 4128 | tf_op jit(solution)/shard_map/ppermute | solution.py:483
  61.6 1.3 %collective-permute-done.7.second = f32[512,128]{1,0:T(8,128)S(1)} collective-permute-done((f32[512,128]{1,0:T(8,128)S(1)}, f32[512,128]{1,0:T(8,128)S(1)}, u32[]{:S(2)}, u32[]{:S(2)}) %collective-permute-start.7) | collective-permute-done | bytes 262176 | tf_op jit(solution)/shard_map/ppermute | solution.py:483
  63.6 0.9 %collective-permute-done.12 = f32[8,128]{1,0:T(8,128)S(1)} collective-permute-done((f32[8,128]{1,0:T(8,128)S(1)}, f32[8,128]{1,0:T(8,128)S(1)}, u32[]{:S(2)}, u32[]{:S(2)}) %collective-permute-start.12) | collective-permute-done | bytes 4128 | tf_op jit(solution)/shard_map/ppermute | solution.py:483
  (49 shorter events, 7.7 us)
Async XLA Ops:
  0.6 6.3 %copy-start = (f32[1,262144]{1,0:T(1,128)S(1)}, f32[1,262144]{1,0:T(1,128)}, u32[]{:S(2)}) copy-start(f32[1,262144]{1,0:T(1,128)} %param.2) | copy-start | bytes 3145732
  1.8 12.4 %collective-permute-start.1 = (f32[512,128]{1,0:T(8,128)S(1)}, f32[512,128]{1,0:T(8,128)S(1)}, u32[]{:S(2)}, u32[]{:S(2)}) collective-permute-start(f32[512,128]{1,0:T(8,128)S(1)} %get-tuple-element.17), channel_id=1, source_target_pairs={{12,0},{13,1},{10,2},{11,3},{8,4},{9,5},{14,6},{15,7},{4,8},{5,9},... | collective-permute-start | bytes 786440 | tf_op jit(solution)/shard_map/ppermute | solution.py:480
  7.0 12.3 %collective-permute-start.2 = (f32[512,128]{1,0:T(8,128)S(1)}, f32[512,128]{1,0:T(8,128)}, u32[]{:S(2)}, u32[]{:S(2)}) collective-permute-start(f32[512,128]{1,0:T(8,128)S(1)} %get-tuple-element.16), channel_id=1, source_target_pairs={{4,0},{5,1},{6,2},{7,3},{0,4},{1,5},{2,6},{3,7},{12,8},{13,9},{14,... | collective-permute-start | bytes 786440 | tf_op jit(solution)/shard_map/ppermute | solution.py:480
  7.0 23.2 %collective-permute-start = (f32[1024,128]{1,0:T(8,128)S(1)}, f32[1024,128]{1,0:T(8,128)S(1)}, u32[]{:S(2)}, u32[]{:S(2)}) collective-permute-start(f32[1024,128]{1,0:T(8,128)S(1)} %bitcast.11), channel_id=1, source_target_pairs={{12,0},{5,1},{10,2},{7,3},{8,4},{1,5},{14,6},{3,7},{4,8},{13,9},{2... | collective-permute-start | bytes 1572872 | tf_op jit(solution)/shard_map/ppermute | solution.py:480
  14.2 24.9 %collective-permute-start.3 = (f32[512,128]{1,0:T(8,128)S(1)}, f32[512,128]{1,0:T(8,128)}, u32[]{:S(2)}, u32[]{:S(2)}) collective-permute-start(f32[512,128]{1,0:T(8,128)S(1)} %collective-permute-done.1.low_even.refs_3_), channel_id=1, source_target_pairs={{0,1},{1,0},{2,3},{3,2},{4,5},{5,4},{6,7},{7,6},{8,9},{9,8},{10,11... | collective-permute-start | bytes 786440 | tf_op jit(solution)/shard_map/ppermute | solution.py:483
  19.3 19.8 %collective-permute-start.4 = (f32[512,128]{1,0:T(8,128)}, f32[512,128]{1,0:T(8,128)}, u32[]{:S(2)}, u32[]{:S(2)}) collective-permute-start(f32[512,128]{1,0:T(8,128)} %collective-permute-done.2.low_odd), channel_id=1, source_target_pairs={{0,1},{1,0},{2,3},{3,2},{4,5},{5,4},{6,7},{7,6},{8,9},{9,8},{10,11... | collective-permute-start | bytes 786440 | tf_op jit(solution)/shard_map/ppermute | solution.py:483
  30.2 14.5 %collective-permute-start.8 = (f32[1024,128]{1,0:T(8,128)S(1)}, f32[1024,128]{1,0:T(8,128)S(1)}, u32[]{:S(2)}, u32[]{:S(2)}) collective-permute-start(f32[1024,128]{1,0:T(8,128)S(1)} %collective-permute-done.visiting.even.mine.refs_0_), channel_id=1, source_target_pairs={{0,1},{1,0},{2,3},{3,2},{4,5},{5,4},{6,7},{7,6},{8,9},{9,8},{10,11... | collective-permute-start | bytes 1572872 | tf_op jit(solution)/shard_map/ppermute | solution.py:483
  35.0 0.9 %copy-start.1 = (bf16[256,256]{1,0:T(8,128)(2,1)S(1)}, bf16[256,256]{1,0:T(8,128)(2,1)}, u32[]{:S(2)}) copy-start(bf16[256,256]{1,0:T(8,128)(2,1)} %get-tuple-element.12.lanes) | copy-start | bytes 393220
  35.9 0.8 %copy-start.4 = (bf16[64,192]{1,0:T(8,128)(2,1)S(1)}, bf16[64,192]{1,0:T(8,128)(2,1)}, u32[]{:S(2)}) copy-start(bf16[64,192]{1,0:T(8,128)(2,1)} %get-tuple-element.11.left_y) | copy-start | bytes 73732
  36.6 0.7 %copy-start.5 = (s32[13]{0:T(128)S(1)}, s32[13]{0:T(128)}, u32[]{:S(2)}) copy-start(s32[13]{0:T(128)} %get-tuple-element.10.places) | copy-start | bytes 160
  37.3 0.7 %copy-start.7 = (f32[10]{0:T(128)S(1)}, f32[10]{0:T(128)}, u32[]{:S(2)}) copy-start(f32[10]{0:T(128)} %get-tuple-element.9.factors) | copy-start | bytes 124
  37.9 1.2 %copy-start.2 = (bf16[256,256]{1,0:T(8,128)(2,1)S(1)}, bf16[256,256]{1,0:T(8,128)(2,1)}, u32[]{:S(2)}) copy-start(bf16[256,256]{1,0:T(8,128)(2,1)} %get-tuple-element.12.lanes) | copy-start | bytes 393220
  37.9 1.2 %copy-start.3 = (bf16[64,192]{1,0:T(8,128)(2,1)S(1)}, bf16[64,192]{1,0:T(8,128)(2,1)}, u32[]{:S(2)}) copy-start(bf16[64,192]{1,0:T(8,128)(2,1)} %get-tuple-element.13.left_back) | copy-start | bytes 73732
  42.8 5.4 %collective-permute-start.6 = (f32[512,128]{1,0:T(8,128)S(1)}, f32[512,128]{1,0:T(8,128)S(1)}, u32[]{:S(2)}, u32[]{:S(2)}) collective-permute-start(f32[512,128]{1,0:T(8,128)S(1)} %shard_map.46), channel_id=1, source_target_pairs={{0,1},{1,0},{2,3},{3,2},{4,5},{5,4},{6,7},{7,6},{8,9},{9,8},{10,11... | collective-permute-start | bytes 786440 | tf_op jit(solution)/shard_map/ppermute | solution.py:483
  43.4 9.2 %collective-permute-start.10 = (f32[512,128]{1,0:T(8,128)S(1)}, f32[512,128]{1,0:T(8,128)S(1)}, u32[]{:S(2)}, u32[]{:S(2)}) collective-permute-start(f32[512,128]{1,0:T(8,128)S(1)} %collective-permute-done.1.low_even.refs_3_), channel_id=1, source_target_pairs={{0,2},{1,3},{2,0},{3,1},{4,6},{5,7},{6,4},{7,5},{8,10},{9,11},{10,... | collective-permute-start | bytes 786440 | tf_op jit(solution)/shard_map/ppermute | solution.py:483
  44.5 8.0 %collective-permute-start.5 = (f32[512,128]{1,0:T(8,128)S(1)}, f32[512,128]{1,0:T(8,128)S(1)}, u32[]{:S(2)}, u32[]{:S(2)}) collective-permute-start(f32[512,128]{1,0:T(8,128)S(1)} %shard_map.43), channel_id=1, source_target_pairs={{0,1},{1,0},{2,3},{3,2},{4,5},{5,4},{6,7},{7,6},{8,9},{9,8},{10,11... | collective-permute-start | bytes 786440 | tf_op jit(solution)/shard_map/ppermute | solution.py:483
  45.3 3.8 %copy-start.6 = (s32[13]{0:T(128)S(1)}, s32[13]{0:T(128)}, u32[]{:S(2)}) copy-start(s32[13]{0:T(128)} %get-tuple-element.10.places) | copy-start | bytes 160
  45.3 12.8 %collective-permute-start.9 = (f32[512,128]{1,0:T(8,128)S(1)}, f32[512,128]{1,0:T(8,128)S(1)}, u32[]{:S(2)}, u32[]{:S(2)}) collective-permute-start(f32[512,128]{1,0:T(8,128)S(1)} %shard_map.49), channel_id=1, source_target_pairs={{0,2},{1,3},{2,0},{3,1},{4,6},{5,7},{6,4},{7,5},{8,10},{9,11},{10,... | collective-permute-start | bytes 786440 | tf_op jit(solution)/shard_map/ppermute | solution.py:483
  48.8 14.1 %collective-permute-start.7 = (f32[512,128]{1,0:T(8,128)S(1)}, f32[512,128]{1,0:T(8,128)S(1)}, u32[]{:S(2)}, u32[]{:S(2)}) collective-permute-start(f32[512,128]{1,0:T(8,128)S(1)} %shard_map.47), channel_id=1, source_target_pairs={{0,2},{1,3},{2,0},{3,1},{4,6},{5,7},{6,4},{7,5},{8,10},{9,11},{10,... | collective-permute-start | bytes 786440 | tf_op jit(solution)/shard_map/ppermute | solution.py:483
  59.7 1.2 %collective-permute-start.11 = (f32[8,128]{1,0:T(8,128)S(1)}, f32[8,128]{1,0:T(8,128)S(1)}, u32[]{:S(2)}, u32[]{:S(2)}) collective-permute-start(f32[8,128]{1,0:T(8,128)S(1)} %shard_map.50), channel_id=1, source_target_pairs={{0,1},{1,0},{2,3},{3,2},{4,5},{5,4},{6,7},{7,6},{8,9},{9,8},{10,11... | collective-permute-start | bytes 12296 | tf_op jit(solution)/shard_map/ppermute | solution.py:483
  60.9 3.6 %collective-permute-start.12 = (f32[8,128]{1,0:T(8,128)S(1)}, f32[8,128]{1,0:T(8,128)S(1)}, u32[]{:S(2)}, u32[]{:S(2)}) collective-permute-start(f32[8,128]{1,0:T(8,128)S(1)} %add.102), channel_id=1, source_target_pairs={{0,2},{1,3},{2,0},{3,1},{4,6},{5,7},{6,4},{7,5},{8,10},{9,11},{10,... | collective-permute-start | bytes 12296 | tf_op jit(solution)/shard_map/ppermute | solution.py:483

commit v5 on v4

--- a/solution.py
+++ b/solution.py
@@ -161,31 +161,34 @@
     lax.fori_loop(0, steps, step_planes, 0, unroll=steps)
 
 
-def first_body(places, factors, own, visiting, left_y, lanes, out, along_z):
-    def visit_at(at):
-        return visiting[at : at + GROUP, :]
-
-    planes_body(own, visit_at, places[SAME] == 1, left_y, lanes, along_z, out, first_row=0)
-
-
-def spectrum_body(
-    places, factors, own, head, low_even, low_odd, high_even, high_odd, kernel, left_y, left_back, lanes, out, late,
-    tail, along_z,
-):
-    plane = NG // 2
-    pairs = NG // 4
-    mask = low_mask(plane)
-    slab_rows = low_even.shape[0]
+def slabs_body(places, own, choices, left_y, lanes, along_z, out, partner, *, first_slab):
+    slab_rows = choices[0].shape[0]
     even = places[LOW] == 0
+    alone = places[SAME] == 1
+    first_row = first_slab * slab_rows
 
     def visit_at(at):
         inside = slice(at % slab_rows, at % slab_rows + GROUP)
-        by_parity = (low_even, low_odd) if at < slab_rows else (high_even, high_odd)
-        value = jnp.where(even, by_parity[0][inside, :], by_parity[1][inside, :])
-        late[at : at + GROUP, :] = value
+        index = at // slab_rows * 2
+        value = jnp.where(even, choices[index][inside, :], choices[index + 1][inside, :])
+        partner[at : at + GROUP, :] = jnp.where(alone, own[first_row + at : first_row + at + GROUP, :], value)
         return value
 
-    planes_body(own, visit_at, places[SAME] == 1, left_y, lanes, along_z, tail, first_row=2 * slab_rows)
+    planes_body(own, visit_at, alone, left_y, lanes, along_z, out, first_row=first_row)
+
+
+def first_body(places, factors, own, *refs, first_slab, count):
+    choices, (left_y, lanes, out, partner, along_z) = refs[: 2 * count], refs[2 * count :]
+    slabs_body(places, own, choices, left_y, lanes, along_z, out, partner, first_slab=first_slab)
+
+
+def spectrum_body(places, factors, own, *refs, heads, first_slab, count):
+    parts, choices, rest = refs[:heads], refs[heads : heads + 2 * count], refs[heads + 2 * count :]
+    kernel, left_y, left_back, lanes, out, partner, tail, along_z = rest
+    plane = NG // 2
+    mask = low_mask(plane)
+    slabs_body(places, own, choices, left_y, lanes, along_z, tail, partner, first_slab=first_slab)
+    parts = (*parts, tail)
     w_forward = left_y[...]
     w_backward = left_back[...]
 
@@ -194,7 +197,9 @@
         for part in range(2):
             row = 4 * step + 2 * part
             first, second = (
-                jnp.concatenate([half[pl.ds(row + odd, pairs, stride=PITCH), :] for half in (head, tail)], axis=0)
+                jnp.concatenate(
+                    [ref[pl.ds(row + odd, ref.shape[0] // PITCH, stride=PITCH), :] for ref in parts], axis=0
+                )
                 for odd in range(2)
             )
             blocks.append(jnp.concatenate(swapped(first, second, mask), axis=0))
@@ -212,88 +217,91 @@
     lax.fori_loop(0, NG // 4, columns, 0, unroll=NG // 4)
 
 
-def first_planes(places, factors, own, visiting, weights):
-    left_y, _, lanes = weights
-    rows = visiting.shape[0]
-    return kernel_call(
-        first_body,
-        (rows // NG * PITCH, LANES),
-        "ssvvvv",
-        rows * LANES * NG * 4,
-        4 * rows * LANES,
-        scratch_shapes=[pltpu.VMEM((rows, LANES), jnp.float32)],
-    )(places, factors, own, visiting, left_y, lanes)
-
-
-def spectrum(places, factors, own, head, quarters, kernel, weights):
-    rows = own.shape[0]
+def planes_call(body, spaces, planes_rows, partner_rows, scratch_rows, flops, cells):
     smem = pl.BlockSpec(memory_space=pltpu.SMEM)
     vmem = pl.BlockSpec(memory_space=pltpu.VMEM)
-    half = rows // 2
     return pl.pallas_call(
-        spectrum_body,
-        out_shape=[
-            jax.ShapeDtypeStruct((rows // NG * PITCH, LANES), jnp.float32),
-            jax.ShapeDtypeStruct((half, LANES), jnp.float32),
-        ],
-        in_specs=[smem] * 2 + [vmem] * 10,
+        body,
+        out_shape=[jax.ShapeDtypeStruct((rows, LANES), jnp.float32) for rows in (planes_rows, partner_rows)],
+        in_specs=[smem] * 2 + [vmem] * spaces,
         out_specs=[vmem] * 2,
-        scratch_shapes=[
-            pltpu.VMEM((half // NG * PITCH, LANES), jnp.float32),
-            pltpu.VMEM((half, LANES), jnp.float32),
-        ],
+        scratch_shapes=[pltpu.VMEM((rows, LANES), jnp.float32) for rows in scratch_rows],
         compiler_params=pltpu.CompilerParams(vmem_limit_bytes=24 << 20),
-        cost_estimate=pl.CostEstimate(
-            flops=rows * LANES * NG * 10, bytes_accessed=24 * rows * LANES, transcendentals=0
-        ),
-        name="spectrum",
-    )(places, factors, own, head, *quarters, kernel, *weights)
-
-
-def term_body(places, spectral, own, even, odd, left_back, lanes, out, back_y, *, which):
+        cost_estimate=pl.CostEstimate(flops=flops, bytes_accessed=4 * cells, transcendentals=0),
+    )
+
+
+def first_planes(first_slab, places, factors, own, choices, weights):
+    left_y, _, lanes = weights
+    count = len(choices) // 2
+    rows = count * choices[0].shape[0]
+    body = functools.partial(first_body, first_slab=first_slab, count=count)
+    pitched = rows // NG * PITCH
+    return planes_call(
+        body, 3 + 2 * count, pitched, rows, (rows,), rows * LANES * NG * 4, 4 * rows * LANES
+    )(places, factors, own, *choices, left_y, lanes)
+
+
+def spectrum(first_slab, places, factors, own, heads, choices, kernel, weights):
+    count = len(choices) // 2
+    rows, last = own.shape[0], count * choices[0].shape[0]
+    body = functools.partial(spectrum_body, heads=len(heads), first_slab=first_slab, count=count)
+    pitched = rows // NG * PITCH, last // NG * PITCH
+    return planes_call(
+        body, 5 + len(heads) + 2 * count, pitched[0], last, (pitched[1], last), rows * LANES * NG * 10, 6 * rows * LANES
+    )(places, factors, own, *heads, *choices, kernel, *weights)
+
+
+def terms_body(places, spectral, *refs, which):
+    partners, (left_back, lanes, *outs, back_y) = refs[: -3 - len(which)], refs[-3 - len(which) :]
     plane = NG // 2
     mask = low_mask(plane)
     w_backward = left_back[...]
     w_lanes = lanes[...]
-    slab_rows = out.shape[0]
-    start = places[which] * slab_rows
-    half_rows = even.shape[0]
-    alone = places[SAME] == 1
-    later = start >= half_rows
-    inside = start % half_rows
-
-    def step_planes(step, _):
-        at = step * (4 * plane)
-        row = (start // NG + 2 * step) * PITCH
-        pair = jnp.concatenate([spectral[pl.ds(row, NG), :], spectral[pl.ds(row + PITCH, NG), :]], axis=1)
-        along_y = from_left(w_backward, pair)
-        for half in range(2):
-            block = along_y[:, half * LANES : (half + 1) * LANES]
-            for second, value in enumerate(swapped(block[:plane], block[plane:], mask)):
-                line = pl.multiple_of(at + (2 * half + second) * plane, plane)
-                back_y[pl.ds(line, plane), :] = value
-        return 0
-
+    slab_rows = outs[0].shape[0]
     steps = slab_rows // (4 * plane)
-    lax.fori_loop(0, steps, step_planes, 0, unroll=steps)
-    for at in range(0, slab_rows, GROUP):
-        potential = along_lanes(back_y[at : at + GROUP, :], w_lanes)
-        near = pl.ds(pl.multiple_of(inside + at, 8), GROUP)
-        visiting = jnp.where(later, odd[near, :], even[near, :])
-        partner = jnp.where(alone, own[pl.ds(pl.multiple_of(start + at, 8), GROUP), :], visiting)
-        out[at : at + GROUP, :] = potential * (partner * (1.0 / NG**3))
-
-
-def term(which, slab_rows, places, spectral, own, pieces, weights):
-    cells = slab_rows * LANES
-    return kernel_call(
-        functools.partial(term_body, which=which),
-        (slab_rows, LANES),
-        "svvvvvv",
-        cells * NG * 12,
-        4 * cells,
-        scratch_shapes=[pltpu.VMEM((slab_rows, LANES), jnp.float32)],
-    )(places, spectral, own, *pieces, weights[1], weights[2])
+
+    def partner_at(slab, at):
+        value, first_slab = None, 0
+        for piece in partners:
+            count = piece.shape[0] // slab_rows
+            row = jnp.clip(slab - first_slab, 0, count - 1) * slab_rows + at
+            here = piece[pl.ds(pl.multiple_of(row, 8), GROUP), :]
+            value = here if value is None else jnp.where(slab >= first_slab, here, value)
+            first_slab += count
+        return value
+
+    for index, entry in enumerate(which):
+        start = places[entry] * slab_rows
+        for step in range(steps):
+            row = (start // NG + 2 * step) * PITCH
+            pair = jnp.concatenate([spectral[pl.ds(row, NG), :], spectral[pl.ds(row + PITCH, NG), :]], axis=1)
+            along_y = from_left(w_backward, pair)
+            for half in range(2):
+                block = along_y[:, half * LANES : (half + 1) * LANES]
+                for second, value in enumerate(swapped(block[:plane], block[plane:], mask)):
+                    line = index * slab_rows + (4 * step + 2 * half + second) * plane
+                    back_y[line : line + plane, :] = value
+    for index, entry in enumerate(which):
+        for at in range(0, slab_rows, GROUP):
+            line = index * slab_rows + at
+            potential = along_lanes(back_y[line : line + GROUP, :], w_lanes)
+            outs[index][at : at + GROUP, :] = potential * (partner_at(places[entry], at) * (1.0 / NG**3))
+
+
+def exchange_terms(which, slab_rows, places, spectral, partners, weights):
+    cells = len(which) * slab_rows * LANES
+    vmem = pl.BlockSpec(memory_space=pltpu.VMEM)
+    return pl.pallas_call(
+        functools.partial(terms_body, which=which),
+        out_shape=[jax.ShapeDtypeStruct((slab_rows, LANES), jnp.float32) for _ in which],
+        in_specs=[pl.BlockSpec(memory_space=pltpu.SMEM)] + [vmem] * (3 + len(partners)),
+        out_specs=[vmem] * len(which),
+        scratch_shapes=[pltpu.VMEM((len(which) * slab_rows, LANES), jnp.float32)],
+        compiler_params=pltpu.CompilerParams(vmem_limit_bytes=24 << 20),
+        cost_estimate=pl.CostEstimate(flops=cells * NG * 12, bytes_accessed=16 * cells, transcendentals=0),
+        name="terms",
+    )(places, spectral, *partners, weights[1], weights[2])
 
 
 def blend_body(factors, kept, met, out):
@@ -304,22 +312,27 @@
     return kernel_call(blend_body, kept.shape, "svv", 3 * kept.size, 3 * kept.size)(factors, kept, met)
 
 
-def join_body(first, second, out):
-    out[...] = first[...] + second[...]
-
-
-def join(first, second):
-    return kernel_call(join_body, first.shape, "vv", first.size, 3 * first.size)(first, second)
-
-
-def pick_body(places, mine, near, out):
-    rows = out.shape[0]
-    out[...] = jnp.where(places[LOW] == 0, mine[:rows, :], near[rows:, :])
-
-
-def pick(places, mine, near):
-    rows = mine.shape[0] // 2
-    return kernel_call(pick_body, (rows, LANES), "svv", rows * LANES, 3 * rows * LANES)(places, mine, near)
+def finish_body(near_sum, arrived, row, other, exchanged, margin):
+    exchanged[...] = near_sum[...] + arrived[...]
+    margin[...] = (row[...] + other[...])[:1, : margin.shape[1]]
+
+
+def finish(near_sum, arrived, row, other, columns):
+    vmem = pl.BlockSpec(memory_space=pltpu.VMEM)
+    return pl.pallas_call(
+        finish_body,
+        out_shape=[
+            jax.ShapeDtypeStruct(near_sum.shape, jnp.float32),
+            jax.ShapeDtypeStruct((1, columns), jnp.float32),
+        ],
+        in_specs=[vmem] * 4,
+        out_specs=[vmem] * 2,
+        compiler_params=pltpu.CompilerParams(vmem_limit_bytes=24 << 20),
+        cost_estimate=pl.CostEstimate(
+            flops=near_sum.size, bytes_accessed=12 * near_sum.size, transcendentals=0
+        ),
+        name="finish",
+    )(near_sum, arrived, row, other)
 
 
 def seat_body(offsets, places, factors, *, blocks, replicas):
@@ -370,7 +383,7 @@
 
 
 def gram_body(places, factors, far, met_far, near, met_near, own, *refs):
-    piece_a, near_a, moved_a, late_a, late_b, moved_b, out = refs
+    *stores, out = refs
     even = places[LOW] == 0
     rows = far.shape[0]
     chunk = 64
@@ -381,23 +394,19 @@
     totals = (jnp.zeros((8, LANES), jnp.float32),) * 8
     for side in range(2):
         is_near = places[HIGH] == side
-        parity_row = places[LOW] * rows
+        piece_a, near_b, moved_a = stores[3 * side : 3 * side + 3]
         own_row = places[OWN + side] * rows
 
-        def step(index, totals, side=side, is_near=is_near, parity_row=parity_row, own_row=own_row):
+        def step(index, totals, is_near=is_near, piece_a=piece_a, near_b=near_b, moved_a=moved_a, own_row=own_row):
             inside = index * chunk
             at = pl.ds(pl.multiple_of(inside, chunk), chunk)
-            half = pl.ds(pl.multiple_of(parity_row + inside, chunk), chunk)
             mine = pl.ds(pl.multiple_of(own_row + inside, chunk), chunk)
             terms = (
                 jnp.where(is_near, near[at, :], far[at, :]),
                 jnp.where(is_near, met_near[at, :], met_far[at, :]),
             )
-            if side == 0:
-                orbitals = (own[mine, :], piece_a[half, :], near_a[half, :], moved_a[at, :])
-            else:
-                of_a, of_b = late_a[at, :], late_b[at, :]
-                orbitals = (own[mine, :], jnp.where(even, of_a, of_b), jnp.where(even, of_b, of_a), moved_b[at, :])
+            of_a, of_b = piece_a[at, :], near_b[at, :]
+            orbitals = (own[mine, :], jnp.where(even, of_a, of_b), jnp.where(even, of_b, of_a), moved_a[at, :])
             return tuple(
                 totals[4 * t + o] + folded_rows(terms[t] * orbitals[o]) for t in range(2) for o in range(4)
             )
@@ -444,15 +453,16 @@
     whole = jnp.zeros((rows, LANES), jnp.float32)
     for visit in visits:
         visit = visit.reshape(rows, LANES)
-        pieces = visit[: rows // 2], visit[rows // 2 :]
-        head = first_planes(places, factors, own, pieces[0], weights)
-        quarters = [pieces[1][at : at + rows // SLABS] for at in (0, 0, rows // SLABS, rows // SLABS)]
-        spectral, _ = spectrum(places, factors, own, head, quarters, kernel, weights)
-        slabs = [
-            term(FAR_SENT, rows // SLABS, places.at[FAR_SENT].set(slab), spectral, own, pieces, weights)
-            for slab in range(SLABS)
-        ]
-        whole = whole + jnp.concatenate(slabs, axis=0)
+        slab_rows = rows // SLABS
+        slabs = [visit[slab * slab_rows : (slab + 1) * slab_rows] for slab in range(SLABS)]
+        choices = [slabs[index // 2] for index in range(2 * SLABS)]
+        head, partner_a = first_planes(0, places, factors, own, choices[:4], weights)
+        spectral, partner_b = spectrum(2, places, factors, own, (head,), choices[4:], kernel, weights)
+        numbers = jnp.arange(SLABS, dtype=jnp.int32)
+        spots = places.at[FAR_SENT : FAR_SENT + SLABS].set(numbers)
+        which = tuple(range(FAR_SENT, FAR_SENT + SLABS))
+        terms = exchange_terms(which, slab_rows, spots, spectral, (partner_a, partner_b), weights)
+        whole = whole + jnp.concatenate(terms, axis=0)
     exchanged = lax.psum_scatter(whole.reshape(1, cells), "rep", scatter_dimension=1, tiled=True)
     quarter = lax.dynamic_slice_in_dim(orbitals, replica * (cells // replicas), cells // replicas, 1)
     slab_orbitals = lax.all_to_all(quarter, "blk", split_axis=1, concat_axis=0, tiled=True)
@@ -485,46 +495,48 @@
     def slab_of(index):
         return lax.dynamic_slice_in_dim(own, index * slab_rows, slab_rows, 0)
 
-    piece_a = along_blocks(own[: 2 * slab_rows], SENT)
-    late_b = along_blocks(slab_of(3 - low), SENT_B)
-    late_a = along_blocks(slab_of(2 + low), SENT_A)
-
-    near_a = replica_swap(piece_a, 1)
-
-    moved_a = replica_swap(pick(places, piece_a, near_a), 2)
+    a_first = along_blocks(slab_of(low), SENT_A)
+    b_first = along_blocks(slab_of(1 - low), SENT_B)
+    b_last = along_blocks(slab_of(3 - low), SENT_B)
+    a_last = along_blocks(slab_of(2 + low), SENT_A)
     kernel = screened_kernel(NG)
-    head = first_planes(places, factors, own, piece_a, weights)
-    near_late_b = replica_swap(late_b, 1)
-    near_late_a = replica_swap(late_a, 1)
-    moved_b = replica_swap(late_a, 2)
-    quarters = late_a, late_b, near_late_a, near_late_b
-    spectral, piece_b = spectrum(places, factors, own, head, quarters, kernel, weights)
-    pieces = piece_a, piece_b
-    terms = {}
-    for which in (FAR_SENT, FAR_KEPT, NEAR_SENT, NEAR_KEPT):
-        terms[which] = term(which, slab_rows, places, spectral, own, pieces, weights)
-    met_far = replica_swap(terms[FAR_SENT], 1)
-    met_near = replica_swap(terms[NEAR_SENT], 1)
-
-    arrived = replica_swap(blend(factors, terms[FAR_KEPT], met_far), 2)
+
+    near_a_first = replica_swap(a_first, 1)
+    near_b_first = replica_swap(b_first, 1)
+    moved_first = replica_swap(a_first, 2)
+    head, partner = first_planes(
+        0, places, factors, own, (a_first, b_first, near_a_first, near_b_first), weights
+    )
+    near_a_last = replica_swap(a_last, 1)
+    near_b_last = replica_swap(b_last, 1)
+    moved_last = replica_swap(a_last, 2)
+    third, third_partner = first_planes(2, places, factors, own, (a_last, b_last), weights)
+    spectral, last_partner = spectrum(
+        3, places, factors, own, (head, third), (near_a_last, near_b_last), kernel, weights
+    )
+    partners = partner, third_partner, last_partner
+    sent = exchange_terms((FAR_SENT, NEAR_SENT), slab_rows, places, spectral, partners, weights)
+    met_far = replica_swap(sent[0], 1)
+    met_near = replica_swap(sent[1], 1)
+    kept = exchange_terms((FAR_KEPT, NEAR_KEPT), slab_rows, places, spectral, partners, weights)
+    arrived = replica_swap(blend(factors, kept[0], met_far), 2)
     row = gram(
         places,
         factors,
-        (terms[FAR_KEPT], met_far),
-        (terms[NEAR_KEPT], met_near),
+        (kept[0], met_far),
+        (kept[1], met_near),
         own,
-        piece_a,
-        near_a,
-        moved_a,
-        late_a,
-        near_late_b,
-        moved_b,
-    )
-    near_sum = blend(factors, terms[NEAR_KEPT], met_near)
+        a_first,
+        near_b_first,
+        moved_first,
+        a_last,
+        near_b_last,
+        moved_last,
+    )
+    near_sum = blend(factors, kept[1], met_near)
     row = row + replica_swap(row, 1)
     other = replica_swap(row, 2)
-    margin = row[:1, :blocks] + other[:1, :blocks]
-    exchanged = join(near_sum, arrived)
+    exchanged, margin = finish(near_sum, arrived, row, other, blocks)
     return exchanged.reshape(1, cells // replicas), margin
 
 

time: 65.4 us -> 60.3 us (0.922)
  local copies, waits for them, and re-layouts: 5.01 us -> 2.14 us
  starting transfers between devices: 9.35 us -> 11.9 us
  Pallas kernels: 14.9 us -> 12.4 us
  waiting for transfers between devices: 31.6 us -> 29.8 us
    ppermute x3 -> x4, waiting for transfers between devices: 20.2 us -> 16.1 us  [along_blocks(): return lax.ppermute(value, ('blk', 'rep'), route)]
    unnamed x16 -> x12, local copies, waits for them, and re-layouts: 3 us -> 0.03 us
    ppermute x10 -> x11, waiting for transfers between devices: 11.4 us -> 13.7 us  [replica_swap(): return lax.ppermute(value, 'rep', [(r, r ^ bit) for r in range(replicas)])]
    pallas_call x8 -> x6, Pallas kernels: 9.18 us -> 7.17 us  [the longest x2 2.24 us: exchange_terms(): pl.pallas_call(functools.partial(terms_body, which=which), out_shape=[jax...]
    ppermute x10 -> x11, starting transfers between devices: 3.25 us -> 4.7 us  [replica_swap(): return lax.ppermute(value, 'rep', [(r, r ^ bit) for r in range(replicas)])]
    ppermute x3 -> x4, starting transfers between devices: 6.11 us -> 7.17 us  [along_blocks(): return lax.ppermute(value, ('blk', 'rep'), route)]
  transfers between devices with their start and end apart: 13 -> 15, of which waited for: 8 -> 6; matrix products, arithmetic and copies ran while one was open for 6% -> 6% of each run, Pallas kernels for 23% -> 14%
where the time goes in v5:
time: 60.3 us; the launch traced here: 60.1 us
  waiting for transfers between devices  29.8 us (49%)
  Pallas kernels  12.4 us (21%)
  starting transfers between devices  11.9 us (20%)
  other arithmetic  2.91 us (5%)
  local copies, waits for them, and re-layouts  2.14 us (4%)
  between operations  0.92 us (2%)
    ppermute x4, waiting for transfers between devices, along_blocks(): return lax.ppermute(value, ('blk', 'rep'), route)  16.1 us
    ppermute x11, waiting for transfers between devices, replica_swap(): return lax.ppermute(value, 'rep', [(r, r ^ bit) for r in range(replicas)])  13.7 us
    ppermute x4, starting transfers between devices, along_blocks(): return lax.ppermute(value, ('blk', 'rep'), route)  7.17 us
    ppermute x11, starting transfers between devices, replica_swap(): return lax.ppermute(value, 'rep', [(r, r ^ bit) for r in range(replicas)])  4.7 us
    pallas_call x2, Pallas kernels, exchange_terms(): pl.pallas_call(functools.partial(terms_body, which=which), out_shape=[jax...  2.24 us
    pallas_call x2, Pallas kernels, first_planes(): planes_call(body, 3 + 2 * count, pitched, rows, (rows,), rows * LANES * N...  2.17 us
    pallas_call x1, Pallas kernels, spectrum(): planes_call(body, 5 + len(heads) + 2 * count, pitched[0], last, (pitched[...  2.02 us
    select_n x1, other arithmetic, screened_kernel(): return jnp.where(k_squared > 0.5, screened, jnp.ones_like(screened))  1.7 us
  transfers between devices with their start and end apart: 15, of which 6 were waited for; matrix products, arithmetic and copies ran while one was open for 6% of the time, Pallas kernels for 14%

profile of v5, /device:TPU:0, one launch (start us, length us, event | category | flops | bytes accessed | tf_op | source)
XLA Modules:
  0.0 60.1 jit_solution(5406172465343523175)
XLA Ops:
  0.7 1.3 %constant_dynamic-slice_fusion = (f32[512,128]{1,0:T(8,128)S(1)}, f32[512,128]{1,0:T(8,128)S(1)}, f32[512,128]{1,0:T(8,128)S(1)}, f32[512,128]{1,0:T(8,128)S(1)}) fusion(f32[2048,128]{1,0:T(8,128)} %bitcast.2, s32[]{:T(128)S(6)} %select_n.75, s32[]{:T(128)S(6)} %select_n.74, s32[]{:T(128)S(6)} %select_n.70, s32[]{:T(128)S(6)} %select_n.69), kind=kLoop, calls=%fused_computation.60 | loop fusion | bytes 2097168 | tf_op jit(solution)/shard_map/dynamic_slice | solution.py:496
  1.9 5.1 %collective-permute-start.4 = (f32[512,128]{1,0:T(8,128)S(1)}, f32[512,128]{1,0:T(8,128)S(1)}, u32[]{:S(2)}, u32[]{:S(2)}) collective-permute-start(f32[512,128]{1,0:T(8,128)S(1)} %get-tuple-element.37), channel_id=1, source_target_pairs={{12,0},{13,1},{10,2},{11,3},{8,4},{9,5},{14,6},{15,7},{4,8},{5,9},... | collective-permute-start | bytes 786440 | tf_op jit(solution)/shard_map/ppermute | solution.py:490
  7.1 0.9 %collective-permute-start = (f32[512,128]{1,0:T(8,128)S(1)}, f32[512,128]{1,0:T(8,128)S(1)}, u32[]{:S(2)}, u32[]{:S(2)}) collective-permute-start(f32[512,128]{1,0:T(8,128)S(1)} %get-tuple-element.39), channel_id=1, source_target_pairs={{12,0},{13,1},{10,2},{11,3},{8,4},{9,5},{14,6},{15,7},{4,8},{5,9},... | collective-permute-start | bytes 786440 | tf_op jit(solution)/shard_map/ppermute | solution.py:490
  8.0 1.1 %collective-permute-start.1 = (f32[512,128]{1,0:T(8,128)S(1)}, f32[512,128]{1,0:T(8,128)S(1)}, u32[]{:S(2)}, u32[]{:S(2)}) collective-permute-start(f32[512,128]{1,0:T(8,128)S(1)} %get-tuple-element.38), channel_id=1, source_target_pairs={{4,0},{5,1},{6,2},{7,3},{0,4},{1,5},{2,6},{3,7},{12,8},{13,9},{14,... | collective-permute-start | bytes 786440 | tf_op jit(solution)/shard_map/ppermute | solution.py:490
  9.4 0.9 %sine_add_fusion.1 = (f32[64,64]{1,0:T(8,128)}, f32[64,64]{1,0:T(8,128)}) fusion(s32[64]{0:T(128)S(1)} %mul.133), kind=kLoop, calls=%fused_computation.34 | loop fusion | flops 122880 | bytes 33024 | tf_op jit(solution)/shard_map/add | solution.py:36
  10.4 0.8 %mul.149.paired = f32[128,128]{1,0:T(8,128)} reshape(f32[2,64,2,64]{3,2,1,0:T(2,128)S(1)} %broadcast_multiply_fusion) | data formatting | bytes 131072 | tf_op jit(solution)/shard_map/jit(kron)/mul | solution.py:547
  11.2 1.4 %seat.1 = (s32[13]{0:T(128)}, f32[10]{0:T(128)}) custom-call(s32[4]{0:T(128)} %offsets.1), custom_call_target="tpu_custom_call" | custom-call | tf_op jit(solution)/shard_map/seat/pallas_call | solution.py:373
  12.6 1.6 %weights.1 = (bf16[64,192]{1,0:T(8,128)(2,1)}, bf16[64,192]{1,0:T(8,128)(2,1)}, bf16[256,256]{1,0:T(8,128)(2,1)}) custom-call(f32[64,64]{1,0:T(8,128)} %get-tuple-element.41.forward, f32[64,64]{1,0:T(8,128)} %get-tuple-element.40.backward, f32[128,128]{1,0:T(8,128)} %mul.149.paired), custom_call_target="tpu_custom_call" | custom-call | tf_op jit(solution)/shard_map/weights/pallas_call | solution.py:128
  14.3 11.4 %collective-permute-done.refs_0_ = f32[512,128]{1,0:T(8,128)S(1)} collective-permute-done((f32[512,128]{1,0:T(8,128)S(1)}, f32[512,128]{1,0:T(8,128)S(1)}, u32[]{:S(2)}, u32[]{:S(2)}) %collective-permute-start) | collective-permute-done | bytes 262176 | tf_op jit(solution)/shard_map/ppermute | solution.py:490
  25.6 4.7 %collective-permute-done.1.refs_1_ = f32[512,128]{1,0:T(8,128)S(1)} collective-permute-done((f32[512,128]{1,0:T(8,128)S(1)}, f32[512,128]{1,0:T(8,128)S(1)}, u32[]{:S(2)}, u32[]{:S(2)}) %collective-permute-start.1) | collective-permute-done | bytes 262176 | tf_op jit(solution)/shard_map/ppermute | solution.py:490
  30.9 1.7 %multiply_select_fusion.refs_4_ = f32[2048,128]{1,0:T(8,128)S(1)} fusion(s32[128]{0:T(128)S(1)} %get-tuple-element.51, s32[128]{0:T(128)S(1)} %get-tuple-element.52, s32[128]{0:T(128)S(1)} %get-tuple-element.50, s32[128]{0:T(128)S(1)} %get-tuple-element.53, s32[2048]{0:T(1024)S(1)} %get-tuple-element.44, s32[2048]{0:T(1024)S(1)} %get-tuple-element.47, ...), kind=kLoop, calls=%fused_computation.11 | loop fusion | flops 8126464 | bytes 1087744 | tf_op jit(solution)/shard_map/jit(_where)/select_n | solution.py:59
  32.7 1.0 %shard_map.42 = (f32[520,128]{1,0:T(8,128)S(1)}, f32[512,128]{1,0:T(8,128)S(1)}) custom-call(s32[13]{0:T(128)S(1)} %copy-done.4, f32[10]{0:T(128)S(1)} %copy-done.5, f32[2048,128]{1,0:T(8,128)S(1)} %bitcast.3, f32[512,128]{1,0:T(8,128)S(1)} %collective-permute-done.4.refs_0_.refs_3_, f32[512,128]{1,0:T(8,128)S(1)} %collective-permute-done.5.refs_1_, ...), custom_call_target="tpu_custom_call" | custom-call | flops 16777216 | bytes 1048576 | tf_op jit(solution)/shard_map/pallas_call | solution.py:240
  33.8 1.1 %shard_map.41 = (f32[1040,128]{1,0:T(8,128)S(1)}, f32[1024,128]{1,0:T(8,128)S(1)}) custom-call(s32[13]{0:T(128)S(1)} %copy-done.4, f32[10]{0:T(128)S(1)} %copy-done.5, f32[2048,128]{1,0:T(8,128)S(1)} %bitcast.4, f32[512,128]{1,0:T(8,128)S(1)} %collective-permute-done.refs_0_, f32[512,128]{1,0:T(8,128)S(1)} %collective-permute-done.1.refs_1_, ...), custom_call_target="tpu_custom_call" | custom-call | flops 33554432 | bytes 2097152 | tf_op jit(solution)/shard_map/pallas_call | solution.py:240
  34.9 2.0 %shard_map.43 = (f32[2080,128]{1,0:T(8,128)S(1)}, f32[512,128]{1,0:T(8,128)S(1)}) custom-call(s32[13]{0:T(128)S(1)} %copy-done.4, f32[10]{0:T(128)S(1)} %copy-done.5, f32[2048,128]{1,0:T(8,128)S(1)} %bitcast.5, f32[1040,128]{1,0:T(8,128)S(1)} %get-tuple-element.23.refs_0_, f32[520,128]{1,0:T(8,128)S(1)} %get-tuple-element.24.refs_1_, ...), custom_call_target="tpu_custom_call" | custom-call | flops 167772160 | bytes 6291456 | tf_op jit(solution)/shard_map/pallas_call | solution.py:250
  37.0 1.1 %terms.3 = (f32[512,128]{1,0:T(8,128)S(1)}, f32[512,128]{1,0:T(8,128)S(1)}) custom-call(s32[13]{0:T(128)S(1)} %copy-done.4, f32[2080,128]{1,0:T(8,128)S(1)} %get-tuple-element.26.spectral, f32[1024,128]{1,0:T(8,128)S(1)} %get-tuple-element.27.refs_0_, f32[512,128]{1,0:T(8,128)S(1)} %get-tuple-element.28.refs_1_, f32[512,128]{1,0:T(8,128)S(1)} %get-tuple-element.29.refs_2_, ...), custom_call_target="tpu_custom_call" | custom-call | flops 100663296 | bytes 2097152 | tf_op jit(solution)/shard_map/terms/pallas_call | solution.py:295
  39.3 1.3 %collective-permute-start.12 = (f32[512,128]{1,0:T(8,128)S(1)}, f32[512,128]{1,0:T(8,128)S(1)}, u32[]{:S(2)}, u32[]{:S(2)}) collective-permute-start(f32[512,128]{1,0:T(8,128)S(1)} %collective-permute-done.4.refs_0_.refs_3_), channel_id=1, source_target_pairs={{0,2},{1,3},{2,0},{3,1},{4,6},{5,7},{6,4},{7,5},{8,10},{9,11},{10,... | collective-permute-start | bytes 786440 | tf_op jit(solution)/shard_map/ppermute | solution.py:493
  40.6 1.1 %terms.2 = (f32[512,128]{1,0:T(8,128)S(1)}, f32[512,128]{1,0:T(8,128)S(1)}) custom-call(s32[13]{0:T(128)S(1)} %copy-done.4, f32[2080,128]{1,0:T(8,128)S(1)} %get-tuple-element.26.spectral, f32[1024,128]{1,0:T(8,128)S(1)} %get-tuple-element.27.refs_0_, f32[512,128]{1,0:T(8,128)S(1)} %get-tuple-element.28.refs_1_, f32[512,128]{1,0:T(8,128)S(1)} %get-tuple-element.29.refs_2_, ...), custom_call_target="tpu_custom_call" | custom-call | flops 100663296 | bytes 2097152 | tf_op jit(solution)/shard_map/terms/pallas_call | solution.py:295
  42.4 0.8 %collective-permute-start.10 = (f32[512,128]{1,0:T(8,128)S(1)}, f32[512,128]{1,0:T(8,128)S(1)}, u32[]{:S(2)}, u32[]{:S(2)}) collective-permute-start(f32[512,128]{1,0:T(8,128)S(1)} %shard_map.45), channel_id=1, source_target_pairs={{0,2},{1,3},{2,0},{3,1},{4,6},{5,7},{6,4},{7,5},{8,10},{9,11},{10,... | collective-permute-start | bytes 786440 | tf_op jit(solution)/shard_map/ppermute | solution.py:493
  43.1 4.6 %collective-permute-done.11.refs_2_ = f32[512,128]{1,0:T(8,128)S(1)} collective-permute-done((f32[512,128]{1,0:T(8,128)S(1)}, f32[512,128]{1,0:T(8,128)S(1)}, u32[]{:S(2)}, u32[]{:S(2)}) %collective-permute-start.11) | collective-permute-done | bytes 262176 | tf_op jit(solution)/shard_map/ppermute | solution.py:493
  47.8 5.6 %collective-permute-done.12.refs_5_ = f32[512,128]{1,0:T(8,128)S(1)} collective-permute-done((f32[512,128]{1,0:T(8,128)S(1)}, f32[512,128]{1,0:T(8,128)S(1)}, u32[]{:S(2)}, u32[]{:S(2)}) %collective-permute-start.12) | collective-permute-done | bytes 262176 | tf_op jit(solution)/shard_map/ppermute | solution.py:493
  53.4 1.1 %shard_map.46 = f32[8,128]{1,0:T(8,128)S(1)} custom-call(s32[13]{0:T(128)S(1)} %copy-done.4, f32[10]{0:T(128)S(1)} %copy-done.5, f32[512,128]{1,0:T(8,128)S(1)} %get-tuple-element.32.kept.far, f32[512,128]{1,0:T(8,128)S(1)} %collective-permute-done.9.met.met_far, f32[512,128]{1,0:T(8,128)S(1)} %get-tuple-element.30.kept.near, ...), custom_call_target="tpu_custom_call" | custom-call | flops 2097152 | bytes 3145728 | tf_op jit(solution)/shard_map/pallas_call | solution.py:425
  54.6 1.2 %collective-permute-done.13 = f32[8,128]{1,0:T(8,128)S(1)} collective-permute-done((f32[8,128]{1,0:T(8,128)S(1)}, f32[8,128]{1,0:T(8,128)S(1)}, u32[]{:S(2)}, u32[]{:S(2)}) %collective-permute-start.13) | collective-permute-done | bytes 4128 | tf_op jit(solution)/shard_map/ppermute | solution.py:493
  57.1 2.3 %collective-permute-done.14.other = f32[8,128]{1,0:T(8,128)S(1)} collective-permute-done((f32[8,128]{1,0:T(8,128)S(1)}, f32[8,128]{1,0:T(8,128)S(1)}, u32[]{:S(2)}, u32[]{:S(2)}) %collective-permute-start.14) | collective-permute-done | bytes 4128 | tf_op jit(solution)/shard_map/ppermute | solution.py:493
  59.4 0.7 %finish.1 = (f32[512,128]{1,0:T(8,128)}, f32[1,4]{1,0:T(1,128)}) custom-call(f32[512,128]{1,0:T(8,128)S(1)} %shard_map.44.near_sum, f32[512,128]{1,0:T(8,128)S(1)} %collective-permute-done.10.arrived, f32[8,128]{1,0:T(8,128)S(1)} %add.107.row, f32[8,128]{1,0:T(8,128)S(1)} %collective-permute-done.14.other), custom_call_target="tpu_custom_call" | custom-call | flops 65536 | bytes 786432 | tf_op jit(solution)/shard_map/finish/pallas_call | solution.py:322
  (45 shorter events, 4.2 us)
Async XLA Ops:
  1.9 30.7 %copy-start = (f32[1,262144]{1,0:T(1,128)S(1)}, f32[1,262144]{1,0:T(1,128)}, u32[]{:S(2)}) copy-start(f32[1,262144]{1,0:T(1,128)} %param.2) | copy-start | bytes 3145732
  1.9 28.4 %collective-permute-start.4 = (f32[512,128]{1,0:T(8,128)S(1)}, f32[512,128]{1,0:T(8,128)S(1)}, u32[]{:S(2)}, u32[]{:S(2)}) collective-permute-start(f32[512,128]{1,0:T(8,128)S(1)} %get-tuple-element.37), channel_id=1, source_target_pairs={{12,0},{13,1},{10,2},{11,3},{8,4},{9,5},{14,6},{15,7},{4,8},{5,9},... | collective-permute-start | bytes 786440 | tf_op jit(solution)/shard_map/ppermute | solution.py:490
  7.1 23.8 %collective-permute-start.5 = (f32[512,128]{1,0:T(8,128)S(1)}, f32[512,128]{1,0:T(8,128)S(1)}, u32[]{:S(2)}, u32[]{:S(2)}) collective-permute-start(f32[512,128]{1,0:T(8,128)S(1)} %get-tuple-element.36), channel_id=1, source_target_pairs={{4,0},{5,1},{6,2},{7,3},{0,4},{1,5},{2,6},{3,7},{12,8},{13,9},{14,... | collective-permute-start | bytes 786440 | tf_op jit(solution)/shard_map/ppermute | solution.py:490
  7.1 18.5 %collective-permute-start = (f32[512,128]{1,0:T(8,128)S(1)}, f32[512,128]{1,0:T(8,128)S(1)}, u32[]{:S(2)}, u32[]{:S(2)}) collective-permute-start(f32[512,128]{1,0:T(8,128)S(1)} %get-tuple-element.39), channel_id=1, source_target_pairs={{12,0},{13,1},{10,2},{11,3},{8,4},{9,5},{14,6},{15,7},{4,8},{5,9},... | collective-permute-start | bytes 786440 | tf_op jit(solution)/shard_map/ppermute | solution.py:490
  8.0 22.4 %collective-permute-start.1 = (f32[512,128]{1,0:T(8,128)S(1)}, f32[512,128]{1,0:T(8,128)S(1)}, u32[]{:S(2)}, u32[]{:S(2)}) collective-permute-start(f32[512,128]{1,0:T(8,128)S(1)} %get-tuple-element.38), channel_id=1, source_target_pairs={{4,0},{5,1},{6,2},{7,3},{0,4},{1,5},{2,6},{3,7},{12,8},{13,9},{14,... | collective-permute-start | bytes 786440 | tf_op jit(solution)/shard_map/ppermute | solution.py:490
  12.6 20.1 %copy-start.4 = (s32[13]{0:T(128)S(1)}, s32[13]{0:T(128)}, u32[]{:S(2)}) copy-start(s32[13]{0:T(128)} %get-tuple-element.20.places) | copy-start | bytes 160
  12.6 20.1 %copy-start.5 = (f32[10]{0:T(128)S(1)}, f32[10]{0:T(128)}, u32[]{:S(2)}) copy-start(f32[10]{0:T(128)} %get-tuple-element.19.factors) | copy-start | bytes 124
  14.2 18.4 %copy-start.1 = (bf16[256,256]{1,0:T(8,128)(2,1)S(1)}, bf16[256,256]{1,0:T(8,128)(2,1)}, u32[]{:S(2)}) copy-start(bf16[256,256]{1,0:T(8,128)(2,1)} %get-tuple-element.22.refs_5_.refs_3_.refs_7_.refs_4_) | copy-start | bytes 393220
  14.2 18.4 %copy-start.3 = (bf16[64,192]{1,0:T(8,128)(2,1)S(1)}, bf16[64,192]{1,0:T(8,128)(2,1)}, u32[]{:S(2)}) copy-start(bf16[64,192]{1,0:T(8,128)(2,1)} %get-tuple-element.21.refs_4_.refs_2_.refs_5_) | copy-start | bytes 73732
  25.6 8.1 %collective-permute-start.2 = (f32[512,128]{1,0:T(8,128)S(1)}, f32[512,128]{1,0:T(8,128)S(1)}, u32[]{:S(2)}, u32[]{:S(2)}) collective-permute-start(f32[512,128]{1,0:T(8,128)S(1)} %collective-permute-done.refs_0_), channel_id=1, source_target_pairs={{0,1},{1,0},{2,3},{3,2},{4,5},{5,4},{6,7},{7,6},{8,9},{9,8},{10,11... | collective-permute-start | bytes 786440 | tf_op jit(solution)/shard_map/ppermute | solution.py:493
  30.3 3.4 %collective-permute-start.3 = (f32[512,128]{1,0:T(8,128)S(1)}, f32[512,128]{1,0:T(8,128)S(1)}, u32[]{:S(2)}, u32[]{:S(2)}) collective-permute-start(f32[512,128]{1,0:T(8,128)S(1)} %collective-permute-done.1.refs_1_), channel_id=1, source_target_pairs={{0,1},{1,0},{2,3},{3,2},{4,5},{5,4},{6,7},{7,6},{8,9},{9,8},{10,11... | collective-permute-start | bytes 786440 | tf_op jit(solution)/shard_map/ppermute | solution.py:493
  30.4 4.5 %collective-permute-start.6 = (f32[512,128]{1,0:T(8,128)S(1)}, f32[512,128]{1,0:T(8,128)S(1)}, u32[]{:S(2)}, u32[]{:S(2)}) collective-permute-start(f32[512,128]{1,0:T(8,128)S(1)} %collective-permute-done.4.refs_0_.refs_3_), channel_id=1, source_target_pairs={{0,1},{1,0},{2,3},{3,2},{4,5},{5,4},{6,7},{7,6},{8,9},{9,8},{10,11... | collective-permute-start | bytes 786440 | tf_op jit(solution)/shard_map/ppermute | solution.py:493
  30.9 4.1 %collective-permute-start.7 = (f32[512,128]{1,0:T(8,128)S(1)}, f32[512,128]{1,0:T(8,128)S(1)}, u32[]{:S(2)}, u32[]{:S(2)}) collective-permute-start(f32[512,128]{1,0:T(8,128)S(1)} %collective-permute-done.5.refs_1_), channel_id=1, source_target_pairs={{0,1},{1,0},{2,3},{3,2},{4,5},{5,4},{6,7},{7,6},{8,9},{9,8},{10,11... | collective-permute-start | bytes 786440 | tf_op jit(solution)/shard_map/ppermute | solution.py:493
  33.7 1.2 %copy-start.2 = (bf16[64,192]{1,0:T(8,128)(2,1)S(1)}, bf16[64,192]{1,0:T(8,128)(2,1)}, u32[]{:S(2)}) copy-start(bf16[64,192]{1,0:T(8,128)(2,1)} %get-tuple-element.25.refs_6_.refs_3_) | copy-start | bytes 73732
  38.1 3.7 %collective-permute-start.9 = (f32[512,128]{1,0:T(8,128)S(1)}, f32[512,128]{1,0:T(8,128)S(1)}, u32[]{:S(2)}, u32[]{:S(2)}) collective-permute-start(f32[512,128]{1,0:T(8,128)S(1)} %get-tuple-element.33), channel_id=1, source_target_pairs={{0,1},{1,0},{2,3},{3,2},{4,5},{5,4},{6,7},{7,6},{8,9},{9,8},{10,11... | collective-permute-start | bytes 786440 | tf_op jit(solution)/shard_map/ppermute | solution.py:493
  38.6 9.2 %collective-permute-start.11 = (f32[512,128]{1,0:T(8,128)S(1)}, f32[512,128]{1,0:T(8,128)S(1)}, u32[]{:S(2)}, u32[]{:S(2)}) collective-permute-start(f32[512,128]{1,0:T(8,128)S(1)} %collective-permute-done.refs_0_), channel_id=1, source_target_pairs={{0,2},{1,3},{2,0},{3,1},{4,6},{5,7},{6,4},{7,5},{8,10},{9,11},{10,... | collective-permute-start | bytes 786440 | tf_op jit(solution)/shard_map/ppermute | solution.py:493
  39.3 14.1 %collective-permute-start.12 = (f32[512,128]{1,0:T(8,128)S(1)}, f32[512,128]{1,0:T(8,128)S(1)}, u32[]{:S(2)}, u32[]{:S(2)}) collective-permute-start(f32[512,128]{1,0:T(8,128)S(1)} %collective-permute-done.4.refs_0_.refs_3_), channel_id=1, source_target_pairs={{0,2},{1,3},{2,0},{3,1},{4,6},{5,7},{6,4},{7,5},{8,10},{9,11},{10,... | collective-permute-start | bytes 786440 | tf_op jit(solution)/shard_map/ppermute | solution.py:493
  40.6 12.8 %collective-permute-start.8 = (f32[512,128]{1,0:T(8,128)S(1)}, f32[512,128]{1,0:T(8,128)S(1)}, u32[]{:S(2)}, u32[]{:S(2)}) collective-permute-start(f32[512,128]{1,0:T(8,128)S(1)} %get-tuple-element.31), channel_id=1, source_target_pairs={{0,1},{1,0},{2,3},{3,2},{4,5},{5,4},{6,7},{7,6},{8,9},{9,8},{10,11... | collective-permute-start | bytes 786440 | tf_op jit(solution)/shard_map/ppermute | solution.py:493
  42.4 17.0 %collective-permute-start.10 = (f32[512,128]{1,0:T(8,128)S(1)}, f32[512,128]{1,0:T(8,128)S(1)}, u32[]{:S(2)}, u32[]{:S(2)}) collective-permute-start(f32[512,128]{1,0:T(8,128)S(1)} %shard_map.45), channel_id=1, source_target_pairs={{0,2},{1,3},{2,0},{3,1},{4,6},{5,7},{6,4},{7,5},{8,10},{9,11},{10,... | collective-permute-start | bytes 786440 | tf_op jit(solution)/shard_map/ppermute | solution.py:493
  54.5 1.2 %collective-permute-start.13 = (f32[8,128]{1,0:T(8,128)S(1)}, f32[8,128]{1,0:T(8,128)S(1)}, u32[]{:S(2)}, u32[]{:S(2)}) collective-permute-start(f32[8,128]{1,0:T(8,128)S(1)} %shard_map.46), channel_id=1, source_target_pairs={{0,1},{1,0},{2,3},{3,2},{4,5},{5,4},{6,7},{7,6},{8,9},{9,8},{10,11... | collective-permute-start | bytes 12296 | tf_op jit(solution)/shard_map/ppermute | solution.py:493
  55.8 3.6 %collective-permute-start.14 = (f32[8,128]{1,0:T(8,128)S(1)}, f32[8,128]{1,0:T(8,128)S(1)}, u32[]{:S(2)}, u32[]{:S(2)}) collective-permute-start(f32[8,128]{1,0:T(8,128)S(1)} %add.107.row), channel_id=1, source_target_pairs={{0,2},{1,3},{2,0},{3,1},{4,6},{5,7},{6,4},{7,5},{8,10},{9,11},{10,... | collective-permute-start | bytes 12296 | tf_op jit(solution)/shard_map/ppermute | solution.py:493

commit v6 on v5

--- a/solution.py
+++ b/solution.py
@@ -182,9 +182,10 @@
     slabs_body(places, own, choices, left_y, lanes, along_z, out, partner, first_slab=first_slab)
 
 
-def spectrum_body(places, factors, own, *refs, heads, first_slab, count):
-    parts, choices, rest = refs[:heads], refs[heads : heads + 2 * count], refs[heads + 2 * count :]
-    kernel, left_y, left_back, lanes, out, partner, tail, along_z = rest
+def spectrum_body(places, factors, own, *refs, heads, first_slab, count, which):
+    parts, known, rest = refs[:heads], refs[heads : 2 * heads], refs[2 * heads :]
+    choices, rest = rest[: 2 * count], rest[2 * count :]
+    kernel, left_y, left_back, lanes, out, partner, *outs, tail, along_z, back_y = rest
     plane = NG // 2
     mask = low_mask(plane)
     slabs_body(places, own, choices, left_y, lanes, along_z, tail, partner, first_slab=first_slab)
@@ -215,16 +216,17 @@
         return 0
 
     lax.fori_loop(0, NG // 4, columns, 0, unroll=NG // 4)
-
-
-def planes_call(body, spaces, planes_rows, partner_rows, scratch_rows, flops, cells):
+    fill_terms(places, out, (*known, partner), left_back, lanes, outs, back_y, which)
+
+
+def planes_call(body, spaces, out_rows, scratch_rows, flops, cells):
     smem = pl.BlockSpec(memory_space=pltpu.SMEM)
     vmem = pl.BlockSpec(memory_space=pltpu.VMEM)
     return pl.pallas_call(
         body,
-        out_shape=[jax.ShapeDtypeStruct((rows, LANES), jnp.float32) for rows in (planes_rows, partner_rows)],
+        out_shape=[jax.ShapeDtypeStruct((rows, LANES), jnp.float32) for rows in out_rows],
         in_specs=[smem] * 2 + [vmem] * spaces,
-        out_specs=[vmem] * 2,
+        out_specs=[vmem] * len(out_rows),
         scratch_shapes=[pltpu.VMEM((rows, LANES), jnp.float32) for rows in scratch_rows],
         compiler_params=pltpu.CompilerParams(vmem_limit_bytes=24 << 20),
         cost_estimate=pl.CostEstimate(flops=flops, bytes_accessed=4 * cells, transcendentals=0),
@@ -238,22 +240,31 @@
     body = functools.partial(first_body, first_slab=first_slab, count=count)
     pitched = rows // NG * PITCH
     return planes_call(
-        body, 3 + 2 * count, pitched, rows, (rows,), rows * LANES * NG * 4, 4 * rows * LANES
+        body, 3 + 2 * count, (pitched, rows), (rows,), rows * LANES * NG * 4, 4 * rows * LANES
     )(places, factors, own, *choices, left_y, lanes)
 
 
-def spectrum(first_slab, places, factors, own, heads, choices, kernel, weights):
+def spectrum(first_slab, which, places, factors, own, heads, known, choices, kernel, weights):
     count = len(choices) // 2
-    rows, last = own.shape[0], count * choices[0].shape[0]
-    body = functools.partial(spectrum_body, heads=len(heads), first_slab=first_slab, count=count)
-    pitched = rows // NG * PITCH, last // NG * PITCH
+    rows, slab_rows = own.shape[0], choices[0].shape[0]
+    last = count * slab_rows
+    body = functools.partial(spectrum_body, heads=len(heads), first_slab=first_slab, count=count, which=which)
     return planes_call(
-        body, 5 + len(heads) + 2 * count, pitched[0], last, (pitched[1], last), rows * LANES * NG * 10, 6 * rows * LANES
-    )(places, factors, own, *heads, *choices, kernel, *weights)
+        body,
+        5 + 2 * len(heads) + 2 * count,
+        (rows // NG * PITCH, last) + (slab_rows,) * len(which),
+        (last // NG * PITCH, last, len(which) * slab_rows),
+        rows * LANES * NG * 16,
+        8 * rows * LANES,
+    )(places, factors, own, *heads, *known, *choices, kernel, *weights)
 
 
 def terms_body(places, spectral, *refs, which):
     partners, (left_back, lanes, *outs, back_y) = refs[: -3 - len(which)], refs[-3 - len(which) :]
+    fill_terms(places, spectral, partners, left_back, lanes, outs, back_y, which)
+
+
+def fill_terms(places, spectral, partners, left_back, lanes, outs, back_y, which):
     plane = NG // 2
     mask = low_mask(plane)
     w_backward = left_back[...]
@@ -457,11 +468,12 @@
         slabs = [visit[slab * slab_rows : (slab + 1) * slab_rows] for slab in range(SLABS)]
         choices = [slabs[index // 2] for index in range(2 * SLABS)]
         head, partner_a = first_planes(0, places, factors, own, choices[:4], weights)
-        spectral, partner_b = spectrum(2, places, factors, own, (head,), choices[4:], kernel, weights)
         numbers = jnp.arange(SLABS, dtype=jnp.int32)
         spots = places.at[FAR_SENT : FAR_SENT + SLABS].set(numbers)
         which = tuple(range(FAR_SENT, FAR_SENT + SLABS))
-        terms = exchange_terms(which, slab_rows, spots, spectral, (partner_a, partner_b), weights)
+        _, _, *terms = spectrum(
+            2, which, spots, factors, own, (head,), (partner_a,), choices[4:], kernel, weights
+        )
         whole = whole + jnp.concatenate(terms, axis=0)
     exchanged = lax.psum_scatter(whole.reshape(1, cells), "rep", scatter_dimension=1, tiled=True)
     quarter = lax.dynamic_slice_in_dim(orbitals, replica * (cells // replicas), cells // replicas, 1)
@@ -511,11 +523,19 @@
     near_b_last = replica_swap(b_last, 1)
     moved_last = replica_swap(a_last, 2)
     third, third_partner = first_planes(2, places, factors, own, (a_last, b_last), weights)
-    spectral, last_partner = spectrum(
-        3, places, factors, own, (head, third), (near_a_last, near_b_last), kernel, weights
+    spectral, last_partner, *sent = spectrum(
+        3,
+        (FAR_SENT, NEAR_SENT),
+        places,
+        factors,
+        own,
+        (head, third),
+        (partner, third_partner),
+        (near_a_last, near_b_last),
+        kernel,
+        weights,
     )
     partners = partner, third_partner, last_partner
-    sent = exchange_terms((FAR_SENT, NEAR_SENT), slab_rows, places, spectral, partners, weights)
     met_far = replica_swap(sent[0], 1)
     met_near = replica_swap(sent[1], 1)
     kept = exchange_terms((FAR_KEPT, NEAR_KEPT), slab_rows, places, spectral, partners, weights)

time: 60.3 us -> 59.8 us (level)
    pallas_call x2 -> x1, Pallas kernels: 2.24 us -> 1.12 us  [exchange_terms(): pl.pallas_call(functools.partial(terms_body, which=which), out_shape=[jax...]
where the time goes in v6:
time: 59.8 us; the launch traced here: 59.6 us
  waiting for transfers between devices  29.8 us (50%)
  starting transfers between devices  11.9 us (20%)
  Pallas kernels  11.9 us (20%)
  other arithmetic  2.92 us (5%)
  local copies, waits for them, and re-layouts  2.13 us (4%)
  between operations  0.91 us (2%)
    ppermute x4, waiting for transfers between devices, along_blocks(): return lax.ppermute(value, ('blk', 'rep'), route)  16.1 us
    ppermute x11, waiting for transfers between devices, replica_swap(): return lax.ppermute(value, 'rep', [(r, r ^ bit) for r in range(replicas)])  13.7 us
    ppermute x4, starting transfers between devices, along_blocks(): return lax.ppermute(value, ('blk', 'rep'), route)  7.17 us
    ppermute x11, starting transfers between devices, replica_swap(): return lax.ppermute(value, 'rep', [(r, r ^ bit) for r in range(replicas)])  4.69 us
    pallas_call x1, Pallas kernels, spectrum(): planes_call(body, 5 + 2 * len(heads) + 2 * count, (rows // NG * PITCH, la...  2.59 us
    pallas_call x2, Pallas kernels, first_planes(): planes_call(body, 3 + 2 * count, (pitched, rows), (rows,), rows * LANES *...  2.18 us
    select_n x1, other arithmetic, screened_kernel(): return jnp.where(k_squared > 0.5, screened, jnp.ones_like(screened))  1.7 us
    pallas_call x1, Pallas kernels, prepared_weights(): pl.pallas_call(weights_body, out_shape=[jax.ShapeDtypeStruct(shape, jnp.b...  1.62 us
  transfers between devices with their start and end apart: 15, of which 6 were waited for; matrix products, arithmetic and copies ran while one was open for 6% of the time, Pallas kernels for 14%

profile of v6, /device:TPU:0, one launch (start us, length us, event | category | flops | bytes accessed | tf_op | source)
XLA Modules:
  0.0 59.6 jit_solution(13637925426568928404)
XLA Ops:
  0.7 1.3 %constant_dynamic-slice_fusion = (f32[512,128]{1,0:T(8,128)S(1)}, f32[512,128]{1,0:T(8,128)S(1)}, f32[512,128]{1,0:T(8,128)S(1)}, f32[512,128]{1,0:T(8,128)S(1)}) fusion(f32[2048,128]{1,0:T(8,128)} %bitcast.2, s32[]{:T(128)S(6)} %select_n.75, s32[]{:T(128)S(6)} %select_n.74, s32[]{:T(128)S(6)} %select_n.70, s32[]{:T(128)S(6)} %select_n.69), kind=kLoop, calls=%fused_computation.60 | loop fusion | bytes 2097168 | tf_op jit(solution)/shard_map/dynamic_slice | solution.py:508
  1.9 5.1 %collective-permute-start.4 = (f32[512,128]{1,0:T(8,128)S(1)}, f32[512,128]{1,0:T(8,128)S(1)}, u32[]{:S(2)}, u32[]{:S(2)}) collective-permute-start(f32[512,128]{1,0:T(8,128)S(1)} %get-tuple-element.37), channel_id=1, source_target_pairs={{12,0},{13,1},{10,2},{11,3},{8,4},{9,5},{14,6},{15,7},{4,8},{5,9},... | collective-permute-start | bytes 786440 | tf_op jit(solution)/shard_map/ppermute | solution.py:502
  7.1 0.9 %collective-permute-start = (f32[512,128]{1,0:T(8,128)S(1)}, f32[512,128]{1,0:T(8,128)S(1)}, u32[]{:S(2)}, u32[]{:S(2)}) collective-permute-start(f32[512,128]{1,0:T(8,128)S(1)} %get-tuple-element.39), channel_id=1, source_target_pairs={{12,0},{13,1},{10,2},{11,3},{8,4},{9,5},{14,6},{15,7},{4,8},{5,9},... | collective-permute-start | bytes 786440 | tf_op jit(solution)/shard_map/ppermute | solution.py:502
  8.0 1.1 %collective-permute-start.1 = (f32[512,128]{1,0:T(8,128)S(1)}, f32[512,128]{1,0:T(8,128)S(1)}, u32[]{:S(2)}, u32[]{:S(2)}) collective-permute-start(f32[512,128]{1,0:T(8,128)S(1)} %get-tuple-element.38), channel_id=1, source_target_pairs={{4,0},{5,1},{6,2},{7,3},{0,4},{1,5},{2,6},{3,7},{12,8},{13,9},{14,... | collective-permute-start | bytes 786440 | tf_op jit(solution)/shard_map/ppermute | solution.py:502
  9.4 0.9 %sine_add_fusion.1 = (f32[64,64]{1,0:T(8,128)}, f32[64,64]{1,0:T(8,128)}) fusion(s32[64]{0:T(128)S(1)} %mul.133), kind=kLoop, calls=%fused_computation.34 | loop fusion | flops 122880 | bytes 33024 | tf_op jit(solution)/shard_map/add | solution.py:36
  10.4 0.7 %mul.149.paired = f32[128,128]{1,0:T(8,128)} reshape(f32[2,64,2,64]{3,2,1,0:T(2,128)S(1)} %broadcast_multiply_fusion) | data formatting | bytes 131072 | tf_op jit(solution)/shard_map/jit(kron)/mul | solution.py:567
  11.2 1.4 %seat.1 = (s32[13]{0:T(128)}, f32[10]{0:T(128)}) custom-call(s32[4]{0:T(128)} %offsets.1), custom_call_target="tpu_custom_call" | custom-call | tf_op jit(solution)/shard_map/seat/pallas_call | solution.py:384
  12.6 1.6 %weights.1 = (bf16[64,192]{1,0:T(8,128)(2,1)}, bf16[64,192]{1,0:T(8,128)(2,1)}, bf16[256,256]{1,0:T(8,128)(2,1)}) custom-call(f32[64,64]{1,0:T(8,128)} %get-tuple-element.41.forward, f32[64,64]{1,0:T(8,128)} %get-tuple-element.40.backward, f32[128,128]{1,0:T(8,128)} %mul.149.paired), custom_call_target="tpu_custom_call" | custom-call | tf_op jit(solution)/shard_map/weights/pallas_call | solution.py:128
  14.2 11.4 %collective-permute-done.refs_0_ = f32[512,128]{1,0:T(8,128)S(1)} collective-permute-done((f32[512,128]{1,0:T(8,128)S(1)}, f32[512,128]{1,0:T(8,128)S(1)}, u32[]{:S(2)}, u32[]{:S(2)}) %collective-permute-start) | collective-permute-done | bytes 262176 | tf_op jit(solution)/shard_map/ppermute | solution.py:502
  25.6 4.7 %collective-permute-done.1.refs_1_ = f32[512,128]{1,0:T(8,128)S(1)} collective-permute-done((f32[512,128]{1,0:T(8,128)S(1)}, f32[512,128]{1,0:T(8,128)S(1)}, u32[]{:S(2)}, u32[]{:S(2)}) %collective-permute-start.1) | collective-permute-done | bytes 262176 | tf_op jit(solution)/shard_map/ppermute | solution.py:502
  30.9 1.7 %multiply_select_fusion.refs_6_ = f32[2048,128]{1,0:T(8,128)S(1)} fusion(s32[128]{0:T(128)S(1)} %get-tuple-element.51, s32[128]{0:T(128)S(1)} %get-tuple-element.52, s32[128]{0:T(128)S(1)} %get-tuple-element.50, s32[128]{0:T(128)S(1)} %get-tuple-element.53, s32[2048]{0:T(1024)S(1)} %get-tuple-element.44, s32[2048]{0:T(1024)S(1)} %get-tuple-element.47, ...), kind=kLoop, calls=%fused_computation.11 | loop fusion | flops 8126464 | bytes 1087744 | tf_op jit(solution)/shard_map/jit(_where)/select_n | solution.py:59
  32.7 1.0 %shard_map.42 = (f32[520,128]{1,0:T(8,128)S(1)}, f32[512,128]{1,0:T(8,128)S(1)}) custom-call(s32[13]{0:T(128)S(1)} %copy-done.5, f32[10]{0:T(128)S(1)} %copy-done.4, f32[2048,128]{1,0:T(8,128)S(1)} %bitcast.3, f32[512,128]{1,0:T(8,128)S(1)} %collective-permute-done.4.refs_0_.refs_3_, f32[512,128]{1,0:T(8,128)S(1)} %collective-permute-done.5.refs_1_, ...), custom_call_target="tpu_custom_call" | custom-call | flops 16777216 | bytes 1048576 | tf_op jit(solution)/shard_map/pallas_call | solution.py:242
  33.8 1.1 %shard_map.41 = (f32[1040,128]{1,0:T(8,128)S(1)}, f32[1024,128]{1,0:T(8,128)S(1)}) custom-call(s32[13]{0:T(128)S(1)} %copy-done.5, f32[10]{0:T(128)S(1)} %copy-done.4, f32[2048,128]{1,0:T(8,128)S(1)} %bitcast.4, f32[512,128]{1,0:T(8,128)S(1)} %collective-permute-done.refs_0_, f32[512,128]{1,0:T(8,128)S(1)} %collective-permute-done.1.refs_1_, ...), custom_call_target="tpu_custom_call" | custom-call | flops 33554432 | bytes 2097152 | tf_op jit(solution)/shard_map/pallas_call | solution.py:242
  34.9 2.6 %shard_map.43 = (f32[2080,128]{1,0:T(8,128)S(1)}, f32[512,128]{1,0:T(8,128)S(1)}, f32[512,128]{1,0:T(8,128)S(1)}, f32[512,128]{1,0:T(8,128)S(1)}) custom-call(s32[13]{0:T(128)S(1)} %copy-done.5, f32[10]{0:T(128)S(1)} %copy-done.4, f32[2048,128]{1,0:T(8,128)S(1)} %bitcast.5, f32[1040,128]{1,0:T(8,128)S(1)} %get-tuple-element.23.refs_0_, ...), custom_call_target="tpu_custom_call" | custom-call | flops 268435456 | bytes 8388608 | tf_op jit(solution)/shard_map/pallas_call | solution.py:252
  38.1 0.7 %collective-permute-start.11 = (f32[512,128]{1,0:T(8,128)S(1)}, f32[512,128]{1,0:T(8,128)S(1)}, u32[]{:S(2)}, u32[]{:S(2)}) collective-permute-start(f32[512,128]{1,0:T(8,128)S(1)} %collective-permute-done.refs_0_), channel_id=1, source_target_pairs={{0,2},{1,3},{2,0},{3,1},{4,6},{5,7},{6,4},{7,5},{8,10},{9,11},{10,... | collective-permute-start | bytes 786440 | tf_op jit(solution)/shard_map/ppermute | solution.py:505
  38.8 1.3 %collective-permute-start.12 = (f32[512,128]{1,0:T(8,128)S(1)}, f32[512,128]{1,0:T(8,128)S(1)}, u32[]{:S(2)}, u32[]{:S(2)}) collective-permute-start(f32[512,128]{1,0:T(8,128)S(1)} %collective-permute-done.4.refs_0_.refs_3_), channel_id=1, source_target_pairs={{0,2},{1,3},{2,0},{3,1},{4,6},{5,7},{6,4},{7,5},{8,10},{9,11},{10,... | collective-permute-start | bytes 786440 | tf_op jit(solution)/shard_map/ppermute | solution.py:505
  40.1 1.1 %terms.1 = (f32[512,128]{1,0:T(8,128)S(1)}, f32[512,128]{1,0:T(8,128)S(1)}) custom-call(s32[13]{0:T(128)S(1)} %copy-done.5, f32[2080,128]{1,0:T(8,128)S(1)} %get-tuple-element.28.spectral, f32[1024,128]{1,0:T(8,128)S(1)} %get-tuple-element.25.refs_2_.refs_0_, f32[512,128]{1,0:T(8,128)S(1)} %get-tuple-element.26.refs_3_.refs_1_, ...), custom_call_target="tpu_custom_call" | custom-call | flops 100663296 | bytes 2097152 | tf_op jit(solution)/shard_map/terms/pallas_call | solution.py:306
  41.8 0.8 %collective-permute-start.10 = (f32[512,128]{1,0:T(8,128)S(1)}, f32[512,128]{1,0:T(8,128)S(1)}, u32[]{:S(2)}, u32[]{:S(2)}) collective-permute-start(f32[512,128]{1,0:T(8,128)S(1)} %shard_map.45), channel_id=1, source_target_pairs={{0,2},{1,3},{2,0},{3,1},{4,6},{5,7},{6,4},{7,5},{8,10},{9,11},{10,... | collective-permute-start | bytes 786440 | tf_op jit(solution)/shard_map/ppermute | solution.py:505
  42.6 4.6 %collective-permute-done.11.refs_2_ = f32[512,128]{1,0:T(8,128)S(1)} collective-permute-done((f32[512,128]{1,0:T(8,128)S(1)}, f32[512,128]{1,0:T(8,128)S(1)}, u32[]{:S(2)}, u32[]{:S(2)}) %collective-permute-start.11) | collective-permute-done | bytes 262176 | tf_op jit(solution)/shard_map/ppermute | solution.py:505
  47.2 5.6 %collective-permute-done.12.refs_5_ = f32[512,128]{1,0:T(8,128)S(1)} collective-permute-done((f32[512,128]{1,0:T(8,128)S(1)}, f32[512,128]{1,0:T(8,128)S(1)}, u32[]{:S(2)}, u32[]{:S(2)}) %collective-permute-start.12) | collective-permute-done | bytes 262176 | tf_op jit(solution)/shard_map/ppermute | solution.py:505
  52.9 1.1 %shard_map.46 = f32[8,128]{1,0:T(8,128)S(1)} custom-call(s32[13]{0:T(128)S(1)} %copy-done.5, f32[10]{0:T(128)S(1)} %copy-done.4, f32[512,128]{1,0:T(8,128)S(1)} %get-tuple-element.32.kept.far, f32[512,128]{1,0:T(8,128)S(1)} %collective-permute-done.9.met.met_far, f32[512,128]{1,0:T(8,128)S(1)} %get-tuple-element.30.kept.near, ...), custom_call_target="tpu_custom_call" | custom-call | flops 2097152 | bytes 3145728 | tf_op jit(solution)/shard_map/pallas_call | solution.py:436
  54.1 1.2 %collective-permute-done.13 = f32[8,128]{1,0:T(8,128)S(1)} collective-permute-done((f32[8,128]{1,0:T(8,128)S(1)}, f32[8,128]{1,0:T(8,128)S(1)}, u32[]{:S(2)}, u32[]{:S(2)}) %collective-permute-start.13) | collective-permute-done | bytes 4128 | tf_op jit(solution)/shard_map/ppermute | solution.py:505
  56.5 2.3 %collective-permute-done.14.other = f32[8,128]{1,0:T(8,128)S(1)} collective-permute-done((f32[8,128]{1,0:T(8,128)S(1)}, f32[8,128]{1,0:T(8,128)S(1)}, u32[]{:S(2)}, u32[]{:S(2)}) %collective-permute-start.14) | collective-permute-done | bytes 4128 | tf_op jit(solution)/shard_map/ppermute | solution.py:505
  58.8 0.7 %finish.1 = (f32[512,128]{1,0:T(8,128)}, f32[1,4]{1,0:T(1,128)}) custom-call(f32[512,128]{1,0:T(8,128)S(1)} %shard_map.44.near_sum, f32[512,128]{1,0:T(8,128)S(1)} %collective-permute-done.10.arrived, f32[8,128]{1,0:T(8,128)S(1)} %add.107.row, f32[8,128]{1,0:T(8,128)S(1)} %collective-permute-done.14.other), custom_call_target="tpu_custom_call" | custom-call | flops 65536 | bytes 786432 | tf_op jit(solution)/shard_map/finish/pallas_call | solution.py:333
  (44 shorter events, 3.5 us)
Async XLA Ops:
  1.9 30.7 %copy-start = (f32[1,262144]{1,0:T(1,128)S(1)}, f32[1,262144]{1,0:T(1,128)}, u32[]{:S(2)}) copy-start(f32[1,262144]{1,0:T(1,128)} %param.2) | copy-start | bytes 3145732
  1.9 28.4 %collective-permute-start.4 = (f32[512,128]{1,0:T(8,128)S(1)}, f32[512,128]{1,0:T(8,128)S(1)}, u32[]{:S(2)}, u32[]{:S(2)}) collective-permute-start(f32[512,128]{1,0:T(8,128)S(1)} %get-tuple-element.37), channel_id=1, source_target_pairs={{12,0},{13,1},{10,2},{11,3},{8,4},{9,5},{14,6},{15,7},{4,8},{5,9},... | collective-permute-start | bytes 786440 | tf_op jit(solution)/shard_map/ppermute | solution.py:502
  7.1 23.8 %collective-permute-start.5 = (f32[512,128]{1,0:T(8,128)S(1)}, f32[512,128]{1,0:T(8,128)S(1)}, u32[]{:S(2)}, u32[]{:S(2)}) collective-permute-start(f32[512,128]{1,0:T(8,128)S(1)} %get-tuple-element.36), channel_id=1, source_target_pairs={{4,0},{5,1},{6,2},{7,3},{0,4},{1,5},{2,6},{3,7},{12,8},{13,9},{14,... | collective-permute-start | bytes 786440 | tf_op jit(solution)/shard_map/ppermute | solution.py:502
  7.1 18.5 %collective-permute-start = (f32[512,128]{1,0:T(8,128)S(1)}, f32[512,128]{1,0:T(8,128)S(1)}, u32[]{:S(2)}, u32[]{:S(2)}) collective-permute-start(f32[512,128]{1,0:T(8,128)S(1)} %get-tuple-element.39), channel_id=1, source_target_pairs={{12,0},{13,1},{10,2},{11,3},{8,4},{9,5},{14,6},{15,7},{4,8},{5,9},... | collective-permute-start | bytes 786440 | tf_op jit(solution)/shard_map/ppermute | solution.py:502
  8.0 22.4 %collective-permute-start.1 = (f32[512,128]{1,0:T(8,128)S(1)}, f32[512,128]{1,0:T(8,128)S(1)}, u32[]{:S(2)}, u32[]{:S(2)}) collective-permute-start(f32[512,128]{1,0:T(8,128)S(1)} %get-tuple-element.38), channel_id=1, source_target_pairs={{4,0},{5,1},{6,2},{7,3},{0,4},{1,5},{2,6},{3,7},{12,8},{13,9},{14,... | collective-permute-start | bytes 786440 | tf_op jit(solution)/shard_map/ppermute | solution.py:502
  12.6 20.1 %copy-start.4 = (f32[10]{0:T(128)S(1)}, f32[10]{0:T(128)}, u32[]{:S(2)}) copy-start(f32[10]{0:T(128)} %get-tuple-element.19.factors) | copy-start | bytes 124
  12.6 20.1 %copy-start.5 = (s32[13]{0:T(128)S(1)}, s32[13]{0:T(128)}, u32[]{:S(2)}) copy-start(s32[13]{0:T(128)} %get-tuple-element.20.places) | copy-start | bytes 160
  14.2 18.5 %copy-start.1 = (bf16[256,256]{1,0:T(8,128)(2,1)S(1)}, bf16[256,256]{1,0:T(8,128)(2,1)}, u32[]{:S(2)}) copy-start(bf16[256,256]{1,0:T(8,128)(2,1)} %get-tuple-element.22.refs_5_.refs_3_.refs_9_.refs_4_) | copy-start | bytes 393220
  14.2 18.5 %copy-start.2 = (bf16[64,192]{1,0:T(8,128)(2,1)S(1)}, bf16[64,192]{1,0:T(8,128)(2,1)}, u32[]{:S(2)}) copy-start(bf16[64,192]{1,0:T(8,128)(2,1)} %get-tuple-element.21.refs_4_.refs_2_.refs_7_) | copy-start | bytes 73732
  25.6 8.1 %collective-permute-start.2 = (f32[512,128]{1,0:T(8,128)S(1)}, f32[512,128]{1,0:T(8,128)S(1)}, u32[]{:S(2)}, u32[]{:S(2)}) collective-permute-start(f32[512,128]{1,0:T(8,128)S(1)} %collective-permute-done.refs_0_), channel_id=1, source_target_pairs={{0,1},{1,0},{2,3},{3,2},{4,5},{5,4},{6,7},{7,6},{8,9},{9,8},{10,11... | collective-permute-start | bytes 786440 | tf_op jit(solution)/shard_map/ppermute | solution.py:505
  30.3 3.4 %collective-permute-start.3 = (f32[512,128]{1,0:T(8,128)S(1)}, f32[512,128]{1,0:T(8,128)S(1)}, u32[]{:S(2)}, u32[]{:S(2)}) collective-permute-start(f32[512,128]{1,0:T(8,128)S(1)} %collective-permute-done.1.refs_1_), channel_id=1, source_target_pairs={{0,1},{1,0},{2,3},{3,2},{4,5},{5,4},{6,7},{7,6},{8,9},{9,8},{10,11... | collective-permute-start | bytes 786440 | tf_op jit(solution)/shard_map/ppermute | solution.py:505
  30.4 4.6 %collective-permute-start.6 = (f32[512,128]{1,0:T(8,128)S(1)}, f32[512,128]{1,0:T(8,128)S(1)}, u32[]{:S(2)}, u32[]{:S(2)}) collective-permute-start(f32[512,128]{1,0:T(8,128)S(1)} %collective-permute-done.4.refs_0_.refs_3_), channel_id=1, source_target_pairs={{0,1},{1,0},{2,3},{3,2},{4,5},{5,4},{6,7},{7,6},{8,9},{9,8},{10,11... | collective-permute-start | bytes 786440 | tf_op jit(solution)/shard_map/ppermute | solution.py:505
  30.9 4.1 %collective-permute-start.7 = (f32[512,128]{1,0:T(8,128)S(1)}, f32[512,128]{1,0:T(8,128)S(1)}, u32[]{:S(2)}, u32[]{:S(2)}) collective-permute-start(f32[512,128]{1,0:T(8,128)S(1)} %collective-permute-done.5.refs_1_), channel_id=1, source_target_pairs={{0,1},{1,0},{2,3},{3,2},{4,5},{5,4},{6,7},{7,6},{8,9},{9,8},{10,11... | collective-permute-start | bytes 786440 | tf_op jit(solution)/shard_map/ppermute | solution.py:505
  33.7 1.2 %copy-start.3 = (bf16[64,192]{1,0:T(8,128)(2,1)S(1)}, bf16[64,192]{1,0:T(8,128)(2,1)}, u32[]{:S(2)}) copy-start(bf16[64,192]{1,0:T(8,128)(2,1)} %get-tuple-element.27.refs_8_.refs_3_) | copy-start | bytes 73732
  37.6 3.7 %collective-permute-start.9 = (f32[512,128]{1,0:T(8,128)S(1)}, f32[512,128]{1,0:T(8,128)S(1)}, u32[]{:S(2)}, u32[]{:S(2)}) collective-permute-start(f32[512,128]{1,0:T(8,128)S(1)} %get-tuple-element.33), channel_id=1, source_target_pairs={{0,1},{1,0},{2,3},{3,2},{4,5},{5,4},{6,7},{7,6},{8,9},{9,8},{10,11... | collective-permute-start | bytes 786440 | tf_op jit(solution)/shard_map/ppermute | solution.py:505
  38.1 9.2 %collective-permute-start.11 = (f32[512,128]{1,0:T(8,128)S(1)}, f32[512,128]{1,0:T(8,128)S(1)}, u32[]{:S(2)}, u32[]{:S(2)}) collective-permute-start(f32[512,128]{1,0:T(8,128)S(1)} %collective-permute-done.refs_0_), channel_id=1, source_target_pairs={{0,2},{1,3},{2,0},{3,1},{4,6},{5,7},{6,4},{7,5},{8,10},{9,11},{10,... | collective-permute-start | bytes 786440 | tf_op jit(solution)/shard_map/ppermute | solution.py:505
  38.8 14.1 %collective-permute-start.12 = (f32[512,128]{1,0:T(8,128)S(1)}, f32[512,128]{1,0:T(8,128)S(1)}, u32[]{:S(2)}, u32[]{:S(2)}) collective-permute-start(f32[512,128]{1,0:T(8,128)S(1)} %collective-permute-done.4.refs_0_.refs_3_), channel_id=1, source_target_pairs={{0,2},{1,3},{2,0},{3,1},{4,6},{5,7},{6,4},{7,5},{8,10},{9,11},{10,... | collective-permute-start | bytes 786440 | tf_op jit(solution)/shard_map/ppermute | solution.py:505
  40.1 12.8 %collective-permute-start.8 = (f32[512,128]{1,0:T(8,128)S(1)}, f32[512,128]{1,0:T(8,128)S(1)}, u32[]{:S(2)}, u32[]{:S(2)}) collective-permute-start(f32[512,128]{1,0:T(8,128)S(1)} %get-tuple-element.31), channel_id=1, source_target_pairs={{0,1},{1,0},{2,3},{3,2},{4,5},{5,4},{6,7},{7,6},{8,9},{9,8},{10,11... | collective-permute-start | bytes 786440 | tf_op jit(solution)/shard_map/ppermute | solution.py:505
  41.8 17.0 %collective-permute-start.10 = (f32[512,128]{1,0:T(8,128)S(1)}, f32[512,128]{1,0:T(8,128)S(1)}, u32[]{:S(2)}, u32[]{:S(2)}) collective-permute-start(f32[512,128]{1,0:T(8,128)S(1)} %shard_map.45), channel_id=1, source_target_pairs={{0,2},{1,3},{2,0},{3,1},{4,6},{5,7},{6,4},{7,5},{8,10},{9,11},{10,... | collective-permute-start | bytes 786440 | tf_op jit(solution)/shard_map/ppermute | solution.py:505
  54.0 1.2 %collective-permute-start.13 = (f32[8,128]{1,0:T(8,128)S(1)}, f32[8,128]{1,0:T(8,128)S(1)}, u32[]{:S(2)}, u32[]{:S(2)}) collective-permute-start(f32[8,128]{1,0:T(8,128)S(1)} %shard_map.46), channel_id=1, source_target_pairs={{0,1},{1,0},{2,3},{3,2},{4,5},{5,4},{6,7},{7,6},{8,9},{9,8},{10,11... | collective-permute-start | bytes 12296 | tf_op jit(solution)/shard_map/ppermute | solution.py:505
  55.2 3.6 %collective-permute-start.14 = (f32[8,128]{1,0:T(8,128)S(1)}, f32[8,128]{1,0:T(8,128)S(1)}, u32[]{:S(2)}, u32[]{:S(2)}) collective-permute-start(f32[8,128]{1,0:T(8,128)S(1)} %add.107.row), channel_id=1, source_target_pairs={{0,2},{1,3},{2,0},{3,1},{4,6},{5,7},{6,4},{7,5},{8,10},{9,11},{10,... | collective-permute-start | bytes 12296 | tf_op jit(solution)/shard_map/ppermute | solution.py:505

commit v7 on v6

--- a/solution.py
+++ b/solution.py
@@ -323,12 +323,13 @@
     return kernel_call(blend_body, kept.shape, "svv", 3 * kept.size, 3 * kept.size)(factors, kept, met)
 
 
-def finish_body(near_sum, arrived, row, other, exchanged, margin):
+def finish_body(near_sum, arrived, *refs):
+    *rows, exchanged, margin = refs
     exchanged[...] = near_sum[...] + arrived[...]
-    margin[...] = (row[...] + other[...])[:1, : margin.shape[1]]
-
-
-def finish(near_sum, arrived, row, other, columns):
+    margin[...] = functools.reduce(jnp.add, [row[...] for row in rows])[:1, : margin.shape[1]]
+
+
+def finish(near_sum, arrived, rows, columns):
     vmem = pl.BlockSpec(memory_space=pltpu.VMEM)
     return pl.pallas_call(
         finish_body,
@@ -336,14 +337,14 @@
             jax.ShapeDtypeStruct(near_sum.shape, jnp.float32),
             jax.ShapeDtypeStruct((1, columns), jnp.float32),
         ],
-        in_specs=[vmem] * 4,
+        in_specs=[vmem] * (2 + len(rows)),
         out_specs=[vmem] * 2,
         compiler_params=pltpu.CompilerParams(vmem_limit_bytes=24 << 20),
         cost_estimate=pl.CostEstimate(
             flops=near_sum.size, bytes_accessed=12 * near_sum.size, transcendentals=0
         ),
         name="finish",
-    )(near_sum, arrived, row, other)
+    )(near_sum, arrived, *rows)
 
 
 def seat_body(offsets, places, factors, *, blocks, replicas):
@@ -554,9 +555,8 @@
         moved_last,
     )
     near_sum = blend(factors, kept[1], met_near)
-    row = row + replica_swap(row, 1)
-    other = replica_swap(row, 2)
-    exchanged, margin = finish(near_sum, arrived, row, other, blocks)
+    others = [replica_swap(row, bits) for bits in (2, 3, 1)]
+    exchanged, margin = finish(near_sum, arrived, (row, *others), blocks)
     return exchanged.reshape(1, cells // replicas), margin
 
 

time: 59.8 us -> 58.7 us (0.982)
  waiting for transfers between devices: 29.8 us -> 27.4 us
  starting transfers between devices: 11.9 us -> 13.3 us
    ppermute x11 -> x12, waiting for transfers between devices: 13.7 us -> 11.3 us  [replica_swap(): return lax.ppermute(value, 'rep', [(r, r ^ bit) for r in range(replicas)])]
    ppermute x11 -> x12, starting transfers between devices: 4.69 us -> 6.11 us  [replica_swap(): return lax.ppermute(value, 'rep', [(r, r ^ bit) for r in range(replicas)])]
  transfers between devices with their start and end apart: 15 -> 16, of which waited for: 6 -> 6; matrix products, arithmetic and copies ran while one was open for 6% -> 6% of each run, Pallas kernels for 14% -> 15%
where the time goes in v7:
time: 58.7 us; the launch traced here: 58.5 us
  waiting for transfers between devices  27.4 us (47%)
  starting transfers between devices  13.3 us (23%)
  Pallas kernels  11.9 us (20%)
  other arithmetic  2.91 us (5%)
  local copies, waits for them, and re-layouts  2.14 us (4%)
  between operations  0.9 us (2%)
    ppermute x4, waiting for transfers between devices, along_blocks(): return lax.ppermute(value, ('blk', 'rep'), route)  16.1 us
    ppermute x12, waiting for transfers between devices, replica_swap(): return lax.ppermute(value, 'rep', [(r, r ^ bit) for r in range(replicas)])  11.3 us
    ppermute x4, starting transfers between devices, along_blocks(): return lax.ppermute(value, ('blk', 'rep'), route)  7.17 us
    ppermute x12, starting transfers between devices, replica_swap(): return lax.ppermute(value, 'rep', [(r, r ^ bit) for r in range(replicas)])  6.11 us
    pallas_call x1, Pallas kernels, spectrum(): planes_call(body, 5 + 2 * len(heads) + 2 * count, (rows // NG * PITCH, la...  2.59 us
    pallas_call x2, Pallas kernels, first_planes(): planes_call(body, 3 + 2 * count, (pitched, rows), (rows,), rows * LANES *...  2.18 us
    select_n x1, other arithmetic, screened_kernel(): return jnp.where(k_squared > 0.5, screened, jnp.ones_like(screened))  1.7 us
    pallas_call x1, Pallas kernels, prepared_weights(): pl.pallas_call(weights_body, out_shape=[jax.ShapeDtypeStruct(shape, jnp.b...  1.63 us
  transfers between devices with their start and end apart: 16, of which 6 were waited for; matrix products, arithmetic and copies ran while one was open for 6% of the time, Pallas kernels for 15%

profile of v7, /device:TPU:0, one launch (start us, length us, event | category | flops | bytes accessed | tf_op | source)
XLA Modules:
  0.0 58.5 jit_solution(7408194960213203098)
XLA Ops:
  0.7 1.3 %constant_dynamic-slice_fusion = (f32[512,128]{1,0:T(8,128)S(1)}, f32[512,128]{1,0:T(8,128)S(1)}, f32[512,128]{1,0:T(8,128)S(1)}, f32[512,128]{1,0:T(8,128)S(1)}) fusion(f32[2048,128]{1,0:T(8,128)} %bitcast.2, s32[]{:T(128)S(6)} %select_n.75, s32[]{:T(128)S(6)} %select_n.74, s32[]{:T(128)S(6)} %select_n.70, s32[]{:T(128)S(6)} %select_n.69), kind=kLoop, calls=%fused_computation.60 | loop fusion | bytes 2097168 | tf_op jit(solution)/shard_map/dynamic_slice | solution.py:509
  1.9 5.1 %collective-permute-start.4 = (f32[512,128]{1,0:T(8,128)S(1)}, f32[512,128]{1,0:T(8,128)S(1)}, u32[]{:S(2)}, u32[]{:S(2)}) collective-permute-start(f32[512,128]{1,0:T(8,128)S(1)} %get-tuple-element.37), channel_id=1, source_target_pairs={{12,0},{13,1},{10,2},{11,3},{8,4},{9,5},{14,6},{15,7},{4,8},{5,9},... | collective-permute-start | bytes 786440 | tf_op jit(solution)/shard_map/ppermute | solution.py:503
  7.1 0.9 %collective-permute-start = (f32[512,128]{1,0:T(8,128)S(1)}, f32[512,128]{1,0:T(8,128)S(1)}, u32[]{:S(2)}, u32[]{:S(2)}) collective-permute-start(f32[512,128]{1,0:T(8,128)S(1)} %get-tuple-element.39), channel_id=1, source_target_pairs={{12,0},{13,1},{10,2},{11,3},{8,4},{9,5},{14,6},{15,7},{4,8},{5,9},... | collective-permute-start | bytes 786440 | tf_op jit(solution)/shard_map/ppermute | solution.py:503
  8.0 1.1 %collective-permute-start.1 = (f32[512,128]{1,0:T(8,128)S(1)}, f32[512,128]{1,0:T(8,128)S(1)}, u32[]{:S(2)}, u32[]{:S(2)}) collective-permute-start(f32[512,128]{1,0:T(8,128)S(1)} %get-tuple-element.38), channel_id=1, source_target_pairs={{4,0},{5,1},{6,2},{7,3},{0,4},{1,5},{2,6},{3,7},{12,8},{13,9},{14,... | collective-permute-start | bytes 786440 | tf_op jit(solution)/shard_map/ppermute | solution.py:503
  9.4 0.9 %sine_add_fusion.1 = (f32[64,64]{1,0:T(8,128)}, f32[64,64]{1,0:T(8,128)}) fusion(s32[64]{0:T(128)S(1)} %mul.133), kind=kLoop, calls=%fused_computation.34 | loop fusion | flops 122880 | bytes 33024 | tf_op jit(solution)/shard_map/add | solution.py:36
  10.4 0.8 %mul.149.paired = f32[128,128]{1,0:T(8,128)} reshape(f32[2,64,2,64]{3,2,1,0:T(2,128)S(1)} %broadcast_multiply_fusion) | data formatting | bytes 131072 | tf_op jit(solution)/shard_map/jit(kron)/mul | solution.py:567
  11.2 1.4 %seat.1 = (s32[13]{0:T(128)}, f32[10]{0:T(128)}) custom-call(s32[4]{0:T(128)} %offsets.1), custom_call_target="tpu_custom_call" | custom-call | tf_op jit(solution)/shard_map/seat/pallas_call | solution.py:385
  12.6 1.6 %weights.1 = (bf16[64,192]{1,0:T(8,128)(2,1)}, bf16[64,192]{1,0:T(8,128)(2,1)}, bf16[256,256]{1,0:T(8,128)(2,1)}) custom-call(f32[64,64]{1,0:T(8,128)} %get-tuple-element.41.forward, f32[64,64]{1,0:T(8,128)} %get-tuple-element.40.backward, f32[128,128]{1,0:T(8,128)} %mul.149.paired), custom_call_target="tpu_custom_call" | custom-call | tf_op jit(solution)/shard_map/weights/pallas_call | solution.py:128
  14.3 11.4 %collective-permute-done.refs_0_ = f32[512,128]{1,0:T(8,128)S(1)} collective-permute-done((f32[512,128]{1,0:T(8,128)S(1)}, f32[512,128]{1,0:T(8,128)S(1)}, u32[]{:S(2)}, u32[]{:S(2)}) %collective-permute-start) | collective-permute-done | bytes 262176 | tf_op jit(solution)/shard_map/ppermute | solution.py:503
  25.6 4.7 %collective-permute-done.1.refs_1_ = f32[512,128]{1,0:T(8,128)S(1)} collective-permute-done((f32[512,128]{1,0:T(8,128)S(1)}, f32[512,128]{1,0:T(8,128)S(1)}, u32[]{:S(2)}, u32[]{:S(2)}) %collective-permute-start.1) | collective-permute-done | bytes 262176 | tf_op jit(solution)/shard_map/ppermute | solution.py:503
  30.9 1.7 %multiply_select_fusion.refs_6_ = f32[2048,128]{1,0:T(8,128)S(1)} fusion(s32[128]{0:T(128)S(1)} %get-tuple-element.51, s32[128]{0:T(128)S(1)} %get-tuple-element.52, s32[128]{0:T(128)S(1)} %get-tuple-element.50, s32[128]{0:T(128)S(1)} %get-tuple-element.53, s32[2048]{0:T(1024)S(1)} %get-tuple-element.44, s32[2048]{0:T(1024)S(1)} %get-tuple-element.47, ...), kind=kLoop, calls=%fused_computation.11 | loop fusion | flops 8126464 | bytes 1087744 | tf_op jit(solution)/shard_map/jit(_where)/select_n | solution.py:59
  32.7 1.0 %shard_map.42 = (f32[520,128]{1,0:T(8,128)S(1)}, f32[512,128]{1,0:T(8,128)S(1)}) custom-call(s32[13]{0:T(128)S(1)} %copy-done.5, f32[10]{0:T(128)S(1)} %copy-done.4, f32[2048,128]{1,0:T(8,128)S(1)} %bitcast.3, f32[512,128]{1,0:T(8,128)S(1)} %collective-permute-done.4.refs_0_.refs_3_, f32[512,128]{1,0:T(8,128)S(1)} %collective-permute-done.5.refs_1_, ...), custom_call_target="tpu_custom_call" | custom-call | flops 16777216 | bytes 1048576 | tf_op jit(solution)/shard_map/pallas_call | solution.py:242
  33.8 1.1 %shard_map.41 = (f32[1040,128]{1,0:T(8,128)S(1)}, f32[1024,128]{1,0:T(8,128)S(1)}) custom-call(s32[13]{0:T(128)S(1)} %copy-done.5, f32[10]{0:T(128)S(1)} %copy-done.4, f32[2048,128]{1,0:T(8,128)S(1)} %bitcast.4, f32[512,128]{1,0:T(8,128)S(1)} %collective-permute-done.refs_0_, f32[512,128]{1,0:T(8,128)S(1)} %collective-permute-done.1.refs_1_, ...), custom_call_target="tpu_custom_call" | custom-call | flops 33554432 | bytes 2097152 | tf_op jit(solution)/shard_map/pallas_call | solution.py:242
  34.9 2.6 %shard_map.43 = (f32[2080,128]{1,0:T(8,128)S(1)}, f32[512,128]{1,0:T(8,128)S(1)}, f32[512,128]{1,0:T(8,128)S(1)}, f32[512,128]{1,0:T(8,128)S(1)}) custom-call(s32[13]{0:T(128)S(1)} %copy-done.5, f32[10]{0:T(128)S(1)} %copy-done.4, f32[2048,128]{1,0:T(8,128)S(1)} %bitcast.5, f32[1040,128]{1,0:T(8,128)S(1)} %get-tuple-element.23.refs_0_, ...), custom_call_target="tpu_custom_call" | custom-call | flops 268435456 | bytes 8388608 | tf_op jit(solution)/shard_map/pallas_call | solution.py:252
  38.8 1.3 %collective-permute-start.12 = (f32[512,128]{1,0:T(8,128)S(1)}, f32[512,128]{1,0:T(8,128)S(1)}, u32[]{:S(2)}, u32[]{:S(2)}) collective-permute-start(f32[512,128]{1,0:T(8,128)S(1)} %collective-permute-done.4.refs_0_.refs_3_), channel_id=1, source_target_pairs={{0,2},{1,3},{2,0},{3,1},{4,6},{5,7},{6,4},{7,5},{8,10},{9,11},{10,... | collective-permute-start | bytes 786440 | tf_op jit(solution)/shard_map/ppermute | solution.py:506
  40.1 1.1 %terms.1 = (f32[512,128]{1,0:T(8,128)S(1)}, f32[512,128]{1,0:T(8,128)S(1)}) custom-call(s32[13]{0:T(128)S(1)} %copy-done.5, f32[2080,128]{1,0:T(8,128)S(1)} %get-tuple-element.28.spectral, f32[1024,128]{1,0:T(8,128)S(1)} %get-tuple-element.25.refs_2_.refs_0_, f32[512,128]{1,0:T(8,128)S(1)} %get-tuple-element.26.refs_3_.refs_1_, ...), custom_call_target="tpu_custom_call" | custom-call | flops 100663296 | bytes 2097152 | tf_op jit(solution)/shard_map/terms/pallas_call | solution.py:306
  41.8 0.8 %collective-permute-start.10 = (f32[512,128]{1,0:T(8,128)S(1)}, f32[512,128]{1,0:T(8,128)S(1)}, u32[]{:S(2)}, u32[]{:S(2)}) collective-permute-start(f32[512,128]{1,0:T(8,128)S(1)} %shard_map.45), channel_id=1, source_target_pairs={{0,2},{1,3},{2,0},{3,1},{4,6},{5,7},{6,4},{7,5},{8,10},{9,11},{10,... | collective-permute-start | bytes 786440 | tf_op jit(solution)/shard_map/ppermute | solution.py:506
  42.6 4.6 %collective-permute-done.11.refs_2_ = f32[512,128]{1,0:T(8,128)S(1)} collective-permute-done((f32[512,128]{1,0:T(8,128)S(1)}, f32[512,128]{1,0:T(8,128)S(1)}, u32[]{:S(2)}, u32[]{:S(2)}) %collective-permute-start.11) | collective-permute-done | bytes 262176 | tf_op jit(solution)/shard_map/ppermute | solution.py:506
  47.2 5.6 %collective-permute-done.12.refs_5_ = f32[512,128]{1,0:T(8,128)S(1)} collective-permute-done((f32[512,128]{1,0:T(8,128)S(1)}, f32[512,128]{1,0:T(8,128)S(1)}, u32[]{:S(2)}, u32[]{:S(2)}) %collective-permute-start.12) | collective-permute-done | bytes 262176 | tf_op jit(solution)/shard_map/ppermute | solution.py:506
  52.9 1.1 %shard_map.46.refs_0_ = f32[8,128]{1,0:T(8,128)S(1)} custom-call(s32[13]{0:T(128)S(1)} %copy-done.5, f32[10]{0:T(128)S(1)} %copy-done.4, f32[512,128]{1,0:T(8,128)S(1)} %get-tuple-element.32.kept.far, f32[512,128]{1,0:T(8,128)S(1)} %collective-permute-done.9.met.met_far, f32[512,128]{1,0:T(8,128)S(1)} %get-tuple-element.30.kept.near, ...), custom_call_target="tpu_custom_call" | custom-call | flops 2097152 | bytes 3145728 | tf_op jit(solution)/shard_map/pallas_call | solution.py:437
  54.0 0.8 %collective-permute-start.13 = (f32[8,128]{1,0:T(8,128)S(1)}, f32[8,128]{1,0:T(8,128)S(1)}, u32[]{:S(2)}, u32[]{:S(2)}) collective-permute-start(f32[8,128]{1,0:T(8,128)S(1)} %shard_map.46.refs_0_), channel_id=1, source_target_pairs={{0,2},{1,3},{2,0},{3,1},{4,6},{5,7},{6,4},{7,5},{8,10},{9,11},{10,... | collective-permute-start | bytes 12296 | tf_op jit(solution)/shard_map/ppermute | solution.py:506
  54.8 1.4 %collective-permute-start.15 = (f32[8,128]{1,0:T(8,128)S(1)}, f32[8,128]{1,0:T(8,128)S(1)}, u32[]{:S(2)}, u32[]{:S(2)}) collective-permute-start(f32[8,128]{1,0:T(8,128)S(1)} %shard_map.46.refs_0_), channel_id=1, source_target_pairs={{0,1},{1,0},{2,3},{3,2},{4,5},{5,4},{6,7},{7,6},{8,9},{9,8},{10,11... | collective-permute-start | bytes 12296 | tf_op jit(solution)/shard_map/ppermute | solution.py:506
  56.8 0.9 %collective-permute-done.13.refs_1_ = f32[8,128]{1,0:T(8,128)S(1)} collective-permute-done((f32[8,128]{1,0:T(8,128)S(1)}, f32[8,128]{1,0:T(8,128)S(1)}, u32[]{:S(2)}, u32[]{:S(2)}) %collective-permute-start.13) | collective-permute-done | bytes 4128 | tf_op jit(solution)/shard_map/ppermute | solution.py:506
  57.8 0.7 %finish.1 = (f32[512,128]{1,0:T(8,128)}, f32[1,4]{1,0:T(1,128)}) custom-call(f32[512,128]{1,0:T(8,128)S(1)} %shard_map.44.near_sum, f32[512,128]{1,0:T(8,128)S(1)} %collective-permute-done.10.arrived, f32[8,128]{1,0:T(8,128)S(1)} %shard_map.46.refs_0_, f32[8,128]{1,0:T(8,128)S(1)} %collective-permute-done.13.refs_1_, ...), custom_call_target="tpu_custom_call" | custom-call | flops 65536 | bytes 786432 | tf_op jit(solution)/shard_map/finish/pallas_call | solution.py:334
  (45 shorter events, 3.5 us)
Async XLA Ops:
  1.9 30.7 %copy-start = (f32[1,262144]{1,0:T(1,128)S(1)}, f32[1,262144]{1,0:T(1,128)}, u32[]{:S(2)}) copy-start(f32[1,262144]{1,0:T(1,128)} %param.2) | copy-start | bytes 3145732
  1.9 28.4 %collective-permute-start.4 = (f32[512,128]{1,0:T(8,128)S(1)}, f32[512,128]{1,0:T(8,128)S(1)}, u32[]{:S(2)}, u32[]{:S(2)}) collective-permute-start(f32[512,128]{1,0:T(8,128)S(1)} %get-tuple-element.37), channel_id=1, source_target_pairs={{12,0},{13,1},{10,2},{11,3},{8,4},{9,5},{14,6},{15,7},{4,8},{5,9},... | collective-permute-start | bytes 786440 | tf_op jit(solution)/shard_map/ppermute | solution.py:503
  7.1 23.8 %collective-permute-start.5 = (f32[512,128]{1,0:T(8,128)S(1)}, f32[512,128]{1,0:T(8,128)S(1)}, u32[]{:S(2)}, u32[]{:S(2)}) collective-permute-start(f32[512,128]{1,0:T(8,128)S(1)} %get-tuple-element.36), channel_id=1, source_target_pairs={{4,0},{5,1},{6,2},{7,3},{0,4},{1,5},{2,6},{3,7},{12,8},{13,9},{14,... | collective-permute-start | bytes 786440 | tf_op jit(solution)/shard_map/ppermute | solution.py:503
  7.1 18.5 %collective-permute-start = (f32[512,128]{1,0:T(8,128)S(1)}, f32[512,128]{1,0:T(8,128)S(1)}, u32[]{:S(2)}, u32[]{:S(2)}) collective-permute-start(f32[512,128]{1,0:T(8,128)S(1)} %get-tuple-element.39), channel_id=1, source_target_pairs={{12,0},{13,1},{10,2},{11,3},{8,4},{9,5},{14,6},{15,7},{4,8},{5,9},... | collective-permute-start | bytes 786440 | tf_op jit(solution)/shard_map/ppermute | solution.py:503
  8.0 22.4 %collective-permute-start.1 = (f32[512,128]{1,0:T(8,128)S(1)}, f32[512,128]{1,0:T(8,128)S(1)}, u32[]{:S(2)}, u32[]{:S(2)}) collective-permute-start(f32[512,128]{1,0:T(8,128)S(1)} %get-tuple-element.38), channel_id=1, source_target_pairs={{4,0},{5,1},{6,2},{7,3},{0,4},{1,5},{2,6},{3,7},{12,8},{13,9},{14,... | collective-permute-start | bytes 786440 | tf_op jit(solution)/shard_map/ppermute | solution.py:503
  12.6 20.1 %copy-start.4 = (f32[10]{0:T(128)S(1)}, f32[10]{0:T(128)}, u32[]{:S(2)}) copy-start(f32[10]{0:T(128)} %get-tuple-element.19.factors) | copy-start | bytes 124
  12.6 20.1 %copy-start.5 = (s32[13]{0:T(128)S(1)}, s32[13]{0:T(128)}, u32[]{:S(2)}) copy-start(s32[13]{0:T(128)} %get-tuple-element.20.places) | copy-start | bytes 160
  14.2 18.4 %copy-start.1 = (bf16[256,256]{1,0:T(8,128)(2,1)S(1)}, bf16[256,256]{1,0:T(8,128)(2,1)}, u32[]{:S(2)}) copy-start(bf16[256,256]{1,0:T(8,128)(2,1)} %get-tuple-element.22.refs_5_.refs_3_.refs_9_.refs_4_) | copy-start | bytes 393220
  14.2 18.4 %copy-start.2 = (bf16[64,192]{1,0:T(8,128)(2,1)S(1)}, bf16[64,192]{1,0:T(8,128)(2,1)}, u32[]{:S(2)}) copy-start(bf16[64,192]{1,0:T(8,128)(2,1)} %get-tuple-element.21.refs_4_.refs_2_.refs_7_) | copy-start | bytes 73732
  25.6 8.1 %collective-permute-start.2 = (f32[512,128]{1,0:T(8,128)S(1)}, f32[512,128]{1,0:T(8,128)S(1)}, u32[]{:S(2)}, u32[]{:S(2)}) collective-permute-start(f32[512,128]{1,0:T(8,128)S(1)} %collective-permute-done.refs_0_), channel_id=1, source_target_pairs={{0,1},{1,0},{2,3},{3,2},{4,5},{5,4},{6,7},{7,6},{8,9},{9,8},{10,11... | collective-permute-start | bytes 786440 | tf_op jit(solution)/shard_map/ppermute | solution.py:506
  30.3 3.4 %collective-permute-start.3 = (f32[512,128]{1,0:T(8,128)S(1)}, f32[512,128]{1,0:T(8,128)S(1)}, u32[]{:S(2)}, u32[]{:S(2)}) collective-permute-start(f32[512,128]{1,0:T(8,128)S(1)} %collective-permute-done.1.refs_1_), channel_id=1, source_target_pairs={{0,1},{1,0},{2,3},{3,2},{4,5},{5,4},{6,7},{7,6},{8,9},{9,8},{10,11... | collective-permute-start | bytes 786440 | tf_op jit(solution)/shard_map/ppermute | solution.py:506
  30.4 4.6 %collective-permute-start.6 = (f32[512,128]{1,0:T(8,128)S(1)}, f32[512,128]{1,0:T(8,128)S(1)}, u32[]{:S(2)}, u32[]{:S(2)}) collective-permute-start(f32[512,128]{1,0:T(8,128)S(1)} %collective-permute-done.4.refs_0_.refs_3_), channel_id=1, source_target_pairs={{0,1},{1,0},{2,3},{3,2},{4,5},{5,4},{6,7},{7,6},{8,9},{9,8},{10,11... | collective-permute-start | bytes 786440 | tf_op jit(solution)/shard_map/ppermute | solution.py:506
  30.9 4.1 %collective-permute-start.7 = (f32[512,128]{1,0:T(8,128)S(1)}, f32[512,128]{1,0:T(8,128)S(1)}, u32[]{:S(2)}, u32[]{:S(2)}) collective-permute-start(f32[512,128]{1,0:T(8,128)S(1)} %collective-permute-done.5.refs_1_), channel_id=1, source_target_pairs={{0,1},{1,0},{2,3},{3,2},{4,5},{5,4},{6,7},{7,6},{8,9},{9,8},{10,11... | collective-permute-start | bytes 786440 | tf_op jit(solution)/shard_map/ppermute | solution.py:506
  33.7 1.2 %copy-start.3 = (bf16[64,192]{1,0:T(8,128)(2,1)S(1)}, bf16[64,192]{1,0:T(8,128)(2,1)}, u32[]{:S(2)}) copy-start(bf16[64,192]{1,0:T(8,128)(2,1)} %get-tuple-element.27.refs_8_.refs_3_) | copy-start | bytes 73732
  37.6 3.7 %collective-permute-start.9 = (f32[512,128]{1,0:T(8,128)S(1)}, f32[512,128]{1,0:T(8,128)S(1)}, u32[]{:S(2)}, u32[]{:S(2)}) collective-permute-start(f32[512,128]{1,0:T(8,128)S(1)} %get-tuple-element.33), channel_id=1, source_target_pairs={{0,1},{1,0},{2,3},{3,2},{4,5},{5,4},{6,7},{7,6},{8,9},{9,8},{10,11... | collective-permute-start | bytes 786440 | tf_op jit(solution)/shard_map/ppermute | solution.py:506
  38.1 9.2 %collective-permute-start.11 = (f32[512,128]{1,0:T(8,128)S(1)}, f32[512,128]{1,0:T(8,128)S(1)}, u32[]{:S(2)}, u32[]{:S(2)}) collective-permute-start(f32[512,128]{1,0:T(8,128)S(1)} %collective-permute-done.refs_0_), channel_id=1, source_target_pairs={{0,2},{1,3},{2,0},{3,1},{4,6},{5,7},{6,4},{7,5},{8,10},{9,11},{10,... | collective-permute-start | bytes 786440 | tf_op jit(solution)/shard_map/ppermute | solution.py:506
  38.8 14.1 %collective-permute-start.12 = (f32[512,128]{1,0:T(8,128)S(1)}, f32[512,128]{1,0:T(8,128)S(1)}, u32[]{:S(2)}, u32[]{:S(2)}) collective-permute-start(f32[512,128]{1,0:T(8,128)S(1)} %collective-permute-done.4.refs_0_.refs_3_), channel_id=1, source_target_pairs={{0,2},{1,3},{2,0},{3,1},{4,6},{5,7},{6,4},{7,5},{8,10},{9,11},{10,... | collective-permute-start | bytes 786440 | tf_op jit(solution)/shard_map/ppermute | solution.py:506
  40.1 12.8 %collective-permute-start.8 = (f32[512,128]{1,0:T(8,128)S(1)}, f32[512,128]{1,0:T(8,128)S(1)}, u32[]{:S(2)}, u32[]{:S(2)}) collective-permute-start(f32[512,128]{1,0:T(8,128)S(1)} %get-tuple-element.31), channel_id=1, source_target_pairs={{0,1},{1,0},{2,3},{3,2},{4,5},{5,4},{6,7},{7,6},{8,9},{9,8},{10,11... | collective-permute-start | bytes 786440 | tf_op jit(solution)/shard_map/ppermute | solution.py:506
  41.8 16.0 %collective-permute-start.10 = (f32[512,128]{1,0:T(8,128)S(1)}, f32[512,128]{1,0:T(8,128)S(1)}, u32[]{:S(2)}, u32[]{:S(2)}) collective-permute-start(f32[512,128]{1,0:T(8,128)S(1)} %shard_map.45), channel_id=1, source_target_pairs={{0,2},{1,3},{2,0},{3,1},{4,6},{5,7},{6,4},{7,5},{8,10},{9,11},{10,... | collective-permute-start | bytes 786440 | tf_op jit(solution)/shard_map/ppermute | solution.py:506
  54.0 3.7 %collective-permute-start.13 = (f32[8,128]{1,0:T(8,128)S(1)}, f32[8,128]{1,0:T(8,128)S(1)}, u32[]{:S(2)}, u32[]{:S(2)}) collective-permute-start(f32[8,128]{1,0:T(8,128)S(1)} %shard_map.46.refs_0_), channel_id=1, source_target_pairs={{0,2},{1,3},{2,0},{3,1},{4,6},{5,7},{6,4},{7,5},{8,10},{9,11},{10,... | collective-permute-start | bytes 12296 | tf_op jit(solution)/shard_map/ppermute | solution.py:506
  54.8 3.0 %collective-permute-start.14 = (f32[8,128]{1,0:T(8,128)S(1)}, f32[8,128]{1,0:T(8,128)S(1)}, u32[]{:S(2)}, u32[]{:S(2)}) collective-permute-start(f32[8,128]{1,0:T(8,128)S(1)} %shard_map.46.refs_0_), channel_id=1, source_target_pairs={{0,3},{1,2},{2,1},{3,0},{4,7},{5,6},{6,5},{7,4},{8,11},{9,10},{10,... | collective-permute-start | bytes 12296 | tf_op jit(solution)/shard_map/ppermute | solution.py:506
  54.8 3.0 %collective-permute-start.15 = (f32[8,128]{1,0:T(8,128)S(1)}, f32[8,128]{1,0:T(8,128)S(1)}, u32[]{:S(2)}, u32[]{:S(2)}) collective-permute-start(f32[8,128]{1,0:T(8,128)S(1)} %shard_map.46.refs_0_), channel_id=1, source_target_pairs={{0,1},{1,0},{2,3},{3,2},{4,5},{5,4},{6,7},{7,6},{8,9},{9,8},{10,11... | collective-permute-start | bytes 12296 | tf_op jit(solution)/shard_map/ppermute | solution.py:506

commit v8 on v7

--- a/solution.py
+++ b/solution.py
@@ -13,7 +13,7 @@
 LANES = 128
 HALF = LANES // 2
 PITCH = NG + 1
-GROUP = 256
+GROUP = 128
 MET = (3, 1, 2, 0)
 SENT = (3, 1, 2, 1)
 SENT_A = (3, 3, 2, 2)
@@ -398,7 +398,7 @@
     *stores, out = refs
     even = places[LOW] == 0
     rows = far.shape[0]
-    chunk = 64
+    chunk = 32
 
     def folded_rows(value):
         return jnp.sum(value.reshape(chunk // 8, 8, LANES), axis=0)
@@ -423,7 +423,7 @@
                 totals[4 * t + o] + folded_rows(terms[t] * orbitals[o]) for t in range(2) for o in range(4)
             )
 
-        totals = lax.fori_loop(0, rows // chunk, step, totals, unroll=4)
+        totals = lax.fori_loop(0, rows // chunk, step, totals, unroll=8)
     lane = lax.broadcasted_iota(jnp.int32, (8, LANES), 1)
     result = jnp.zeros((8, LANES), jnp.float32)
     for o in range(4):

time: 58.7 us -> 58.6 us (level)
  no operation moved by 1% of the time
where the time goes in v8:
time: 58.6 us; the launch traced here: 58.4 us
  waiting for transfers between devices  27.4 us (47%)
  starting transfers between devices  13.3 us (23%)
  Pallas kernels  11.8 us (20%)
  other arithmetic  2.91 us (5%)
  local copies, waits for them, and re-layouts  2.14 us (4%)
  between operations  0.9 us (2%)
    ppermute x4, waiting for transfers between devices, along_blocks(): return lax.ppermute(value, ('blk', 'rep'), route)  16.1 us
    ppermute x12, waiting for transfers between devices, replica_swap(): return lax.ppermute(value, 'rep', [(r, r ^ bit) for r in range(replicas)])  11.3 us
    ppermute x4, starting transfers between devices, along_blocks(): return lax.ppermute(value, ('blk', 'rep'), route)  7.17 us
    ppermute x12, starting transfers between devices, replica_swap(): return lax.ppermute(value, 'rep', [(r, r ^ bit) for r in range(replicas)])  6.11 us
    pallas_call x1, Pallas kernels, spectrum(): planes_call(body, 5 + 2 * len(heads) + 2 * count, (rows // NG * PITCH, la...  2.56 us
    pallas_call x2, Pallas kernels, first_planes(): planes_call(body, 3 + 2 * count, (pitched, rows), (rows,), rows * LANES *...  2.15 us
    select_n x1, other arithmetic, screened_kernel(): return jnp.where(k_squared > 0.5, screened, jnp.ones_like(screened))  1.7 us
    pallas_call x1, Pallas kernels, prepared_weights(): pl.pallas_call(weights_body, out_shape=[jax.ShapeDtypeStruct(shape, jnp.b...  1.63 us
  transfers between devices with their start and end apart: 16, of which 6 were waited for; matrix products, arithmetic and copies ran while one was open for 6% of the time, Pallas kernels for 15%

profile of v8, /device:TPU:0, one launch (start us, length us, event | category | flops | bytes accessed | tf_op | source)
XLA Modules:
  0.0 58.4 jit_solution(13520241585306326447)
XLA Ops:
  0.7 1.3 %constant_dynamic-slice_fusion = (f32[512,128]{1,0:T(8,128)S(1)}, f32[512,128]{1,0:T(8,128)S(1)}, f32[512,128]{1,0:T(8,128)S(1)}, f32[512,128]{1,0:T(8,128)S(1)}) fusion(f32[2048,128]{1,0:T(8,128)} %bitcast.2, s32[]{:T(128)S(6)} %select_n.75, s32[]{:T(128)S(6)} %select_n.74, s32[]{:T(128)S(6)} %select_n.70, s32[]{:T(128)S(6)} %select_n.69), kind=kLoop, calls=%fused_computation.60 | loop fusion | bytes 2097168 | tf_op jit(solution)/shard_map/dynamic_slice | solution.py:509
  1.9 5.1 %collective-permute-start.4 = (f32[512,128]{1,0:T(8,128)S(1)}, f32[512,128]{1,0:T(8,128)S(1)}, u32[]{:S(2)}, u32[]{:S(2)}) collective-permute-start(f32[512,128]{1,0:T(8,128)S(1)} %get-tuple-element.37), channel_id=1, source_target_pairs={{12,0},{13,1},{10,2},{11,3},{8,4},{9,5},{14,6},{15,7},{4,8},{5,9},... | collective-permute-start | bytes 786440 | tf_op jit(solution)/shard_map/ppermute | solution.py:503
  7.1 0.9 %collective-permute-start = (f32[512,128]{1,0:T(8,128)S(1)}, f32[512,128]{1,0:T(8,128)S(1)}, u32[]{:S(2)}, u32[]{:S(2)}) collective-permute-start(f32[512,128]{1,0:T(8,128)S(1)} %get-tuple-element.39), channel_id=1, source_target_pairs={{12,0},{13,1},{10,2},{11,3},{8,4},{9,5},{14,6},{15,7},{4,8},{5,9},... | collective-permute-start | bytes 786440 | tf_op jit(solution)/shard_map/ppermute | solution.py:503
  8.0 1.1 %collective-permute-start.1 = (f32[512,128]{1,0:T(8,128)S(1)}, f32[512,128]{1,0:T(8,128)S(1)}, u32[]{:S(2)}, u32[]{:S(2)}) collective-permute-start(f32[512,128]{1,0:T(8,128)S(1)} %get-tuple-element.38), channel_id=1, source_target_pairs={{4,0},{5,1},{6,2},{7,3},{0,4},{1,5},{2,6},{3,7},{12,8},{13,9},{14,... | collective-permute-start | bytes 786440 | tf_op jit(solution)/shard_map/ppermute | solution.py:503
  9.4 0.9 %sine_add_fusion.1 = (f32[64,64]{1,0:T(8,128)}, f32[64,64]{1,0:T(8,128)}) fusion(s32[64]{0:T(128)S(1)} %mul.133), kind=kLoop, calls=%fused_computation.34 | loop fusion | flops 122880 | bytes 33024 | tf_op jit(solution)/shard_map/add | solution.py:36
  10.4 0.8 %mul.149.paired = f32[128,128]{1,0:T(8,128)} reshape(f32[2,64,2,64]{3,2,1,0:T(2,128)S(1)} %broadcast_multiply_fusion) | data formatting | bytes 131072 | tf_op jit(solution)/shard_map/jit(kron)/mul | solution.py:567
  11.2 1.4 %seat.1 = (s32[13]{0:T(128)}, f32[10]{0:T(128)}) custom-call(s32[4]{0:T(128)} %offsets.1), custom_call_target="tpu_custom_call" | custom-call | tf_op jit(solution)/shard_map/seat/pallas_call | solution.py:385
  12.6 1.6 %weights.1 = (bf16[64,192]{1,0:T(8,128)(2,1)}, bf16[64,192]{1,0:T(8,128)(2,1)}, bf16[256,256]{1,0:T(8,128)(2,1)}) custom-call(f32[64,64]{1,0:T(8,128)} %get-tuple-element.41.forward, f32[64,64]{1,0:T(8,128)} %get-tuple-element.40.backward, f32[128,128]{1,0:T(8,128)} %mul.149.paired), custom_call_target="tpu_custom_call" | custom-call | tf_op jit(solution)/shard_map/weights/pallas_call | solution.py:128
  14.3 11.4 %collective-permute-done.refs_0_ = f32[512,128]{1,0:T(8,128)S(1)} collective-permute-done((f32[512,128]{1,0:T(8,128)S(1)}, f32[512,128]{1,0:T(8,128)S(1)}, u32[]{:S(2)}, u32[]{:S(2)}) %collective-permute-start) | collective-permute-done | bytes 262176 | tf_op jit(solution)/shard_map/ppermute | solution.py:503
  25.6 4.7 %collective-permute-done.1.refs_1_ = f32[512,128]{1,0:T(8,128)S(1)} collective-permute-done((f32[512,128]{1,0:T(8,128)S(1)}, f32[512,128]{1,0:T(8,128)S(1)}, u32[]{:S(2)}, u32[]{:S(2)}) %collective-permute-start.1) | collective-permute-done | bytes 262176 | tf_op jit(solution)/shard_map/ppermute | solution.py:503
  30.9 1.7 %multiply_select_fusion.refs_6_ = f32[2048,128]{1,0:T(8,128)S(1)} fusion(s32[128]{0:T(128)S(1)} %get-tuple-element.51, s32[128]{0:T(128)S(1)} %get-tuple-element.52, s32[128]{0:T(128)S(1)} %get-tuple-element.50, s32[128]{0:T(128)S(1)} %get-tuple-element.53, s32[2048]{0:T(1024)S(1)} %get-tuple-element.44, s32[2048]{0:T(1024)S(1)} %get-tuple-element.47, ...), kind=kLoop, calls=%fused_computation.11 | loop fusion | flops 8126464 | bytes 1087744 | tf_op jit(solution)/shard_map/jit(_where)/select_n | solution.py:59
  32.7 1.0 %shard_map.42 = (f32[520,128]{1,0:T(8,128)S(1)}, f32[512,128]{1,0:T(8,128)S(1)}) custom-call(s32[13]{0:T(128)S(1)} %copy-done.5, f32[10]{0:T(128)S(1)} %copy-done.4, f32[2048,128]{1,0:T(8,128)S(1)} %bitcast.3, f32[512,128]{1,0:T(8,128)S(1)} %collective-permute-done.4.refs_0_.refs_3_, f32[512,128]{1,0:T(8,128)S(1)} %collective-permute-done.5.refs_1_, ...), custom_call_target="tpu_custom_call" | custom-call | flops 16777216 | bytes 1048576 | tf_op jit(solution)/shard_map/pallas_call | solution.py:242
  33.7 1.1 %shard_map.41 = (f32[1040,128]{1,0:T(8,128)S(1)}, f32[1024,128]{1,0:T(8,128)S(1)}) custom-call(s32[13]{0:T(128)S(1)} %copy-done.5, f32[10]{0:T(128)S(1)} %copy-done.4, f32[2048,128]{1,0:T(8,128)S(1)} %bitcast.4, f32[512,128]{1,0:T(8,128)S(1)} %collective-permute-done.refs_0_, f32[512,128]{1,0:T(8,128)S(1)} %collective-permute-done.1.refs_1_, ...), custom_call_target="tpu_custom_call" | custom-call | flops 33554432 | bytes 2097152 | tf_op jit(solution)/shard_map/pallas_call | solution.py:242
  34.9 2.6 %shard_map.43 = (f32[2080,128]{1,0:T(8,128)S(1)}, f32[512,128]{1,0:T(8,128)S(1)}, f32[512,128]{1,0:T(8,128)S(1)}, f32[512,128]{1,0:T(8,128)S(1)}) custom-call(s32[13]{0:T(128)S(1)} %copy-done.5, f32[10]{0:T(128)S(1)} %copy-done.4, f32[2048,128]{1,0:T(8,128)S(1)} %bitcast.5, f32[1040,128]{1,0:T(8,128)S(1)} %get-tuple-element.23.refs_0_, ...), custom_call_target="tpu_custom_call" | custom-call | flops 268435456 | bytes 8388608 | tf_op jit(solution)/shard_map/pallas_call | solution.py:252
  38.7 1.3 %collective-permute-start.12 = (f32[512,128]{1,0:T(8,128)S(1)}, f32[512,128]{1,0:T(8,128)S(1)}, u32[]{:S(2)}, u32[]{:S(2)}) collective-permute-start(f32[512,128]{1,0:T(8,128)S(1)} %collective-permute-done.4.refs_0_.refs_3_), channel_id=1, source_target_pairs={{0,2},{1,3},{2,0},{3,1},{4,6},{5,7},{6,4},{7,5},{8,10},{9,11},{10,... | collective-permute-start | bytes 786440 | tf_op jit(solution)/shard_map/ppermute | solution.py:506
  40.0 1.1 %terms.1 = (f32[512,128]{1,0:T(8,128)S(1)}, f32[512,128]{1,0:T(8,128)S(1)}) custom-call(s32[13]{0:T(128)S(1)} %copy-done.5, f32[2080,128]{1,0:T(8,128)S(1)} %get-tuple-element.28.spectral, f32[1024,128]{1,0:T(8,128)S(1)} %get-tuple-element.25.refs_2_.refs_0_, f32[512,128]{1,0:T(8,128)S(1)} %get-tuple-element.26.refs_3_.refs_1_, ...), custom_call_target="tpu_custom_call" | custom-call | flops 100663296 | bytes 2097152 | tf_op jit(solution)/shard_map/terms/pallas_call | solution.py:306
  41.7 0.8 %collective-permute-start.10 = (f32[512,128]{1,0:T(8,128)S(1)}, f32[512,128]{1,0:T(8,128)S(1)}, u32[]{:S(2)}, u32[]{:S(2)}) collective-permute-start(f32[512,128]{1,0:T(8,128)S(1)} %shard_map.45), channel_id=1, source_target_pairs={{0,2},{1,3},{2,0},{3,1},{4,6},{5,7},{6,4},{7,5},{8,10},{9,11},{10,... | collective-permute-start | bytes 786440 | tf_op jit(solution)/shard_map/ppermute | solution.py:506
  42.5 4.7 %collective-permute-done.11.refs_2_ = f32[512,128]{1,0:T(8,128)S(1)} collective-permute-done((f32[512,128]{1,0:T(8,128)S(1)}, f32[512,128]{1,0:T(8,128)S(1)}, u32[]{:S(2)}, u32[]{:S(2)}) %collective-permute-start.11) | collective-permute-done | bytes 262176 | tf_op jit(solution)/shard_map/ppermute | solution.py:506
  47.2 5.6 %collective-permute-done.12.refs_5_ = f32[512,128]{1,0:T(8,128)S(1)} collective-permute-done((f32[512,128]{1,0:T(8,128)S(1)}, f32[512,128]{1,0:T(8,128)S(1)}, u32[]{:S(2)}, u32[]{:S(2)}) %collective-permute-start.12) | collective-permute-done | bytes 262176 | tf_op jit(solution)/shard_map/ppermute | solution.py:506
  52.8 1.1 %shard_map.46.refs_0_ = f32[8,128]{1,0:T(8,128)S(1)} custom-call(s32[13]{0:T(128)S(1)} %copy-done.5, f32[10]{0:T(128)S(1)} %copy-done.4, f32[512,128]{1,0:T(8,128)S(1)} %get-tuple-element.32.kept.far, f32[512,128]{1,0:T(8,128)S(1)} %collective-permute-done.9.met.met_far, f32[512,128]{1,0:T(8,128)S(1)} %get-tuple-element.30.kept.near, ...), custom_call_target="tpu_custom_call" | custom-call | flops 2097152 | bytes 3145728 | tf_op jit(solution)/shard_map/pallas_call | solution.py:437
  53.9 0.8 %collective-permute-start.13 = (f32[8,128]{1,0:T(8,128)S(1)}, f32[8,128]{1,0:T(8,128)S(1)}, u32[]{:S(2)}, u32[]{:S(2)}) collective-permute-start(f32[8,128]{1,0:T(8,128)S(1)} %shard_map.46.refs_0_), channel_id=1, source_target_pairs={{0,2},{1,3},{2,0},{3,1},{4,6},{5,7},{6,4},{7,5},{8,10},{9,11},{10,... | collective-permute-start | bytes 12296 | tf_op jit(solution)/shard_map/ppermute | solution.py:506
  54.7 1.4 %collective-permute-start.15 = (f32[8,128]{1,0:T(8,128)S(1)}, f32[8,128]{1,0:T(8,128)S(1)}, u32[]{:S(2)}, u32[]{:S(2)}) collective-permute-start(f32[8,128]{1,0:T(8,128)S(1)} %shard_map.46.refs_0_), channel_id=1, source_target_pairs={{0,1},{1,0},{2,3},{3,2},{4,5},{5,4},{6,7},{7,6},{8,9},{9,8},{10,11... | collective-permute-start | bytes 12296 | tf_op jit(solution)/shard_map/ppermute | solution.py:506
  56.7 0.9 %collective-permute-done.13.refs_1_ = f32[8,128]{1,0:T(8,128)S(1)} collective-permute-done((f32[8,128]{1,0:T(8,128)S(1)}, f32[8,128]{1,0:T(8,128)S(1)}, u32[]{:S(2)}, u32[]{:S(2)}) %collective-permute-start.13) | collective-permute-done | bytes 4128 | tf_op jit(solution)/shard_map/ppermute | solution.py:506
  57.7 0.7 %finish.1 = (f32[512,128]{1,0:T(8,128)}, f32[1,4]{1,0:T(1,128)}) custom-call(f32[512,128]{1,0:T(8,128)S(1)} %shard_map.44.near_sum, f32[512,128]{1,0:T(8,128)S(1)} %collective-permute-done.10.arrived, f32[8,128]{1,0:T(8,128)S(1)} %shard_map.46.refs_0_, f32[8,128]{1,0:T(8,128)S(1)} %collective-permute-done.13.refs_1_, ...), custom_call_target="tpu_custom_call" | custom-call | flops 65536 | bytes 786432 | tf_op jit(solution)/shard_map/finish/pallas_call | solution.py:334
  (45 shorter events, 3.5 us)
Async XLA Ops:
  1.9 30.7 %copy-start = (f32[1,262144]{1,0:T(1,128)S(1)}, f32[1,262144]{1,0:T(1,128)}, u32[]{:S(2)}) copy-start(f32[1,262144]{1,0:T(1,128)} %param.2) | copy-start | bytes 3145732
  1.9 28.4 %collective-permute-start.4 = (f32[512,128]{1,0:T(8,128)S(1)}, f32[512,128]{1,0:T(8,128)S(1)}, u32[]{:S(2)}, u32[]{:S(2)}) collective-permute-start(f32[512,128]{1,0:T(8,128)S(1)} %get-tuple-element.37), channel_id=1, source_target_pairs={{12,0},{13,1},{10,2},{11,3},{8,4},{9,5},{14,6},{15,7},{4,8},{5,9},... | collective-permute-start | bytes 786440 | tf_op jit(solution)/shard_map/ppermute | solution.py:503
  7.1 23.8 %collective-permute-start.5 = (f32[512,128]{1,0:T(8,128)S(1)}, f32[512,128]{1,0:T(8,128)S(1)}, u32[]{:S(2)}, u32[]{:S(2)}) collective-permute-start(f32[512,128]{1,0:T(8,128)S(1)} %get-tuple-element.36), channel_id=1, source_target_pairs={{4,0},{5,1},{6,2},{7,3},{0,4},{1,5},{2,6},{3,7},{12,8},{13,9},{14,... | collective-permute-start | bytes 786440 | tf_op jit(solution)/shard_map/ppermute | solution.py:503
  7.1 18.5 %collective-permute-start = (f32[512,128]{1,0:T(8,128)S(1)}, f32[512,128]{1,0:T(8,128)S(1)}, u32[]{:S(2)}, u32[]{:S(2)}) collective-permute-start(f32[512,128]{1,0:T(8,128)S(1)} %get-tuple-element.39), channel_id=1, source_target_pairs={{12,0},{13,1},{10,2},{11,3},{8,4},{9,5},{14,6},{15,7},{4,8},{5,9},... | collective-permute-start | bytes 786440 | tf_op jit(solution)/shard_map/ppermute | solution.py:503
  8.0 22.4 %collective-permute-start.1 = (f32[512,128]{1,0:T(8,128)S(1)}, f32[512,128]{1,0:T(8,128)S(1)}, u32[]{:S(2)}, u32[]{:S(2)}) collective-permute-start(f32[512,128]{1,0:T(8,128)S(1)} %get-tuple-element.38), channel_id=1, source_target_pairs={{4,0},{5,1},{6,2},{7,3},{0,4},{1,5},{2,6},{3,7},{12,8},{13,9},{14,... | collective-permute-start | bytes 786440 | tf_op jit(solution)/shard_map/ppermute | solution.py:503
  12.6 20.1 %copy-start.4 = (f32[10]{0:T(128)S(1)}, f32[10]{0:T(128)}, u32[]{:S(2)}) copy-start(f32[10]{0:T(128)} %get-tuple-element.19.factors) | copy-start | bytes 124
  12.6 20.1 %copy-start.5 = (s32[13]{0:T(128)S(1)}, s32[13]{0:T(128)}, u32[]{:S(2)}) copy-start(s32[13]{0:T(128)} %get-tuple-element.20.places) | copy-start | bytes 160
  14.2 18.4 %copy-start.1 = (bf16[256,256]{1,0:T(8,128)(2,1)S(1)}, bf16[256,256]{1,0:T(8,128)(2,1)}, u32[]{:S(2)}) copy-start(bf16[256,256]{1,0:T(8,128)(2,1)} %get-tuple-element.22.refs_5_.refs_3_.refs_9_.refs_4_) | copy-start | bytes 393220
  14.2 18.4 %copy-start.2 = (bf16[64,192]{1,0:T(8,128)(2,1)S(1)}, bf16[64,192]{1,0:T(8,128)(2,1)}, u32[]{:S(2)}) copy-start(bf16[64,192]{1,0:T(8,128)(2,1)} %get-tuple-element.21.refs_4_.refs_2_.refs_7_) | copy-start | bytes 73732
  25.6 8.1 %collective-permute-start.2 = (f32[512,128]{1,0:T(8,128)S(1)}, f32[512,128]{1,0:T(8,128)S(1)}, u32[]{:S(2)}, u32[]{:S(2)}) collective-permute-start(f32[512,128]{1,0:T(8,128)S(1)} %collective-permute-done.refs_0_), channel_id=1, source_target_pairs={{0,1},{1,0},{2,3},{3,2},{4,5},{5,4},{6,7},{7,6},{8,9},{9,8},{10,11... | collective-permute-start | bytes 786440 | tf_op jit(solution)/shard_map/ppermute | solution.py:506
  30.3 3.4 %collective-permute-start.3 = (f32[512,128]{1,0:T(8,128)S(1)}, f32[512,128]{1,0:T(8,128)S(1)}, u32[]{:S(2)}, u32[]{:S(2)}) collective-permute-start(f32[512,128]{1,0:T(8,128)S(1)} %collective-permute-done.1.refs_1_), channel_id=1, source_target_pairs={{0,1},{1,0},{2,3},{3,2},{4,5},{5,4},{6,7},{7,6},{8,9},{9,8},{10,11... | collective-permute-start | bytes 786440 | tf_op jit(solution)/shard_map/ppermute | solution.py:506
  30.4 4.5 %collective-permute-start.6 = (f32[512,128]{1,0:T(8,128)S(1)}, f32[512,128]{1,0:T(8,128)S(1)}, u32[]{:S(2)}, u32[]{:S(2)}) collective-permute-start(f32[512,128]{1,0:T(8,128)S(1)} %collective-permute-done.4.refs_0_.refs_3_), channel_id=1, source_target_pairs={{0,1},{1,0},{2,3},{3,2},{4,5},{5,4},{6,7},{7,6},{8,9},{9,8},{10,11... | collective-permute-start | bytes 786440 | tf_op jit(solution)/shard_map/ppermute | solution.py:506
  30.9 4.0 %collective-permute-start.7 = (f32[512,128]{1,0:T(8,128)S(1)}, f32[512,128]{1,0:T(8,128)S(1)}, u32[]{:S(2)}, u32[]{:S(2)}) collective-permute-start(f32[512,128]{1,0:T(8,128)S(1)} %collective-permute-done.5.refs_1_), channel_id=1, source_target_pairs={{0,1},{1,0},{2,3},{3,2},{4,5},{5,4},{6,7},{7,6},{8,9},{9,8},{10,11... | collective-permute-start | bytes 786440 | tf_op jit(solution)/shard_map/ppermute | solution.py:506
  33.7 1.2 %copy-start.3 = (bf16[64,192]{1,0:T(8,128)(2,1)S(1)}, bf16[64,192]{1,0:T(8,128)(2,1)}, u32[]{:S(2)}) copy-start(bf16[64,192]{1,0:T(8,128)(2,1)} %get-tuple-element.27.refs_8_.refs_3_) | copy-start | bytes 73732
  37.5 3.6 %collective-permute-start.9 = (f32[512,128]{1,0:T(8,128)S(1)}, f32[512,128]{1,0:T(8,128)S(1)}, u32[]{:S(2)}, u32[]{:S(2)}) collective-permute-start(f32[512,128]{1,0:T(8,128)S(1)} %get-tuple-element.33), channel_id=1, source_target_pairs={{0,1},{1,0},{2,3},{3,2},{4,5},{5,4},{6,7},{7,6},{8,9},{9,8},{10,11... | collective-permute-start | bytes 786440 | tf_op jit(solution)/shard_map/ppermute | solution.py:506
  38.0 9.2 %collective-permute-start.11 = (f32[512,128]{1,0:T(8,128)S(1)}, f32[512,128]{1,0:T(8,128)S(1)}, u32[]{:S(2)}, u32[]{:S(2)}) collective-permute-start(f32[512,128]{1,0:T(8,128)S(1)} %collective-permute-done.refs_0_), channel_id=1, source_target_pairs={{0,2},{1,3},{2,0},{3,1},{4,6},{5,7},{6,4},{7,5},{8,10},{9,11},{10,... | collective-permute-start | bytes 786440 | tf_op jit(solution)/shard_map/ppermute | solution.py:506
  38.7 14.1 %collective-permute-start.12 = (f32[512,128]{1,0:T(8,128)S(1)}, f32[512,128]{1,0:T(8,128)S(1)}, u32[]{:S(2)}, u32[]{:S(2)}) collective-permute-start(f32[512,128]{1,0:T(8,128)S(1)} %collective-permute-done.4.refs_0_.refs_3_), channel_id=1, source_target_pairs={{0,2},{1,3},{2,0},{3,1},{4,6},{5,7},{6,4},{7,5},{8,10},{9,11},{10,... | collective-permute-start | bytes 786440 | tf_op jit(solution)/shard_map/ppermute | solution.py:506
  40.0 12.8 %collective-permute-start.8 = (f32[512,128]{1,0:T(8,128)S(1)}, f32[512,128]{1,0:T(8,128)S(1)}, u32[]{:S(2)}, u32[]{:S(2)}) collective-permute-start(f32[512,128]{1,0:T(8,128)S(1)} %get-tuple-element.31), channel_id=1, source_target_pairs={{0,1},{1,0},{2,3},{3,2},{4,5},{5,4},{6,7},{7,6},{8,9},{9,8},{10,11... | collective-permute-start | bytes 786440 | tf_op jit(solution)/shard_map/ppermute | solution.py:506
  41.7 16.0 %collective-permute-start.10 = (f32[512,128]{1,0:T(8,128)S(1)}, f32[512,128]{1,0:T(8,128)S(1)}, u32[]{:S(2)}, u32[]{:S(2)}) collective-permute-start(f32[512,128]{1,0:T(8,128)S(1)} %shard_map.45), channel_id=1, source_target_pairs={{0,2},{1,3},{2,0},{3,1},{4,6},{5,7},{6,4},{7,5},{8,10},{9,11},{10,... | collective-permute-start | bytes 786440 | tf_op jit(solution)/shard_map/ppermute | solution.py:506
  53.9 3.7 %collective-permute-start.13 = (f32[8,128]{1,0:T(8,128)S(1)}, f32[8,128]{1,0:T(8,128)S(1)}, u32[]{:S(2)}, u32[]{:S(2)}) collective-permute-start(f32[8,128]{1,0:T(8,128)S(1)} %shard_map.46.refs_0_), channel_id=1, source_target_pairs={{0,2},{1,3},{2,0},{3,1},{4,6},{5,7},{6,4},{7,5},{8,10},{9,11},{10,... | collective-permute-start | bytes 12296 | tf_op jit(solution)/shard_map/ppermute | solution.py:506
  54.7 3.0 %collective-permute-start.14 = (f32[8,128]{1,0:T(8,128)S(1)}, f32[8,128]{1,0:T(8,128)S(1)}, u32[]{:S(2)}, u32[]{:S(2)}) collective-permute-start(f32[8,128]{1,0:T(8,128)S(1)} %shard_map.46.refs_0_), channel_id=1, source_target_pairs={{0,3},{1,2},{2,1},{3,0},{4,7},{5,6},{6,5},{7,4},{8,11},{9,10},{10,... | collective-permute-start | bytes 12296 | tf_op jit(solution)/shard_map/ppermute | solution.py:506
  54.7 3.0 %collective-permute-start.15 = (f32[8,128]{1,0:T(8,128)S(1)}, f32[8,128]{1,0:T(8,128)S(1)}, u32[]{:S(2)}, u32[]{:S(2)}) collective-permute-start(f32[8,128]{1,0:T(8,128)S(1)} %shard_map.46.refs_0_), channel_id=1, source_target_pairs={{0,1},{1,0},{2,3},{3,2},{4,5},{5,4},{6,7},{7,6},{8,9},{9,8},{10,11... | collective-permute-start | bytes 12296 | tf_op jit(solution)/shard_map/ppermute | solution.py:506
